TPU v7x, 32 devices: a whole 2x2x4 slice. The times are simulated.
32 devices in a mesh: dp: 8 (over y, x, core), tensor: 4 (over z).
Axes of the slice: x: 2, y: 2, z: 4, core: 2. Of those that a mesh axis runs over, the one named last changes fastest.
Arguments:
- clips: bfloat16 [16, 1568, 768], P('dp', 'tensor'), may hold values from -6 to 6
- clip_live: int32 [16], P('dp'), may hold values 0 or 1
- qkv_weight: bfloat16 [2, 768, 3, 768], P(None, 'dp', None, 'tensor'), may hold values from -0.21875 to 0.21875
- proj_weight: bfloat16 [2, 768, 768], P(None, 'tensor', 'dp'), may hold values from -2.236068 to 2.236068
- fc1_weight: bfloat16 [768, 3072], P('dp', 'tensor'), may hold values from -0.21875 to 0.21875
- fc2_weight: bfloat16 [3072, 768], P('tensor', 'dp'), may hold values from -0.109375 to 0.109375
- attn_bias: bfloat16 [2, 2, 12, 64], P(None, None, 'tensor', 'dp'), may hold values from -3 to 3
- fc1_bias: bfloat16 [4, 768], P('tensor', 'dp'), may hold values from -3 to 3
- norm_params: bfloat16 [3, 2, 768], P(None, None, ('dp', 'tensor')), may hold values from -1.2 to 1.6
- tfc_weight: bfloat16 [768, 768], P(('dp', 'tensor')), may hold values from -0.21875 to 0.21875
- out_bias: bfloat16 [4, 768], P(None, ('dp', 'tensor')), may hold values from -2 to 2
- cotangent: bfloat16 [16, 1568, 768], P('dp', 'tensor'), may hold values from -6 to 6
Outputs:
- outputs: bfloat16 [16, 1568, 768], P('dp', 'tensor')
- grad_clips: float32 [16, 1568, 768], P('dp', 'tensor')
- grad_qkv: float32 [2, 768, 3, 768], P(None, 'dp', None, 'tensor')
- grad_proj: float32 [2, 768, 768], P(None, 'tensor', 'dp')
- grad_fc1: float32 [768, 3072], P('dp', 'tensor')
- grad_fc2: float32 [3072, 768], P('tensor', 'dp')
- grad_attn_bias: float32 [2, 2, 12, 64], P(None, None, 'tensor', 'dp')
- grad_fc1_bias: float32 [4, 768], P('tensor', 'dp')
- grad_norm: float32 [3, 2, 768], P(None, None, ('dp', 'tensor'))
- grad_tfc: float32 [768, 768], P(('dp', 'tensor'))
- grad_out_bias: float32 [4, 768], P(None, ('dp', 'tensor'))
Inputs may be any that keep to these rules, and one draw needn't show every extreme that they name: `clip_live`: 1 where the slot holds a clip, 0 where it is empty.
All inputs are finite; a program needn't handle non-finite values. No bound on the sum of `clip_live` on one device may be relied on, other than what follows from the above.
Results may differ from a plain program's by a relative error of at most 0.034.
Values may be sent and summed in bfloat16 or wider, within the bound.
No kernel may reach another device: no remote copies, remote signals or barrier semaphores. Data moves between devices by JAX's collectives and lax.ppermute only.
A program may use at most 192 MiB of HBM per device.

v0:
```python
from functools import partial

import jax
import jax.numpy as jnp
from jax import lax
from jax.sharding import PartitionSpec as P

FRAMES = 8


EPS = 1e-06


def layer_norm(inputs, norm_gain, norm_shift):
    average = jnp.mean(inputs, axis=-1, keepdims=True)
    centred = inputs - average
    variance = jnp.mean(centred * centred, axis=-1, keepdims=True)
    return centred * lax.rsqrt(variance + EPS) * norm_gain + norm_shift


def contract_rows(left, right):
    return lax.dot_general(
        left, right, (((0,), (0,)), ((), ())), preferred_element_type=jnp.float32
    )


def times_transpose(left, right):
    return lax.dot_general(
        left, right, (((1,), (1,)), ((), ())), preferred_element_type=jnp.float32
    )


def gather_rows(normed):
    return lax.all_gather(normed, "tensor", axis=0, tiled=True)


def gather_grads(grad_low):
    return lax.all_gather(grad_low, "tensor", axis=0, tiled=True)


def scatter_forward(inputs, weight, local_rows):

    def partial_rows(start, count):
        return jnp.dot(inputs, weight, preferred_element_type=jnp.float32)

    return lax.psum_scatter(
        partial_rows(jnp.int32(0), local_rows * lax.axis_size("tensor")).astype(jnp.bfloat16),
        "tensor",
        scatter_dimension=0,
        tiled=True,
    ).astype(jnp.float32)


def scatter_backward(grads, weight, local_rows):

    def partial_rows(start, count):
        return times_transpose(grads, weight)

    return lax.psum_scatter(
        partial_rows(jnp.int32(0), local_rows * lax.axis_size("tensor")).astype(jnp.bfloat16),
        "tensor",
        scatter_dimension=0,
        tiled=True,
    ).astype(jnp.float32)


def attend(query, keys, values, spatial):
    scale = query.shape[-1] ** (-0.5)
    if spatial:
        scores = jnp.einsum("fphd,fqhd->hfpq", query, keys, preferred_element_type=jnp.float32)
    else:
        scores = jnp.einsum("fphd,gphd->hpfg", query, keys, preferred_element_type=jnp.float32)
    probs = jax.nn.softmax(scores * scale, axis=-1)
    probs_low = probs.astype(jnp.bfloat16)
    if spatial:
        heads = jnp.einsum("hfpq,fqhd->fphd", probs_low, values, preferred_element_type=jnp.float32)
    else:
        heads = jnp.einsum("hpfg,gphd->fphd", probs_low, values, preferred_element_type=jnp.float32)
    return (probs, heads.astype(jnp.bfloat16))


def attend_back(query, keys, values, probs, grad_heads, spatial):
    scale = query.shape[-1] ** (-0.5)
    probs_low = probs.astype(jnp.bfloat16)
    if spatial:
        grad_probs = jnp.einsum(
            "fphd,fqhd->hfpq", grad_heads, values, preferred_element_type=jnp.float32
        )
        grad_values = jnp.einsum(
            "hfpq,fphd->fqhd", probs_low, grad_heads, preferred_element_type=jnp.float32
        )
    else:
        grad_probs = jnp.einsum(
            "fphd,gphd->hpfg", grad_heads, values, preferred_element_type=jnp.float32
        )
        grad_values = jnp.einsum(
            "hpfg,fphd->gphd", probs_low, grad_heads, preferred_element_type=jnp.float32
        )
    grad_scores = probs * (grad_probs - jnp.sum(grad_probs * probs, axis=-1, keepdims=True))
    grad_scaled = grad_scores.astype(jnp.bfloat16) * scale
    if spatial:
        grad_query = jnp.einsum(
            "hfpq,fqhd->fphd", grad_scaled, keys, preferred_element_type=jnp.float32
        )
        grad_keys = jnp.einsum(
            "hfpq,fphd->fqhd", grad_scaled, query, preferred_element_type=jnp.float32
        )
    else:
        grad_query = jnp.einsum(
            "hpfg,gphd->fphd", grad_scaled, keys, preferred_element_type=jnp.float32
        )
        grad_keys = jnp.einsum(
            "hpfg,fphd->gphd", grad_scaled, query, preferred_element_type=jnp.float32
        )
    stacked = jnp.stack([grad_query, grad_keys, grad_values], axis=2)
    return stacked.reshape(stacked.shape[0] * stacked.shape[1], -1).astype(jnp.bfloat16)


def heads_branch(residual, weights, branch):
    (
        qkv_full,
        proj_full,
        fc1_full,
        fc2_full,
        attn_full,
        hidden_bias,
        norm_full,
        tfc_full,
        out_full,
    ) = weights
    head_count = attn_full.shape[2]
    head_size = attn_full.shape[3]
    width = head_count * head_size
    normed_full = gather_rows(
        layer_norm(residual, norm_full[branch, 0], norm_full[branch, 1]).astype(jnp.bfloat16)
    )
    weight_flat = qkv_full[branch].reshape(-1, 3 * width)
    bias_rows = attn_full[branch].astype(jnp.float32).reshape(2, width)
    bias_flat = jnp.stack([bias_rows[0], jnp.zeros((width,), jnp.float32), bias_rows[1]]).reshape(
        3 * width
    )
    mixed = (
        jnp.dot(normed_full, weight_flat, preferred_element_type=jnp.float32) + bias_flat
    ).astype(jnp.bfloat16)
    mixed = mixed.reshape(FRAMES, -1, 3, head_count, head_size)
    probs, heads = attend(mixed[:, :, 0], mixed[:, :, 1], mixed[:, :, 2], branch == 1)
    heads_flat = heads.reshape(-1, width)
    summed = (
        scatter_forward(heads_flat, proj_full[branch], residual.shape[0]) + out_full[2 * branch]
    )
    return (summed, (normed_full, mixed, probs, heads_flat))


def heads_branch_back(grad_out, residual, weights, saved, branch):
    (
        qkv_full,
        proj_full,
        fc1_full,
        fc2_full,
        attn_full,
        hidden_bias,
        norm_full,
        tfc_full,
        out_full,
    ) = weights
    normed_full, mixed, probs, heads_flat = saved
    head_count = attn_full.shape[2]
    head_size = attn_full.shape[3]
    width = head_count * head_size
    grad_low = grad_out.astype(jnp.bfloat16)
    grad_bias_out = jnp.sum(grad_low.astype(jnp.float32), axis=0)
    grad_full = gather_grads(grad_low)
    grad_proj = contract_rows(heads_flat, grad_full)
    grad_heads = times_transpose(grad_full, proj_full[branch]).astype(jnp.bfloat16)
    grad_heads = grad_heads.reshape(FRAMES, -1, head_count, head_size)
    grad_mixed = attend_back(
        mixed[:, :, 0], mixed[:, :, 1], mixed[:, :, 2], probs, grad_heads, branch == 1
    )
    grad_qkv = contract_rows(normed_full, grad_mixed).reshape(-1, 3, width)
    column_sums = jnp.sum(grad_mixed.astype(jnp.float32), axis=0).reshape(3, head_count, head_size)
    grad_attn = jnp.stack([column_sums[0], column_sums[2]])
    grad_normed = scatter_backward(
        grad_mixed, qkv_full[branch].reshape(-1, 3 * width), residual.shape[0]
    )
    norm_value, norm_back = jax.vjp(
        layer_norm, residual, norm_full[branch, 0], norm_full[branch, 1]
    )
    grad_in, grad_gain, grad_shift = norm_back(grad_normed)
    return (grad_in, grad_gain, grad_shift, grad_bias_out, grad_proj, grad_qkv, grad_attn)


def forward_clip(inputs, weights):
    (
        qkv_full,
        proj_full,
        fc1_full,
        fc2_full,
        attn_full,
        hidden_bias,
        norm_full,
        tfc_full,
        out_full,
    ) = weights
    summed_t, saved_t = heads_branch(inputs, weights, 0)
    summed_low = summed_t.astype(jnp.bfloat16)
    first = inputs + jnp.dot(summed_low, tfc_full, preferred_element_type=jnp.float32) + out_full[1]
    summed_s, saved_s = heads_branch(first, weights, 1)
    second = first + summed_s
    normed_local = layer_norm(second, norm_full[2, 0], norm_full[2, 1]).astype(jnp.bfloat16)
    normed_full = gather_rows(normed_local)
    hidden = jnp.dot(
        normed_full, fc1_full, preferred_element_type=jnp.float32
    ) + hidden_bias.astype(jnp.float32).reshape(-1)
    active_low = jax.nn.gelu(hidden, approximate=False).astype(jnp.bfloat16)
    projected = scatter_forward(active_low, fc2_full, inputs.shape[0])
    result = second + projected + out_full[3]
    return (result, (saved_t, summed_low, first, saved_s, second, normed_full, hidden, active_low))


def backward_clip(inputs, grad_result, weights, saved):
    (
        qkv_full,
        proj_full,
        fc1_full,
        fc2_full,
        attn_full,
        hidden_bias,
        norm_full,
        tfc_full,
        out_full,
    ) = weights
    saved_t, summed_low, first, saved_s, second, normed_full, hidden, active_low = saved
    width_full = inputs.shape[1]
    grad_low = grad_result.astype(jnp.bfloat16)
    bias_fc2 = jnp.sum(grad_low.astype(jnp.float32), axis=0)
    grad_full = gather_grads(grad_low)
    grad_fc2 = contract_rows(active_low, grad_full)
    grad_active = times_transpose(grad_full, fc2_full)
    gelu_value, gelu_back = jax.vjp(partial(jax.nn.gelu, approximate=False), hidden)
    grad_hidden = gelu_back(grad_active)[0].astype(jnp.bfloat16)
    grad_fc1 = contract_rows(normed_full, grad_hidden)
    grad_hidden_bias = jnp.sum(grad_hidden.astype(jnp.float32), axis=0).reshape(-1, width_full)
    grad_normed = scatter_backward(grad_hidden, fc1_full, inputs.shape[0])
    norm_value, norm_back = jax.vjp(layer_norm, second, norm_full[2, 0], norm_full[2, 1])
    grad_second_in, gain_mlp, shift_mlp = norm_back(grad_normed)
    grad_second = grad_result + grad_second_in
    spatial_in, gain_s, shift_s, bias_s, proj_s, qkv_s, attn_s = heads_branch_back(
        grad_second, first, weights, saved_s, 1
    )
    grad_first = grad_second + spatial_in
    temporal_low = grad_first.astype(jnp.bfloat16)
    bias_tfc = jnp.sum(temporal_low.astype(jnp.float32), axis=0)
    grad_tfc = contract_rows(summed_low, temporal_low)
    grad_summed = times_transpose(temporal_low, tfc_full)
    temporal_in, gain_t, shift_t, bias_t, proj_t, qkv_t, attn_t = heads_branch_back(
        grad_summed, inputs, weights, saved_t, 0
    )
    grad_inputs = grad_first + temporal_in
    split_part = (
        jnp.stack([qkv_t, qkv_s]),
        jnp.stack([proj_t, proj_s]),
        grad_fc1,
        grad_fc2,
        jnp.stack([attn_t, attn_s]),
        grad_hidden_bias,
    )
    norm_grads = jnp.stack(
        [
            jnp.stack([gain_t, shift_t]),
            jnp.stack([gain_s, shift_s]),
            jnp.stack([gain_mlp, shift_mlp]),
        ]
    )
    shared_part = (norm_grads, grad_tfc, jnp.stack([bias_t, bias_tfc, bias_s, bias_fc2]))
    return (grad_inputs, (split_part, shared_part))


def reduce_grads(grads):
    split_part, shared_part = grads
    qkv_sum, proj_sum, fc1_sum, fc2_sum, attn_sum, hidden_sum = split_part
    norm_sum, tfc_sum, outb_sum = shared_part
    split_done = (
        lax.psum_scatter(qkv_sum, "dp", scatter_dimension=1, tiled=True),
        lax.psum_scatter(proj_sum, "dp", scatter_dimension=2, tiled=True),
        lax.psum_scatter(fc1_sum, "dp", scatter_dimension=0, tiled=True),
        lax.psum_scatter(fc2_sum, "dp", scatter_dimension=1, tiled=True),
        lax.psum_scatter(attn_sum, "dp", scatter_dimension=3, tiled=True),
        lax.psum_scatter(hidden_sum, "dp", scatter_dimension=1, tiled=True),
    )
    shared_done = (
        lax.psum_scatter(norm_sum, ("dp", "tensor"), scatter_dimension=2, tiled=True),
        lax.psum_scatter(tfc_sum, ("dp", "tensor"), scatter_dimension=0, tiled=True),
        lax.psum_scatter(outb_sum, ("dp", "tensor"), scatter_dimension=1, tiled=True),
    )
    return (tuple(split_done), tuple(shared_done))


def shards(
    clips,
    clip_live,
    qkv_weight,
    proj_weight,
    fc1_weight,
    fc2_weight,
    attn_bias,
    fc1_bias,
    norm_params,
    tfc_weight,
    out_bias,
    cotangent,
):
    split_full = (
        lax.all_gather(qkv_weight, "dp", axis=1, tiled=True),
        lax.all_gather(proj_weight, "dp", axis=2, tiled=True),
        lax.all_gather(fc1_weight, "dp", axis=0, tiled=True),
        lax.all_gather(fc2_weight, "dp", axis=1, tiled=True),
        lax.all_gather(attn_bias, "dp", axis=3, tiled=True),
        lax.all_gather(fc1_bias, "dp", axis=1, tiled=True),
    )
    norm_full, tfc_full, out_full = (
        lax.all_gather(norm_params, ("dp", "tensor"), axis=2, tiled=True),
        lax.all_gather(tfc_weight, ("dp", "tensor"), axis=0, tiled=True),
        lax.all_gather(out_bias, ("dp", "tensor"), axis=1, tiled=True),
    )
    qkv_full, proj_full, fc1_part, fc2_part, attn_full, bias_part = split_full
    weights = (
        qkv_full,
        proj_full,
        fc1_part,
        fc2_part,
        attn_full,
        bias_part,
        norm_full.astype(jnp.float32),
        tfc_full,
        out_full.astype(jnp.float32),
    )
    results = []
    grad_rows = []
    totals = None
    for micro in range(clips.shape[0]):
        live = clip_live[micro].astype(jnp.float32)
        inputs = clips[micro].astype(jnp.float32)
        result, saved = forward_clip(inputs, weights)
        results.append((result * live).astype(jnp.bfloat16))
        grad_in, grads = backward_clip(
            inputs, cotangent[micro].astype(jnp.float32) * live, weights, saved
        )
        grad_rows.append(grad_in)
        totals = grads if totals is None else jax.tree.map(jnp.add, totals, grads)
    totals = reduce_grads(totals)
    split_done, shared_done = totals
    return (
        jnp.stack(results),
        jnp.stack(grad_rows),
        split_done[0],
        split_done[1],
        split_done[2],
        split_done[3],
        split_done[4],
        split_done[5],
        shared_done[0],
        shared_done[1],
        shared_done[2],
    )


def solution(mesh):
    return jax.shard_map(
        shards,
        mesh=mesh,
        in_specs=(
            P("dp", "tensor", None),
            P("dp"),
            P(None, "dp", None, "tensor"),
            P(None, "tensor", "dp"),
            P("dp", "tensor"),
            P("tensor", "dp"),
            P(None, None, "tensor", "dp"),
            P("tensor", "dp"),
            P(None, None, ("dp", "tensor")),
            P(("dp", "tensor"), None),
            P(None, ("dp", "tensor")),
            P("dp", "tensor", None),
        ),
        out_specs=(
            P("dp", "tensor", None),
            P("dp", "tensor", None),
            P(None, "dp", None, "tensor"),
            P(None, "tensor", "dp"),
            P("dp", "tensor"),
            P("tensor", "dp"),
            P(None, None, "tensor", "dp"),
            P("tensor", "dp"),
            P(None, None, ("dp", "tensor")),
            P(("dp", "tensor"), None),
            P(None, ("dp", "tensor")),
        ),
        check_vma=False,
    )
```

profile of v0, /device:TPU:24, one launch (start us, length us, event | category | flops | bytes accessed | tf_op | source)
XLA Modules:
  0.0 1811.1 jit_solution(4580061671718601709)
XLA Ops:
  10.2 63.5 %all_gather.63 = bf16[3,2,768]{0,1,2:T(2,128)(2,1)S(1)} all-gather(bf16[3,2,24]{0,1,2:T(2,128)(2,1)S(1)} %copy.271), channel_id=1, replica_groups=mesh['dp'=8,'tensor'=4] {'dp','tensor'}, dimensions={2}, use_global_device_ids=true | all-gather | bytes 9504 | tf_op jit(solution)/shard_map/all_gather | solution.py:321
  75.3 12.6 slice_reduce_fusion.1
  91.1 11.2 all_gather.66
  103.4 9.4 all_gather.67
  115.5 8.7 fusion.235
  124.3 6.4 copy.378
  130.7 12.0 all-gather.18.cloned.1.call-done
  146.4 4.5 reshape.429
  182.0 12.5 all-gather.32.cloned.1.call-done
  198.1 4.5 reshape.433
  233.9 65.8 %all-gather = bf16[32,24,4]{1,2,0:T(4,128)(2,1)S(1)} all-gather(bf16[1,24,4]{1,2,0:T(4,128)(2,1)S(1)} %bitcast.484), channel_id=1, replica_groups=mesh['dp'=8,'tensor'=4] {'dp','tensor'}, dimensions={0}, use_global_device_ids=true | all-gather | bytes 6336 | tf_op jit(solution)/shard_map/all_gather | solution.py:323
  304.3 48.1 %reduce-scatter.34.cloned.1.call-done = bf16[392,768]{1,0:T(8,128)(2,1)} async-done(((bf16[1568,768]{1,0:T(8,128)(2,1)}), bf16[392,768]{1,0:T(8,128)(2,1)}) %reduce-scatter.34.cloned.1.call-update) | async-done | bytes 602128 | tf_op jit(solution)/shard_map/reduce_scatter | solution.py:46
  358.1 6.4 copy.383
  364.5 42.5 %all-gather.24.cloned.1.call-done = bf16[1568,768]{1,0:T(8,128)(2,1)} async-done(((bf16[392,768]{1,0:T(8,128)(2,1)}), bf16[1568,768]{1,0:T(8,128)(2,1)}) %all-gather.24.cloned.1.call-update) | async-done | bytes 2408464 | tf_op jit(solution)/shard_map/all_gather | solution.py:34
  407.0 5.0 add_convert_fusion.4
  411.9 5.8 reshape.431
  422.0 4.1 fusion.249
  435.6 23.1 %all-gather.34.cloned.1.call-done = bf16[1568,768]{1,0:T(8,128)(2,1)} async-done(((bf16[392,768]{1,0:T(8,128)(2,1)}), bf16[1568,768]{1,0:T(8,128)(2,1)}) %all-gather.34.cloned.1.call-update) | async-done | bytes 2408464 | tf_op jit(solution)/shard_map/all_gather | solution.py:34
  458.7 5.0 add_convert_fusion.2
  463.7 5.8 reshape.435
  493.5 16.6 reduce-scatter.30.cloned.1.call-done
  510.1 50.8 %reduce-scatter.36.cloned.1.call-done = bf16[392,768]{1,0:T(8,128)(2,1)} async-done(((bf16[1568,768]{1,0:T(8,128)(2,1)}), bf16[392,768]{1,0:T(8,128)(2,1)}) %reduce-scatter.36.cloned.1.call-update) | async-done | bytes 602128 | tf_op jit(solution)/shard_map/reduce_scatter | solution.py:46
  567.5 14.4 all-reduce
  581.9 6.3 all-gather.30.cloned.1.call-done
  588.2 50.3 %all-gather.44.cloned.1.call-done = bf16[1568,768]{1,0:T(8,128)(2,1)} async-done(((bf16[392,768]{1,0:T(8,128)(2,1)}), bf16[1568,768]{1,0:T(8,128)(2,1)}) %all-gather.44.cloned.1.call-update) | async-done | bytes 2408464 | tf_op jit(solution)/shard_map/all_gather | solution.py:38
  638.5 6.2 fusion.254
  644.7 21.0 %all-gather.28.cloned.1.call-done = bf16[768,768]{1,0:T(8,128)(2,1)} async-done(((bf16[96,768]{1,0:T(8,128)(2,1)}), bf16[768,768]{1,0:T(8,128)(2,1)}) %all-gather.28.cloned.1.call-update) | async-done | bytes 1179664 | tf_op jit(solution)/shard_map/all_gather | solution.py:315
  665.7 50.9 %all-gather.26.cloned.1.call-done = bf16[1568,768]{1,0:T(8,128)(2,1)} async-done(((bf16[392,768]{1,0:T(8,128)(2,1)}), bf16[1568,768]{1,0:T(8,128)(2,1)}) %all-gather.26.cloned.1.call-update) | async-done | bytes 2408464 | tf_op jit(solution)/shard_map/all_gather | solution.py:34
  716.6 6.3 fusion.251
  722.9 45.2 %all-gather.36.cloned.1.call-done = bf16[1568,768]{1,0:T(8,128)(2,1)} async-done(((bf16[392,768]{1,0:T(8,128)(2,1)}), bf16[1568,768]{1,0:T(8,128)(2,1)}) %all-gather.36.cloned.1.call-update) | async-done | bytes 2408464 | tf_op jit(solution)/shard_map/all_gather | solution.py:34
  768.2 5.9 fusion.252
  774.0 45.7 %all-gather.38.cloned.1.call-done = bf16[1568,768]{1,0:T(8,128)(2,1)} async-done(((bf16[392,768]{1,0:T(8,128)(2,1)}), bf16[1568,768]{1,0:T(8,128)(2,1)}) %all-gather.38.cloned.1.call-update) | async-done | bytes 2408464 | tf_op jit(solution)/shard_map/all_gather | solution.py:38
  819.7 29.4 %convert_reduce_fusion.3 = (f32[768]{0:T(1024)}, bf16[1568,768]{1,0:T(8,128)(2,1)S(1)}, f32[1568,768]{1,0:T(8,128)}, f32[768]{0:T(1024)}, bf16[1568,768]{1,0:T(8,128)(2,1)S(1)}, /*index=5*/f32[1568,768]{1,0:T(8,128)}) fusion(f32[1568,768]{1,0:T(8,128)} %fusion.251, f32[768]{0:T(1024)S(1)} %add.417, f32[1568,768]{1,0:T(8,128)} %fusion.254, ...), kind=kOutput, calls=%fused_computation.25 | convolution fusion | flops 2030320128 | bytes 32498688 | tf_op jit(solution)/shard_map/dot_general | solution.py:28
  854.2 4.7 convolution_convert_fusion.2
  859.1 9.9 multiply_convert_fusion.3
  868.9 5.7 convolution_convert_fusion.6
  876.3 4.7 convolution_convert_fusion.9
  881.1 21.6 %reduce-scatter.40.cloned.1.call-done = bf16[392,768]{1,0:T(8,128)(2,1)} async-done(((bf16[1568,768]{1,0:T(8,128)(2,1)}), bf16[392,768]{1,0:T(8,128)(2,1)}) %reduce-scatter.40.cloned.1.call-update) | async-done | bytes 602128 | tf_op jit(solution)/shard_map/reduce_scatter | solution.py:59
  902.7 50.8 %reduce-scatter.46.cloned.1.call-done = bf16[392,768]{1,0:T(8,128)(2,1)} async-done(((bf16[1568,768]{1,0:T(8,128)(2,1)}), bf16[392,768]{1,0:T(8,128)(2,1)}) %reduce-scatter.46.cloned.1.call-update) | async-done | bytes 602128 | tf_op jit(solution)/shard_map/reduce_scatter | solution.py:59
  956.4 47.9 %reduce-scatter.38.cloned.1.call-done = bf16[392,768]{1,0:T(8,128)(2,1)} async-done(((bf16[1568,768]{1,0:T(8,128)(2,1)}), bf16[392,768]{1,0:T(8,128)(2,1)}) %reduce-scatter.38.cloned.1.call-update) | async-done | bytes 602128 | tf_op jit(solution)/shard_map/reduce_scatter | solution.py:46
  1004.4 50.8 %reduce-scatter.32.cloned.1.call-done = bf16[392,768]{1,0:T(8,128)(2,1)} async-done(((bf16[1568,768]{1,0:T(8,128)(2,1)}), bf16[392,768]{1,0:T(8,128)(2,1)}) %reduce-scatter.32.cloned.1.call-update) | async-done | bytes 602128 | tf_op jit(solution)/shard_map/reduce_scatter | solution.py:46
  1061.8 49.2 %all-gather.40.cloned.1.call-done = bf16[1568,768]{1,0:T(8,128)(2,1)} async-done(((bf16[392,768]{1,0:T(8,128)(2,1)}), bf16[1568,768]{1,0:T(8,128)(2,1)}) %all-gather.40.cloned.1.call-update) | async-done | bytes 2408464 | tf_op jit(solution)/shard_map/all_gather | solution.py:38
  1131.1 5.3 convolution_convert_fusion.4
  1136.8 25.9 %all-gather.46.cloned.1.call-done = bf16[1568,768]{1,0:T(8,128)(2,1)} async-done(((bf16[392,768]{1,0:T(8,128)(2,1)}), bf16[1568,768]{1,0:T(8,128)(2,1)}) %all-gather.46.cloned.1.call-update) | async-done | bytes 2408464 | tf_op jit(solution)/shard_map/all_gather | solution.py:38
  1182.7 5.1 convolution_convert_fusion.1
  1188.1 26.1 %reduce-scatter.42.cloned.1.call-done = bf16[392,768]{1,0:T(8,128)(2,1)} async-done(((bf16[1568,768]{1,0:T(8,128)(2,1)}), bf16[392,768]{1,0:T(8,128)(2,1)}) %reduce-scatter.42.cloned.1.call-update) | async-done | bytes 602128 | tf_op jit(solution)/shard_map/reduce_scatter | solution.py:59
  1215.7 49.3 %reduce-scatter.48.cloned.1.call-done = bf16[392,768]{1,0:T(8,128)(2,1)} async-done(((bf16[1568,768]{1,0:T(8,128)(2,1)}), bf16[392,768]{1,0:T(8,128)(2,1)}) %reduce-scatter.48.cloned.1.call-update) | async-done | bytes 602128 | tf_op jit(solution)/shard_map/reduce_scatter | solution.py:59
  1287.3 34.1 %all-gather.42.cloned.1.call-done = bf16[1568,768]{1,0:T(8,128)(2,1)} async-done(((bf16[392,768]{1,0:T(8,128)(2,1)}), bf16[1568,768]{1,0:T(8,128)(2,1)}) %all-gather.42.cloned.1.call-update) | async-done | bytes 2408464 | tf_op jit(solution)/shard_map/all_gather | solution.py:38
  1326.6 46.9 %all-gather.48.cloned.1.call-done = bf16[1568,768]{1,0:T(8,128)(2,1)} async-done(((bf16[392,768]{1,0:T(8,128)(2,1)}), bf16[1568,768]{1,0:T(8,128)(2,1)}) %all-gather.48.cloned.1.call-update) | async-done | bytes 2408464 | tf_op jit(solution)/shard_map/all_gather | solution.py:38
  1405.2 6.7 copy.326
  1417.1 4.7 convolution_convert_fusion.3
  1453.5 6.7 copy.346
  1460.2 4.3 convert_element_type.455
  1465.9 4.7 convolution_convert_fusion
  1484.5 6.8 copy.365
  1491.3 8.0 reshape.468
  1499.6 5.0 fusion.256
  1508.7 5.0 fusion.257
  1526.5 15.3 all-reduce.1
  1544.4 8.2 reduce-scatter.50.cloned.1.call-done
  1556.3 40.8 %all-reduce.4 = (f32[3,2,768]{2,1,0:T(2,128)S(1)}, f32[4,768]{1,0:T(4,128)S(1)}) all-reduce(f32[3,2,768]{2,1,0:T(2,128)S(1)} %maximum_add_fusion.2, f32[4,768]{1,0:T(4,128)S(1)} %maximum_add_fusion.3), channel_id=20, replica_groups=mesh['dp'=8,'tensor'=4] {'dp','tensor'}, use_global_device_ids=true, to_apply=%region_72.0.clone | all-reduce | flops 7680 | bytes 61440
  1608.5 44.3 %reduce-scatter.52.cloned.1.call-done = f32[96,768]{1,0:T(8,128)} async-done(((f32[768,768]{1,0:T(8,128)}), f32[96,768]{1,0:T(8,128)}) %reduce-scatter.52.cloned.1.call-update) | async-done | bytes 294928 | tf_op jit(solution)/shard_map/reduce_scatter | solution.py:285
  1652.8 46.3 %reduce-scatter.54.cloned.1.call-done = f32[768,96]{0,1:T(8,128)} async-done(((f32[768,768]{0,1:T(8,128)}), f32[768,96]{0,1:T(8,128)}) %reduce-scatter.54.cloned.1.call-update) | async-done | bytes 294928 | tf_op jit(solution)/shard_map/reduce_scatter | solution.py:286
  1699.1 104.7 %reduce-scatter.56.cloned.1.call-done = f32[24,768]{1,0:T(8,128)} async-done(((f32[768,768]{1,0:T(8,128)}), f32[24,768]{1,0:T(8,128)}) %reduce-scatter.56.cloned.1.call-update) | async-done | bytes 73744 | tf_op jit(solution)/shard_map/reduce_scatter | solution.py:292
  (607 shorter events, 335.9 us)
Async XLA Ops:
  7.2 66.7 %copy-start.4 = (bf16[2,392,768]{2,1,0:T(8,128)(2,1)S(1)}, bf16[2,392,768]{2,1,0:T(8,128)(2,1)}, u32[]{:S(2)}) copy-start(bf16[2,392,768]{2,1,0:T(8,128)(2,1)} %param.12) | copy-start | bytes 3612676
  7.2 108.3 %all-gather.20.cloned.1.call-start = ((), (), s32[]{:S(2)}) async-start(), calls=%async_computation.19 | async-start | bytes 2654208 | tf_op jit(solution)/shard_map/all_gather | solution.py:313
  9.3 133.3 %all-gather.18.cloned.1.call-start = ((), (), s32[]{:S(2)}) async-start(), calls=%async_computation.18 | async-start | bytes 3010560 | tf_op jit(solution)/shard_map/all_gather | solution.py:34
  87.9 267.2 %copy-start.79 = (f32[768]{0:T(1024)}, f32[768]{0:T(1024)S(1)}, u32[]{:S(2)}) copy-start(f32[768]{0:T(1024)S(1)} %get-tuple-element.89) | copy-start | bytes 9220
  89.6 104.8 %all-gather.32.cloned.1.call-start = ((), (), s32[]{:S(2)}) async-start(), calls=%async_computation.28 | async-start | bytes 3010560 | tf_op jit(solution)/shard_map/all_gather | solution.py:34
  90.3 210.3 %all-gather.22.cloned.1.call-start = ((), (), s32[]{:S(2)}) async-start(), calls=%async_computation.21 | async-start | bytes 1216512 | tf_op jit(solution)/shard_map/all_gather | solution.py:322
  90.9 210.9 %reduce-scatter.28.cloned.1.call-start = ((), (), s32[]{:S(2)}) async-start(), calls=%async_computation.20 | async-start | bytes 3010560 | tf_op jit(solution)/shard_map/reduce_scatter | solution.py:46
  115.5 115.4 %copy-start.49 = (bf16[1,192,768]{2,1,0:T(8,128)(2,1)}, bf16[1,192,768]{2,1,0:T(8,128)(2,1)S(1)}, u32[]{:S(2)}) copy-start(bf16[1,192,768]{2,1,0:T(8,128)(2,1)S(1)} %copy.382) | copy-start | bytes 884740
  181.9 170.5 %reduce-scatter.34.cloned.1.call-start = ((), (), s32[]{:S(2)}) async-start(), calls=%async_computation.29 | async-start | bytes 3010560 | tf_op jit(solution)/shard_map/reduce_scatter | solution.py:46
  233.2 173.7 %all-gather.24.cloned.1.call-start = ((), (), s32[]{:S(2)}) async-start(), calls=%async_computation.22 | async-start | bytes 3010560 | tf_op jit(solution)/shard_map/all_gather | solution.py:34
  300.6 51.9 %copy-start.96 = (f32[768]{0:T(1024)}, f32[768]{0:T(1024)S(1)}, u32[]{:S(2)}) copy-start(f32[768]{0:T(1024)S(1)} %get-tuple-element.101) | copy-start | bytes 9220
  304.0 256.9 %copy-start.2 = (f32[392,768]{1,0:T(8,128)}, f32[392,768]{1,0:T(8,128)S(1)}, u32[]{:S(2)}) copy-start(f32[392,768]{1,0:T(8,128)S(1)} %get-tuple-element.220) | copy-start | bytes 3612676
  304.0 51.2 %copy-start.90 = (f32[392]{0:T(512)}, f32[392]{0:T(512)S(1)}, u32[]{:S(2)}) copy-start(f32[392]{0:T(512)S(1)} %broadcast_multiply_fusion.4) | copy-start | bytes 4708
  304.3 50.5 %copy-start.116 = (f32[392]{0:T(512)}, f32[392]{0:T(512)S(1)}, u32[]{:S(2)}) copy-start(f32[392]{0:T(512)S(1)} %multiply_reduce_fusion.7) | copy-start | bytes 4708
  304.3 50.9 %copy-start.98 = (f32[392]{0:T(512)}, f32[392]{0:T(512)S(1)}, u32[]{:S(2)}) copy-start(f32[392]{0:T(512)S(1)} %fusion.208) | copy-start | bytes 4708
  354.8 206.1 %copy-start = (f32[392,768]{1,0:T(8,128)}, f32[392,768]{1,0:T(8,128)S(1)}, u32[]{:S(2)}) copy-start(f32[392,768]{1,0:T(8,128)S(1)} %get-tuple-element.224) | copy-start | bytes 3612676
  356.7 101.9 %all-gather.34.cloned.1.call-start = ((), (), s32[]{:S(2)}) async-start(), calls=%async_computation.30 | async-start | bytes 3010560 | tf_op jit(solution)/shard_map/all_gather | solution.py:34
  357.5 152.6 %reduce-scatter.30.cloned.1.call-start = ((), (), s32[]{:S(2)}) async-start(), calls=%async_computation.23 | async-start | bytes 3010560 | tf_op jit(solution)/shard_map/reduce_scatter | solution.py:46
  435.3 125.6 %reduce-scatter.36.cloned.1.call-start = ((), (), s32[]{:S(2)}) async-start(), calls=%async_computation.31 | async-start | bytes 3010560 | tf_op jit(solution)/shard_map/reduce_scatter | solution.py:46
  486.8 101.4 %all-gather.30.cloned.1.call-start = ((), (), s32[]{:S(2)}) async-start(), calls=%async_computation.26 | async-start | bytes 1327104 | tf_op jit(solution)/shard_map/all_gather | solution.py:316
  487.6 150.9 %all-gather.44.cloned.1.call-start = ((), (), s32[]{:S(2)}) async-start(), calls=%async_computation.40 | async-start | bytes 3010560 | tf_op jit(solution)/shard_map/all_gather | solution.py:38
  492.7 173.0 %all-gather.28.cloned.1.call-start = ((), (), s32[]{:S(2)}) async-start(), calls=%async_computation.25 | async-start | bytes 1327104 | tf_op jit(solution)/shard_map/all_gather | solution.py:315
  493.5 223.1 %all-gather.26.cloned.1.call-start = ((), (), s32[]{:S(2)}) async-start(), calls=%async_computation.24 | async-start | bytes 3010560 | tf_op jit(solution)/shard_map/all_gather | solution.py:34
  564.7 203.4 %all-gather.36.cloned.1.call-start = ((), (), s32[]{:S(2)}) async-start(), calls=%async_computation.32 | async-start | bytes 3010560 | tf_op jit(solution)/shard_map/all_gather | solution.py:34
  565.3 254.4 %all-gather.38.cloned.1.call-start = ((), (), s32[]{:S(2)}) async-start(), calls=%async_computation.34 | async-start | bytes 3010560 | tf_op jit(solution)/shard_map/all_gather | solution.py:38
  565.9 336.8 %reduce-scatter.40.cloned.1.call-start = ((), (), s32[]{:S(2)}) async-start(), calls=%async_computation.35 | async-start | bytes 3010560 | tf_op jit(solution)/shard_map/reduce_scatter | solution.py:59
  665.7 102.4 %copy-start.137 = (bf16[768,768]{1,0:T(8,128)(2,1)S(1)}, bf16[768,768]{1,0:T(8,128)(2,1)}, u32[]{:S(2)}) copy-start(bf16[768,768]{1,0:T(8,128)(2,1)} %all-gather.28.cloned.1.call-done) | copy-start | bytes 3538948
  819.7 30.8 %copy-start.138 = (bf16[768,768]{1,0:T(8,128)(2,1)S(1)}, bf16[768,768]{1,0:T(8,128)(2,1)}, u32[]{:S(2)}) copy-start(bf16[768,768]{1,0:T(8,128)(2,1)} %all-gather.28.cloned.1.call-done) | copy-start | bytes 3538948
  854.0 99.5 %reduce-scatter.46.cloned.1.call-start = ((), (), s32[]{:S(2)}) async-start(), calls=%async_computation.41 | async-start | bytes 3010560 | tf_op jit(solution)/shard_map/reduce_scatter | solution.py:59
  859.0 145.4 %reduce-scatter.38.cloned.1.call-start = ((), (), s32[]{:S(2)}) async-start(), calls=%async_computation.33 | async-start | bytes 3010560 | tf_op jit(solution)/shard_map/reduce_scatter | solution.py:46
  874.6 180.6 %reduce-scatter.32.cloned.1.call-start = ((), (), s32[]{:S(2)}) async-start(), calls=%async_computation.27 | async-start | bytes 3010560 | tf_op jit(solution)/shard_map/reduce_scatter | solution.py:46
  881.0 72.5 %copy-start.7 = (f32[392,768]{1,0:T(8,128)S(1)}, f32[392,768]{1,0:T(8,128)}, u32[]{:S(2)}) copy-start(f32[392,768]{1,0:T(8,128)} %copy-done.6) | copy-start | bytes 3612676
  881.0 72.5 %copy-start.9 = (f32[392,768]{1,0:T(8,128)S(1)}, f32[392,768]{1,0:T(8,128)}, u32[]{:S(2)}) copy-start(f32[392,768]{1,0:T(8,128)} %copy-done.8) | copy-start | bytes 3612676
  881.0 174.2 %copy-start.118 = (f32[768]{0:T(1024)S(1)}, f32[768]{0:T(1024)}, u32[]{:S(2)}) copy-start(f32[768]{0:T(1024)} %get-tuple-element.98) | copy-start | bytes 9220
  881.0 230.0 %all-gather.40.cloned.1.call-start = ((), (), s32[]{:S(2)}) async-start(), calls=%async_computation.36 | async-start | bytes 3010560 | tf_op jit(solution)/shard_map/all_gather | solution.py:38
  902.7 152.5 %copy-start.55 = (bf16[392,768]{1,0:T(8,128)(2,1)S(1)}, bf16[392,768]{1,0:T(8,128)(2,1)}, u32[]{:S(2)}) copy-start(bf16[392,768]{1,0:T(8,128)(2,1)} %reduce-scatter.40.cloned.1.call-done) | copy-start | bytes 1806340
  1060.7 102.0 %all-gather.46.cloned.1.call-start = ((), (), s32[]{:S(2)}) async-start(), calls=%async_computation.42 | async-start | bytes 3010560 | tf_op jit(solution)/shard_map/all_gather | solution.py:38
  1061.5 56.2 %copy-start.28 = (bf16[3,8,196,196]{2,3,1,0:T(8,128)(2,1)S(1)}, bf16[3,8,196,196]{2,3,1,0:T(8,128)(2,1)}, u32[]{:S(2)}) copy-start(bf16[3,8,196,196]{2,3,1,0:T(8,128)(2,1)} %copy-done.27) | copy-start | bytes 5531908
  1061.5 152.6 %reduce-scatter.42.cloned.1.call-start = ((), (), s32[]{:S(2)}) async-start(), calls=%async_computation.37 | async-start | bytes 3010560 | tf_op jit(solution)/shard_map/reduce_scatter | solution.py:59
  1136.4 33.0 %copy-start.26 = (bf16[3,8,196,196]{2,3,1,0:T(8,128)(2,1)S(1)}, bf16[3,8,196,196]{2,3,1,0:T(8,128)(2,1)}, u32[]{:S(2)}) copy-start(bf16[3,8,196,196]{2,3,1,0:T(8,128)(2,1)} %copy-done.25) | copy-start | bytes 5531908
  1136.4 128.6 %reduce-scatter.48.cloned.1.call-start = ((), (), s32[]{:S(2)}) async-start(), calls=%async_computation.43 | async-start | bytes 3010560 | tf_op jit(solution)/shard_map/reduce_scatter | solution.py:59
  1187.8 77.2 %copy-start.1 = (f32[392,768]{1,0:T(8,128)S(1)}, f32[392,768]{1,0:T(8,128)}, u32[]{:S(2)}) copy-start(f32[392,768]{1,0:T(8,128)} %copy-done) | copy-start | bytes 3612676
  1187.8 77.2 %copy-start.89 = (f32[392]{0:T(512)S(1)}, f32[392]{0:T(512)}, u32[]{:S(2)}) copy-start(f32[392]{0:T(512)} %copy-done.88) | copy-start | bytes 4708
  1187.8 77.1 %copy-start.99 = (f32[392]{0:T(512)S(1)}, f32[392]{0:T(512)}, u32[]{:S(2)}) copy-start(f32[392]{0:T(512)} %copy-done.98) | copy-start | bytes 4708
  1187.9 133.5 %all-gather.42.cloned.1.call-start = ((), (), s32[]{:S(2)}) async-start(), calls=%async_computation.38 | async-start | bytes 3010560 | tf_op jit(solution)/shard_map/all_gather | solution.py:38
  1214.2 50.8 %copy-start.29 = (bf16[392,768]{1,0:T(8,128)(2,1)S(1)}, bf16[392,768]{1,0:T(8,128)(2,1)}, u32[]{:S(2)}) copy-start(bf16[392,768]{1,0:T(8,128)(2,1)} %reduce-scatter.42.cloned.1.call-done) | copy-start | bytes 1806340
  1215.6 51.6 %copy-start.115 = (f32[392]{0:T(512)S(1)}, f32[392]{0:T(512)}, u32[]{:S(2)}) copy-start(f32[392]{0:T(512)} %copy-done.114) | copy-start | bytes 4708
  1215.6 51.6 %copy-start.101 = (f32[392]{0:T(512)S(1)}, f32[392]{0:T(512)}, u32[]{:S(2)}) copy-start(f32[392]{0:T(512)} %copy-done.100) | copy-start | bytes 4708
  1271.1 102.4 %all-gather.48.cloned.1.call-start = ((), (), s32[]{:S(2)}) async-start(), calls=%async_computation.44 | async-start | bytes 3010560 | tf_op jit(solution)/shard_map/all_gather | solution.py:38
  1274.9 244.0 %reduce-scatter.62.cloned.1.call-start = ((), (), s32[]{:S(2)}) async-start(), calls=%async_computation.51 | async-start | bytes 442368
  1282.1 260.4 %reduce-scatter.60.cloned.1.call-start = ((), (), s32[]{:S(2)}) async-start(), calls=%async_computation.50 | async-start | bytes 1327104
  1285.7 35.7 %copy-start.50 = (bf16[1,192,768]{2,1,0:T(8,128)(2,1)S(1)}, bf16[1,192,768]{2,1,0:T(8,128)(2,1)}, u32[]{:S(2)}) copy-start(bf16[1,192,768]{2,1,0:T(8,128)(2,1)} %copy-done.49) | copy-start | bytes 884740
  1287.3 37.8 %copy-start.52 = (bf16[1568,192]{0,1:T(8,128)(2,1)S(1)}, bf16[1568,192]{0,1:T(8,128)(2,1)}, u32[]{:S(2)}) copy-start(bf16[1568,192]{0,1:T(8,128)(2,1)} %copy-done.51) | copy-start | bytes 1806340
  1326.6 49.6 %copy-start.72 = (f32[1,192,768]{2,1,0:T(8,128)S(1)}, f32[1,192,768]{2,1,0:T(8,128)}, u32[]{:S(2)}) copy-start(f32[1,192,768]{2,1,0:T(8,128)} %convolution_bitcast_fusion.8) | copy-start | bytes 1769476
  1388.4 156.0 %reduce-scatter.44.cloned.1.call-start = ((), (), s32[]{:S(2)}) async-start(), calls=%async_computation.39 | async-start | bytes 3010560 | tf_op jit(solution)/shard_map/reduce_scatter | solution.py:59
  1421.9 130.7 %reduce-scatter.50.cloned.1.call-start = ((), (), s32[]{:S(2)}) async-start(), calls=%async_computation.45 | async-start | bytes 3010560 | tf_op jit(solution)/shard_map/reduce_scatter | solution.py:59
  1470.6 135.3 %reduce-scatter.58.cloned.1.call-start = ((), (), s32[]{:S(2)}) async-start(), calls=%async_computation.49 | async-start | bytes 3981312
  1499.4 153.4 %reduce-scatter.52.cloned.1.call-start = ((), (), s32[]{:S(2)}) async-start(), calls=%async_computation.46 | async-start | bytes 2654208 | tf_op jit(solution)/shard_map/reduce_scatter | solution.py:285
  1508.6 190.5 %reduce-scatter.54.cloned.1.call-start = ((), (), s32[]{:S(2)}) async-start(), calls=%async_computation.47 | async-start | bytes 2654208 | tf_op jit(solution)/shard_map/reduce_scatter | solution.py:286
  1517.7 286.1 %reduce-scatter.56.cloned.1.call-start = ((), (), s32[]{:S(2)}) async-start(), calls=%async_computation.48 | async-start | bytes 2433024 | tf_op jit(solution)/shard_map/reduce_scatter | solution.py:292
  1526.3 28.3 %copy-start.113 = (f32[392]{0:T(512)S(1)}, f32[392]{0:T(512)}, u32[]{:S(2)}) copy-start(f32[392]{0:T(512)} %copy-done.112) | copy-start | bytes 4708
  1526.3 28.3 %copy-start.111 = (f32[392]{0:T(512)S(1)}, f32[392]{0:T(512)}, u32[]{:S(2)}) copy-start(f32[392]{0:T(512)} %copy-done.110) | copy-start | bytes 4708
  1526.3 28.4 %copy-start.103 = (f32[392]{0:T(512)S(1)}, f32[392]{0:T(512)}, u32[]{:S(2)}) copy-start(f32[392]{0:T(512)} %copy-done.102) | copy-start | bytes 4708
  1526.3 28.4 %copy-start.105 = (f32[392]{0:T(512)S(1)}, f32[392]{0:T(512)}, u32[]{:S(2)}) copy-start(f32[392]{0:T(512)} %copy-done.104) | copy-start | bytes 4708
  (115 other events, 582.5 us)
Sparse Core Ops, SparseCore 0:
  10.5 30.0 all-gather.19
  89.7 52.9 all-gather.17
  144.2 50.1 all-gather.31
  197.1 54.2 all-gather.21
  254.1 47.5 reduce-scatter.27
  304.0 48.3 reduce-scatter.33
  356.8 50.0 all-gather.23
  408.5 50.0 all-gather.33
  461.6 48.5 reduce-scatter.29
  512.4 48.5 reduce-scatter.35
  562.8 25.3 all-gather.29
  589.6 48.8 all-gather.43
  640.4 25.3 all-gather.27
  667.7 48.8 all-gather.25
  718.0 50.0 all-gather.35
  769.6 50.0 all-gather.37
  854.1 48.5 reduce-scatter.39
  905.0 48.5 reduce-scatter.45
  955.8 48.5 reduce-scatter.37
  1006.6 48.5 reduce-scatter.31
  1060.9 50.0 all-gather.39
  1112.6 50.0 all-gather.45
  1165.6 48.5 reduce-scatter.41
  1216.4 48.5 reduce-scatter.47
  1271.2 50.0 all-gather.41
  1323.4 50.0 all-gather.47
  1376.4 35.1 reduce-scatter.61
  1414.8 36.7 reduce-scatter.59
  1454.6 47.2 reduce-scatter.43
  1504.0 48.4 reduce-scatter.49
  1556.5 49.4 reduce-scatter.57
  1610.3 42.4 reduce-scatter.51
  1656.6 42.4 reduce-scatter.53
  1705.8 97.9 reduce-scatter.55
where the time goes:
time: 1830 us; the launch traced here: 1810 us
  waiting for transfers between devices  1040 us (57%)
  local copies, waits for them, and re-layouts  233 us (13%)
  blocking collectives  220 us (12%)
  matrix products  219 us (12%)
  other arithmetic  74.1 us (4%)
  between operations  19.8 us (1%)
    all_gather x6, waiting for transfers between devices, gather_grads(): return lax.all_gather(grad_low, 'tensor', axis=0, tiled=True)  252 us
    reduce_scatter x6, waiting for transfers between devices, scatter_forward(): lax.psum_scatter(partial_rows(jnp.int32(0), local_rows * lax.axis_size('t...  215 us
    all_gather x6, waiting for transfers between devices, gather_rows(): return lax.all_gather(normed, 'tensor', axis=0, tiled=True)  186 us
    reduce_scatter x6, waiting for transfers between devices, scatter_backward(): lax.psum_scatter(partial_rows(jnp.int32(0), local_rows * lax.axis_size('t...  156 us
    reduce_scatter x1, waiting for transfers between devices, reduce_grads(): lax.psum_scatter(tfc_sum, ('dp', 'tensor'), scatter_dimension=0, tiled=True)  105 us
    unnamed x320, local copies, waits for them, and re-layouts  82.3 us
    dot_general x14, matrix products, times_transpose(): lax.dot_general(left, right, (((1,), (1,)), ((), ())), preferred_element_...  80.9 us
    unnamed x3, blocking collectives  70.6 us
  transfers between devices with their start and end apart: 34, of which 29 were waited for; matrix products, arithmetic and copies ran while one was open for 25% of the time, Pallas kernels for 0%

commit v1 on v0

v1 whole, which is shorter than its diff:
```python
from functools import partial

import jax
import jax.numpy as jnp
from jax import lax
from jax.experimental import pallas as pl
from jax.experimental.pallas import tpu as pltpu
from jax.sharding import PartitionSpec as P

FRAMES = 8
EPS = 1e-06
LOW = jnp.bfloat16
F32 = jnp.float32
NEG = -1e30


def dot_nn(left, right):
    return lax.dot_general(left, right, (((1,), (0,)), ((), ())), preferred_element_type=F32)


def dot_nt(left, right):
    return lax.dot_general(left, right, (((1,), (1,)), ((), ())), preferred_element_type=F32)


def dot_tn(left, right):
    return lax.dot_general(left, right, (((0,), (0,)), ((), ())), preferred_element_type=F32)


def line_moves(count):
    up = [(i, i + 1) for i in range(count - 1)]
    return up, [(b, a) for a, b in up]


def line_gather(block):
    count = lax.axis_size("tensor")
    place = lax.axis_index("tensor")
    up, down = line_moves(count)
    below, above = [block], [block]
    for _ in range(count - 1):
        below.append(lax.ppermute(below[-1], "tensor", up))
        above.append(lax.ppermute(above[-1], "tensor", down))
    back = [block] + [
        jnp.where(place >= k, below[k], above[count - k]) for k in range(1, count)
    ]
    ring = jnp.stack([back[(-j) % count] for j in range(count)] * 2)
    return lax.dynamic_slice_in_dim(ring, count - place, count, axis=0)


def line_scatter(blocks):
    count = lax.axis_size("tensor")
    place = lax.axis_index("tensor")
    up, down = line_moves(count)
    ahead = [
        lax.dynamic_index_in_dim(blocks, lax.rem(place + k, count), axis=0, keepdims=False)
        for k in range(count)
    ]
    zero = jnp.zeros_like(ahead[0])
    rise = [jnp.where(place + k < count, ahead[k], zero) for k in range(1, count)]
    fall = [jnp.where(place >= k, ahead[count - k], zero) for k in range(1, count)]
    sums = []
    for parts, moves in ((rise, up), (fall, down)):
        held = parts[-1]
        for k in range(count - 2, -1, -1):
            arrived = lax.ppermute(held, "tensor", moves)
            held = (parts[k].astype(F32) + arrived.astype(F32)).astype(LOW)
        sums.append(lax.ppermute(held, "tensor", moves))
    return ahead[0].astype(F32) + sums[0].astype(F32) + sums[1].astype(F32)


def swap_blocks(blocks, sign):
    count = lax.axis_size("tensor")
    moved = [blocks[0]]
    for k in range(1, count):
        pairs = [(i, (i + sign * k) % count) for i in range(count)]
        moved.append(lax.ppermute(blocks[k], "tensor", pairs))
    return jnp.concatenate(moved, axis=0)


def pair_lanes(rows):
    lane = lax.broadcasted_iota(jnp.int32, (rows, 128), 1)
    return lane < 64


def allowed(rows, group, keys):
    row = lax.broadcasted_iota(jnp.int32, (rows, rows), 0)
    col = lax.broadcasted_iota(jnp.int32, (rows, rows), 1)
    if keys is not None:
        return col < keys
    return (row // group) == (col // group)


def softmax_rows(query, keys, mask):
    scores = dot_nt(query, keys) * 0.125
    scores = jnp.where(mask, scores, NEG)
    top = jnp.max(scores, axis=-1, keepdims=True)
    grown = jnp.exp(scores - top)
    return grown / jnp.sum(grown, axis=-1, keepdims=True)


def attend_kernel(group, keys, width, mixed_ref, out_ref):
    rows = out_ref.shape[-2]
    mask = allowed(rows, group, keys)
    first = pair_lanes(rows)

    def pair(index, carry):
        at = pl.multiple_of(index * 128, 128)
        query = mixed_ref[:, pl.ds(at, 128)]
        key = mixed_ref[:, pl.ds(width + at, 128)]
        value = mixed_ref[:, pl.ds(2 * width + at, 128)]
        zero = jnp.zeros_like(query)
        total = jnp.zeros((rows, 128), F32)
        for side in (first, jnp.logical_not(first)):
            probs = softmax_rows(query, jnp.where(side, key, zero), mask).astype(LOW)
            total = total + dot_nn(probs, jnp.where(side, value, zero))
        out_ref[:, pl.ds(at, 128)] = total.astype(LOW)
        return carry

    lax.fori_loop(0, width // 128, pair, 0)


def attend_back_kernel(group, keys, width, mixed_ref, grad_ref, out_ref):
    rows = grad_ref.shape[-2]
    mask = allowed(rows, group, keys)
    first = pair_lanes(rows)

    def pair(index, carry):
        at = pl.multiple_of(index * 128, 128)
        query = mixed_ref[:, pl.ds(at, 128)]
        key = mixed_ref[:, pl.ds(width + at, 128)]
        value = mixed_ref[:, pl.ds(2 * width + at, 128)]
        grad = grad_ref[:, pl.ds(at, 128)]
        zero = jnp.zeros_like(query)
        dq = jnp.zeros((rows, 128), F32)
        dk = jnp.zeros((rows, 128), F32)
        dv = jnp.zeros((rows, 128), F32)
        for side in (first, jnp.logical_not(first)):
            key_side = jnp.where(side, key, zero)
            probs = softmax_rows(query, key_side, mask)
            grad_probs = dot_nt(grad, jnp.where(side, value, zero))
            inner = jnp.sum(grad_probs * probs, axis=-1, keepdims=True)
            grad_scores = ((probs * (grad_probs - inner)).astype(LOW)) * 0.125
            grad_scores = grad_scores.astype(LOW)
            dv = dv + dot_tn(probs.astype(LOW), jnp.where(side, grad, zero))
            dq = dq + dot_nn(grad_scores, key_side)
            dk = dk + dot_tn(grad_scores, jnp.where(side, query, zero))
        out_ref[:, pl.ds(at, 128)] = dq.astype(LOW)
        out_ref[:, pl.ds(width + at, 128)] = dk.astype(LOW)
        out_ref[:, pl.ds(2 * width + at, 128)] = dv.astype(LOW)
        return carry

    lax.fori_loop(0, width // 128, pair, 0)


def attend(mixed, blocks, rows, group, keys):
    width = mixed.shape[1] // 3
    out = pl.pallas_call(
        partial(attend_kernel, group, keys, width),
        grid=(blocks,),
        in_specs=[pl.BlockSpec((None, rows, 3 * width), lambda i: (i, 0, 0))],
        out_specs=pl.BlockSpec((None, rows, width), lambda i: (i, 0, 0)),
        out_shape=jax.ShapeDtypeStruct((blocks, rows, width), LOW),
        compiler_params=pltpu.CompilerParams(vmem_limit_bytes=32 << 20),
        name="attend",
    )(mixed.reshape(blocks, rows, 3 * width))
    return out.reshape(blocks * rows, width)


def attend_back(mixed, grad, blocks, rows, group, keys):
    width = grad.shape[1]
    out = pl.pallas_call(
        partial(attend_back_kernel, group, keys, width),
        grid=(blocks,),
        in_specs=[
            pl.BlockSpec((None, rows, 3 * width), lambda i: (i, 0, 0)),
            pl.BlockSpec((None, rows, width), lambda i: (i, 0, 0)),
        ],
        out_specs=pl.BlockSpec((None, rows, 3 * width), lambda i: (i, 0, 0)),
        out_shape=jax.ShapeDtypeStruct((blocks, rows, 3 * width), LOW),
        compiler_params=pltpu.CompilerParams(vmem_limit_bytes=32 << 20),
        name="attend_back",
    )(mixed.reshape(blocks, rows, 3 * width), grad.reshape(blocks, rows, width))
    return out.reshape(blocks * rows, 3 * width)


def norm_stats(rows):
    centred = rows - jnp.mean(rows, axis=-1, keepdims=True)
    scale = lax.rsqrt(jnp.mean(centred * centred, axis=-1, keepdims=True) + EPS)
    return centred * scale, scale


def norm_low(rows, gain, shift):
    return (norm_stats(rows)[0] * gain + shift).astype(LOW)


def norm_back(grad, rows, gain):
    unit, scale = norm_stats(rows)
    scaled = grad * gain
    mean_plain = jnp.mean(scaled, axis=-1, keepdims=True)
    mean_unit = jnp.mean(scaled * unit, axis=-1, keepdims=True)
    back = (scaled - mean_plain - unit * mean_unit) * scale
    return back, jnp.sum(grad * unit, axis=0), jnp.sum(grad, axis=0)


def column_sums(rows):
    return jnp.sum(rows.astype(F32), axis=0)


def gelu_parts(hidden):
    cdf = 0.5 * (1.0 + lax.erf(hidden * (2.0**-0.5)))
    return cdf


def gelu_slope(hidden):
    density = jnp.exp(-0.5 * hidden * hidden) * 0.3989422804014327
    return gelu_parts(hidden) + hidden * density


def shards(
    clips,
    clip_live,
    qkv_weight,
    proj_weight,
    fc1_weight,
    fc2_weight,
    attn_bias,
    fc1_bias,
    norm_params,
    tfc_weight,
    out_bias,
    cotangent,
):
    tp = lax.axis_size("tensor")
    place = lax.axis_index("tensor")
    slots, tokens, width = clips.shape
    part = qkv_weight.shape[3]
    drow = qkv_weight.shape[1]
    srow = tfc_weight.shape[0]
    hidden_part = fc1_weight.shape[1]
    frames = FRAMES // tp
    patches = tokens // frames
    share = patches // tp
    padded = -(-patches // 8) * 8
    images = slots * frames
    rows_f = images * padded
    group_rows = images * share
    block_rows = -(-group_rows // 8) * 8
    rows_t = slots * share * FRAMES

    small = jnp.concatenate(
        [
            norm_params.reshape(6, srow).T,
            out_bias.T,
            attn_bias.reshape(4, srow).T,
            fc1_bias.reshape(tp, srow).T,
        ],
        axis=1,
    )
    small_cols = small.shape[1]
    shared_cols = width + 256
    shared = jnp.concatenate(
        [tfc_weight, jnp.pad(small, ((0, 0), (0, 256 - small_cols)))], axis=1
    ).reshape(drow, shared_cols // tp)

    def branch_rows(both):
        qkv = both[:, :, : 3 * part].reshape(tp, drow, 3, part)
        proj = both[:, :, 3 * part : 4 * part]
        return [
            qkv.transpose(1, 2, 0, 3).reshape(drow, 3 * width),
            proj.transpose(1, 0, 2).reshape(drow, width),
        ]

    def spread(rows):
        return lax.all_gather(rows, "dp", axis=0, tiled=True)

    gathered = line_gather(
        jnp.concatenate([qkv_weight[0].reshape(drow, 3 * part), proj_weight[0].T, shared], axis=1)
    )
    shared_rows = gathered[:, :, 4 * part :].reshape(drow, shared_cols)
    time_all = spread(jnp.concatenate(branch_rows(gathered) + [shared_rows], axis=1))
    gathered = line_gather(
        jnp.concatenate([qkv_weight[1].reshape(drow, 3 * part), proj_weight[1].T], axis=1)
    )
    space_all = spread(jnp.concatenate(branch_rows(gathered), axis=1))
    gathered = line_gather(jnp.concatenate([fc1_weight, fc2_weight.T], axis=1))
    mlp_all = spread(
        jnp.concatenate(
            [
                gathered[:, :, :hidden_part].transpose(1, 0, 2).reshape(drow, tp * hidden_part),
                gathered[:, :, hidden_part:].transpose(1, 0, 2).reshape(drow, tp * hidden_part),
            ],
            axis=1,
        )
    )
    qkv_w = (time_all[:, : 3 * width], space_all[:, : 3 * width])
    proj_w = (time_all[:, 3 * width : 4 * width], space_all[:, 3 * width :])
    tfc_w = time_all[:, 4 * width : 5 * width]
    fc1_w = mlp_all[:, : tp * hidden_part]
    fc2_w = mlp_all[:, tp * hidden_part :]
    small_all = time_all[:, 5 * width : 5 * width + small_cols].astype(F32).T
    norms = small_all[:6].reshape(3, 2, width)
    out_b = small_all[6:10]
    dp = width // drow
    heads_local = attn_bias.shape[2]
    attn_b = (
        small_all[10:14]
        .reshape(2, 2, dp, tp, heads_local, -1)
        .transpose(0, 1, 3, 4, 2, 5)
        .reshape(2, 2, width)
    )
    hidden_b = (
        small_all[14 : 14 + tp].reshape(tp, dp, tp, srow).transpose(2, 1, 0, 3).reshape(-1)
    )
    bias_rows = [
        jnp.concatenate([attn_b[b, 0], jnp.zeros((width,), F32), attn_b[b, 1]]) for b in (0, 1)
    ]

    row = lax.broadcasted_iota(jnp.int32, (tp, block_rows, images, padded), 1)
    shift = lax.broadcasted_iota(jnp.int32, (tp, block_rows, images, padded), 0)
    image = lax.broadcasted_iota(jnp.int32, (tp, block_rows, images, padded), 2)
    patch = lax.broadcasted_iota(jnp.int32, (tp, block_rows, images, padded), 3)
    target = lax.rem(place + shift, tp)
    pick = ((row // share) == image) & ((row % share) + target * share == patch)
    pick = (pick & (row < group_rows)).astype(LOW).reshape(tp * block_rows, rows_f)
    row = lax.broadcasted_iota(jnp.int32, (rows_t, tp, block_rows), 0)
    shift = lax.broadcasted_iota(jnp.int32, (rows_t, tp, block_rows), 1)
    sent = lax.broadcasted_iota(jnp.int32, (rows_t, tp, block_rows), 2)
    source = lax.rem(place - shift + tp, tp)
    frame = row % FRAMES
    merge = (frame // frames) == source
    merge = merge & (
        ((row // (FRAMES * share)) * frames + frame % frames) * share + (row // FRAMES) % share
        == sent
    )
    merge = merge.astype(LOW).reshape(rows_t, tp * block_rows)

    def cut(rows):
        return [rows[k * block_rows : (k + 1) * block_rows] for k in range(tp)]

    def to_patches(rows):
        sent = dot_nn(pick, rows).astype(LOW)
        return dot_nn(merge, swap_blocks(cut(sent), 1))

    def to_frames(rows):
        sent = dot_tn(merge, rows).astype(LOW)
        return dot_tn(pick, swap_blocks(cut(sent), -1))

    def pad_rows(values):
        shaped = values.reshape(images, patches, width)
        return jnp.pad(shaped, ((0, 0), (0, padded - patches), (0, 0))).reshape(rows_f, width)

    def drop_rows(values):
        return values.reshape(images, padded, width)[:, :patches].reshape(slots, tokens, width)

    inputs_low = pad_rows(clips)
    live = jnp.repeat(clip_live.astype(F32), frames * padded)[:, None]

    def qkv_of(normed, b):
        return (dot_nn(normed, qkv_w[b]) + bias_rows[b]).astype(LOW)

    time_core = (rows_t // 112, 112, FRAMES, None)
    space_core = (images, padded, None, patches)

    inputs_t = to_patches(inputs_low)
    n1 = norm_low(inputs_t, norms[0, 0], norms[0, 1])
    mixed_t = qkv_of(n1, 0)
    heads_t = attend(mixed_t, *time_core)
    summed = (dot_nt(heads_t, proj_w[0]) + out_b[0]).astype(LOW)
    moved = (dot_nn(summed, tfc_w) + out_b[1]).astype(LOW)
    first = inputs_low.astype(F32) + to_frames(moved)
    n2 = norm_low(first, norms[1, 0], norms[1, 1])
    mixed_s = qkv_of(n2, 1)
    heads_s = attend(mixed_s, *space_core)
    second = first + dot_nt(heads_s, proj_w[1]) + out_b[2]
    n3 = norm_low(second, norms[2, 0], norms[2, 1])
    hidden = dot_nn(n3, fc1_w) + hidden_b
    active = (hidden * gelu_parts(hidden)).astype(LOW)
    result = second + dot_nt(active, fc2_w) + out_b[3]
    outputs = drop_rows((result * live).astype(LOW))

    grad_result = pad_rows(cotangent).astype(F32) * live
    grad_low = grad_result.astype(LOW)
    grad_fc2 = dot_tn(grad_low, active).astype(LOW)
    grad_hidden = (dot_nn(grad_low, fc2_w) * gelu_slope(hidden)).astype(LOW)
    grad_fc1 = dot_tn(n3, grad_hidden).astype(LOW)
    grad_n3 = dot_nt(grad_hidden, fc1_w)
    back, gain_m, shift_m = norm_back(grad_n3, second, norms[2, 0])
    grad_second = grad_result + back

    def branch_back(low, mixed, heads, normed, b, core):
        grad_proj = dot_tn(low, heads).astype(LOW)
        grad_heads = dot_nn(low, proj_w[b]).astype(LOW)
        grad_mixed = attend_back(mixed, grad_heads, *core)
        grad_qkv = dot_tn(normed, grad_mixed).astype(LOW)
        sums = column_sums(grad_mixed)
        grad_normed = dot_nt(grad_mixed, qkv_w[b])
        return grad_normed, grad_qkv, grad_proj, sums

    low_s = grad_second.astype(LOW)
    grad_n2, qkv_s, proj_s, sums_s = branch_back(low_s, mixed_s, heads_s, n2, 1, space_core)
    back, gain_s, shift_s = norm_back(grad_n2, first, norms[1, 0])
    grad_first = grad_second + back
    low_f = to_patches(grad_first.astype(LOW)).astype(LOW)
    grad_tfc = dot_tn(summed, low_f).astype(LOW)
    low_t = dot_nt(low_f, tfc_w).astype(LOW)
    grad_n1, qkv_t, proj_t, sums_t = branch_back(low_t, mixed_t, heads_t, n1, 0, time_core)
    back, gain_t, shift_t = norm_back(grad_n1, inputs_t, norms[0, 0])
    grad_inputs = grad_first + to_frames(back.astype(LOW))
    grad_clips = drop_rows(grad_inputs)

    feature = jnp.stack(
        [
            gain_t,
            shift_t,
            gain_s,
            shift_s,
            gain_m,
            shift_m,
            column_sums(low_t),
            column_sums(low_f),
            column_sums(low_s),
            column_sums(grad_low),
        ]
    )
    attn_sums = jnp.stack(
        [sums_t[:width], sums_t[2 * width :], sums_s[:width], sums_s[2 * width :]]
    )
    attn_sums = (
        attn_sums.reshape(4, tp, heads_local, dp, -1).transpose(0, 3, 1, 2, 4).reshape(4, width)
    )
    hidden_sums = (
        column_sums(grad_hidden).reshape(tp, dp, tp, srow).transpose(2, 1, 0, 3).reshape(tp, width)
    )
    small_grad = jnp.concatenate([feature, attn_sums, hidden_sums]).astype(LOW)
    small_grad = jnp.pad(small_grad, ((0, 256 - small_cols), (0, 0))).T

    def collect(rows):
        return lax.psum_scatter(rows, "dp", scatter_dimension=0, tiled=True)

    def split_cols(rows, pieces):
        return rows.reshape(drow, pieces, tp, -1).transpose(2, 0, 1, 3)

    fc2_done = line_scatter(split_cols(collect(grad_fc2), 1))
    fc1_done = line_scatter(split_cols(collect(grad_fc1), 1))

    def branch_blocks(rows):
        return jnp.concatenate(
            [
                split_cols(rows[:, : 3 * width], 3).reshape(tp, drow, 3 * part),
                split_cols(rows[:, 3 * width : 4 * width], 1).reshape(tp, drow, part),
            ],
            axis=2,
        )

    space_done = line_scatter(branch_blocks(collect(jnp.concatenate([qkv_s, proj_s], axis=1))))
    time_rows = collect(jnp.concatenate([qkv_t, proj_t, grad_tfc, small_grad], axis=1))
    shared_back = time_rows[:, 4 * width :].reshape(tp, srow, shared_cols)
    time_done = line_scatter(
        jnp.concatenate(
            [branch_blocks(time_rows), shared_back.reshape(tp, drow, shared_cols // tp)], axis=2
        )
    )
    grad_qkv = jnp.stack([time_done[:, : 3 * part], space_done[:, : 3 * part]]).reshape(
        2, drow, 3, part
    )
    grad_proj = jnp.stack([time_done[:, 3 * part : 4 * part].T, space_done[:, 3 * part :].T])
    shared_done = time_done[:, 4 * part :].reshape(srow, shared_cols)
    smalls = shared_done[:, width : width + small_cols].T
    return (
        outputs,
        grad_clips,
        grad_qkv,
        grad_proj,
        fc1_done.reshape(drow, hidden_part),
        fc2_done.reshape(drow, hidden_part).T,
        smalls[10:14].reshape(attn_bias.shape),
        smalls[14 : 14 + tp].reshape(fc1_bias.shape),
        smalls[:6].reshape(3, 2, srow),
        shared_done[:, :width],
        smalls[6:10],
    )


def solution(mesh):
    return jax.shard_map(
        shards,
        mesh=mesh,
        in_specs=(
            P("dp", "tensor", None),
            P("dp"),
            P(None, "dp", None, "tensor"),
            P(None, "tensor", "dp"),
            P("dp", "tensor"),
            P("tensor", "dp"),
            P(None, None, "tensor", "dp"),
            P("tensor", "dp"),
            P(None, None, ("dp", "tensor")),
            P(("dp", "tensor"), None),
            P(None, ("dp", "tensor")),
            P("dp", "tensor", None),
        ),
        out_specs=(
            P("dp", "tensor", None),
            P("dp", "tensor", None),
            P(None, "dp", None, "tensor"),
            P(None, "tensor", "dp"),
            P("dp", "tensor"),
            P("tensor", "dp"),
            P(None, None, "tensor", "dp"),
            P("tensor", "dp"),
            P(None, None, ("dp", "tensor")),
            P(("dp", "tensor"), None),
            P(None, ("dp", "tensor")),
        ),
        check_vma=False,
    )
```

time: 1830 us -> 662 us (0.36)
  waiting for transfers between devices: 1040 us -> 104 us
  blocking collectives: 220 us -> 0 us
  starting transfers between devices: 3.39 us -> 176 us
  local copies, waits for them, and re-layouts: 233 us -> 62.7 us
  Pallas kernels: 0 us -> 90.9 us
  matrix products: 219 us -> 140 us
    reduce_scatter x15 -> x4, waiting for transfers between devices: 567 us -> 0.03 us  [collect(): return lax.psum_scatter(rows, 'dp', scatter_dimension=0, tiled=True)]
    all_gather x16 -> x3, waiting for transfers between devices: 466 us -> 0.04 us  [spread(): return lax.all_gather(rows, 'dp', axis=0, tiled=True)]
    ppermute x0 -> x62, starting transfers between devices: none -> 175 us  [the longest x24 69.2 us: line_scatter(): arrived = lax.ppermute(held, 'tensor', moves)]
    all_gather x4 -> x0, blocking collectives: 150 us -> none  [the longest x1 65.8 us: shards(): lax.all_gather(out_bias, ('dp', 'tensor'), axis=1, tiled=True)]
    ppermute x0 -> x62, waiting for transfers between devices: none -> 103 us  [the longest x12 58.1 us: swap_blocks(): moved.append(lax.ppermute(blocks[k], 'tensor', pairs))]
    pallas_call x0 -> x4, Pallas kernels: none -> 90.9 us  [the longest x2 50.9 us: attend_back(): pl.pallas_call(partial(attend_back_kernel, group, keys, width), grid=(blo...]
    dot_general x66 -> x28, matrix products: 219 us -> 140 us  [the longest x10 50.3 us: dot_nn(): lax.dot_general(left, right, (((1,), (0,)), ((), ())), preferred_element_...]
    unnamed x3 -> x0, blocking collectives: 70.6 us -> none
  transfers between devices with their start and end apart: 34 -> 69, of which waited for: 29 -> 22; matrix products, arithmetic and copies ran while one was open for 25% -> 34% of each run, Pallas kernels for 0% -> 14%
where the time goes in v1:
time: 662 us; the launch traced here: 650 us
  starting transfers between devices  176 us (27%)
  matrix products  140 us (21%)
  waiting for transfers between devices  104 us (16%)
  Pallas kernels  90.9 us (14%)
  local copies, waits for them, and re-layouts  62.7 us (9%)
  other arithmetic  60.6 us (9%)
  between operations  17 us (3%)
    ppermute x24, starting transfers between devices, line_scatter(): arrived = lax.ppermute(held, 'tensor', moves)  69.2 us
    ppermute x12, waiting for transfers between devices, swap_blocks(): moved.append(lax.ppermute(blocks[k], 'tensor', pairs))  58.1 us
    pallas_call x2, Pallas kernels, attend_back(): pl.pallas_call(partial(attend_back_kernel, group, keys, width), grid=(blo...  50.9 us
    dot_general x10, matrix products, dot_nn(): lax.dot_general(left, right, (((1,), (0,)), ((), ())), preferred_element_...  50.3 us
    dot_general x11, matrix products, dot_tn(): lax.dot_general(left, right, (((0,), (0,)), ((), ())), preferred_element_...  48.8 us
    ppermute x9, starting transfers between devices, line_gather(): above.append(lax.ppermute(above[-1], 'tensor', down))  42.1 us
    dot_general x7, matrix products, dot_nt(): lax.dot_general(left, right, (((1,), (1,)), ((), ())), preferred_element_...  40.8 us
    pallas_call x2, Pallas kernels, attend(): pl.pallas_call(partial(attend_kernel, group, keys, width), grid=(blocks,)...  40 us
  transfers between devices with their start and end apart: 69, of which 22 were waited for; matrix products, arithmetic and copies ran while one was open for 34% of the time, Pallas kernels for 14%

profile of v1, /device:TPU:24, one launch (start us, length us, event | category | flops | bytes accessed | tf_op | source)
XLA Modules:
  0.0 650.2 jit_solution(11737072634285861009)
XLA Ops:
  17.3 5.2 collective-permute-start.6
  22.5 4.6 collective-permute-start.15
  28.3 3.6 collective-permute-done.15
  31.9 5.2 collective-permute-start.16
  38.4 4.6 collective-permute-start.7
  45.1 4.7 collective-permute-start.17
  51.1 4.6 collective-permute-start.8
  78.0 4.6 collective-permute-start.21
  86.7 4.4 collective-permute-start.22
  91.1 3.4 collective-permute-done.19
  96.0 4.4 collective-permute-start.23
  108.0 3.5 convolution_convert_fusion.8
  123.6 8.0 %collective-permute-done.1 = bf16[200,768]{1,0:T(8,128)(2,1)S(1)} collective-permute-done((bf16[200,768]{1,0:T(8,128)(2,1)S(1)}, bf16[200,768]{1,0:T(8,128)(2,1)S(1)}, u32[]{:S(2)}, u32[]{:S(2)}) %collective-permute-start.1) | collective-permute-done | bytes 307232 | tf_op jit(solution)/shard_map/ppermute | solution.py:75
  142.8 5.7 add_convert_fusion.1
  148.6 23.3 %attend.2 = bf16[7,112,768]{2,1,0:T(8,128)(2,1)S(1)} custom-call(bf16[7,112,2304]{2,1,0:T(8,128)(2,1)S(1)} %bitcast.253), custom_call_target="tpu_custom_call" | custom-call | tf_op jit(solution)/shard_map/attend/pallas_call | solution.py:156
  175.7 4.8 convolution_convert_fusion.7
  181.4 6.8 %collective-permute-start.11 = (bf16[200,768]{1,0:T(8,128)(2,1)}, bf16[200,768]{1,0:T(8,128)(2,1)}, u32[]{:S(2)}, u32[]{:S(2)}) collective-permute-start(bf16[200,768]{1,0:T(8,128)(2,1)} %get-tuple-element.105), channel_id=1, source_target_pairs={{0,1},{1,2},{2,3},{3,0},{4,5},{5,6},{6,7},{7,4},{8,9},{9,10},{10,1... | collective-permute-start | bytes 921608 | tf_op jit(solution)/shard_map/ppermute | solution.py:75
  196.3 18.2 %collective-permute-done.10 = bf16[200,768]{1,0:T(8,128)(2,1)} collective-permute-done((bf16[200,768]{1,0:T(8,128)(2,1)}, bf16[200,768]{1,0:T(8,128)(2,1)}, u32[]{:S(2)}, u32[]{:S(2)}) %collective-permute-start.10) | collective-permute-done | bytes 307232 | tf_op jit(solution)/shard_map/ppermute | solution.py:75
  214.6 4.0 fusion.149
  220.5 6.1 add_convert_fusion
  226.6 16.7 %attend.3 = bf16[4,200,768]{2,1,0:T(8,128)(2,1)S(1)} custom-call(bf16[4,200,2304]{2,1,0:T(8,128)(2,1)S(1)} %bitcast.249), custom_call_target="tpu_custom_call" | custom-call | tf_op jit(solution)/shard_map/attend/pallas_call | solution.py:156
  247.8 9.5 %multiply_convert_fusion = (bf16[800,3072]{1,0:T(8,128)(2,1)S(1)}, f32[800,3072]{1,0:T(8,128)}) fusion(f32[3072]{0:T(1024)S(1)} %add.424, bf16[768,6144]{1,0:T(8,128)(2,1)} %all-gather.8.cloned.1.call-done, f32[800,768]{1,0:T(8,128)} %copy-done.9, f32[768]{0:T(1024)S(1)} %copy-done.64, f32[768]{0:T(1024)S(1)} %get-tuple-element.82, ...), kind=kOutput, calls=%fused_computation.7 | convolution fusion | flops 3792691200 | bytes 21946624 | tf_op jit(solution)/shard_map/dot_general | solution.py:18
  259.7 7.2 %convolution_convert_fusion.2 = bf16[768,3072]{1,0:T(8,128)(2,1)} fusion(bf16[800,768]{1,0:T(8,128)(2,1)S(1)} %copy-done.25, bf16[800,3072]{1,0:T(8,128)(2,1)S(1)} %get-tuple-element.153), kind=kOutput, calls=%fused_computation.18 | convolution fusion | flops 3777232896 | bytes 10862592 | tf_op jit(solution)/shard_map/dot_general | solution.py:26
  266.9 10.3 %fusion.153 = (bf16[3072]{0:T(1024)(128)(2,1)S(1)}, bf16[800,3072]{1,0:T(8,128)(2,1)S(1)}) fusion(f32[800,3072]{1,0:T(8,128)} %get-tuple-element.154, f32[3072]{0:T(1024)S(1)} %add.424, bf16[800,768]{1,0:T(8,128)(2,1)} %fusion.37, bf16[768,6144]{1,0:T(8,128)(2,1)} %all-gather.8.cloned.1.call-done), kind=kOutput, calls=%fused_computation.365 | convolution fusion | flops 3804361728 | bytes 20711424 | tf_op jit(solution)/shard_map/dot_general | solution.py:18
  279.5 7.7 %convolution_convert_fusion.3 = bf16[768,3072]{1,0:T(8,128)(2,1)} fusion(bf16[800,3072]{1,0:T(8,128)(2,1)S(1)} %get-tuple-element.163, f32[800,768]{1,0:T(8,128)S(1)} %copy-done.10, f32[768]{0:T(1024)S(1)} %copy-done.64, f32[768]{0:T(1024)S(1)} %get-tuple-element.82, f32[800]{0:T(1024)S(1)} %add_rsqrt_fusion, f32[800]{0:T(1024)S(1)} %broadcast_multiply_fusion.4), kind=kOutput, calls=%fused_computation.19 | convolution fusion | flops 3780304896 | bytes 12103936 | tf_op jit(solution)/shard_map/dot_general | solution.py:26
  288.0 9.9 %multiply_reduce_fusion = (bf16[768]{0:T(1024)(128)(2,1)S(1)}, f32[800]{0:T(1024)S(1)}, f32[800]{0:T(1024)S(1)}, bf16[768]{0:T(1024)(128)(2,1)S(1)}, f32[800,768]{1,0:T(8,128)S(1)}) fusion(f32[800,768]{1,0:T(8,128)} %copy-done.9, f32[800]{0:T(1024)S(1)} %add_rsqrt_fusion, f32[800]{0:T(1024)S(1)} %broadcast_multiply_fusion.4, ...), kind=kOutput, calls=%fused_computation.63 | convolution fusion | flops 3780400128 | bytes 14567936 | tf_op jit(solution)/shard_map/dot_general | solution.py:22
  299.4 3.3 convolution_convert_fusion.6
  302.8 21.8 %attend_back.2 = bf16[4,200,2304]{2,1,0:T(8,128)(2,1)S(1)} custom-call(bf16[4,200,2304]{2,1,0:T(8,128)(2,1)S(1)} %bitcast.250, bf16[4,200,768]{2,1,0:T(8,128)(2,1)S(1)} %bitcast.259), custom_call_target="tpu_custom_call" | custom-call | tf_op jit(solution)/shard_map/attend_back/pallas_call | solution.py:170
  324.6 4.8 multiply_reduce_fusion.1
  330.9 4.4 convolution_convert_fusion
  338.3 4.1 multiply_add_fusion
  346.5 3.3 collective-permute-start.24
  353.4 4.3 collective-permute-done.26
  357.7 9.3 %collective-permute-done.25 = bf16[200,768]{1,0:T(8,128)(2,1)} collective-permute-done((bf16[200,768]{1,0:T(8,128)(2,1)S(1)}, bf16[200,768]{1,0:T(8,128)(2,1)}, u32[]{:S(2)}, u32[]{:S(2)}) %collective-permute-start.25) | collective-permute-done | bytes 307232 | tf_op jit(solution)/shard_map/ppermute | solution.py:75
  367.0 3.4 fusion.152
  376.2 29.1 %attend_back.3 = bf16[7,112,2304]{2,1,0:T(8,128)(2,1)S(1)} custom-call(bf16[7,112,2304]{2,1,0:T(8,128)(2,1)S(1)} %bitcast.254, bf16[7,112,768]{2,1,0:T(8,128)(2,1)S(1)} %bitcast.262), custom_call_target="tpu_custom_call" | custom-call | tf_op jit(solution)/shard_map/attend_back/pallas_call | solution.py:170
  410.1 7.8 %multiply_reduce_fusion.6 = (bf16[768]{0:T(1024)(128)(2,1)S(1)}, f32[784]{0:T(1024)S(1)}, f32[784]{0:T(1024)S(1)}, bf16[768]{0:T(1024)(128)(2,1)S(1)}, f32[784,768]{1,0:T(8,128)}) fusion(f32[784,768]{1,0:T(8,128)S(1)} %copy-done.20, f32[784]{0:T(1024)S(1)} %copy-done.58, f32[784]{0:T(1024)S(1)} %copy-done.35, f32[768]{0:T(1024)S(1)} %copy-done.60, ...), kind=kOutput, calls=%fused_computation.76 | convolution fusion | flops 2779948032 | bytes 11987200 | tf_op jit(solution)/shard_map/dot_general | solution.py:22
  424.2 4.4 convolution_convert_fusion.1
  428.6 3.3 pad_maximum_fusion
  432.0 5.0 convolution_convert_fusion.4
  437.8 9.2 %collective-permute-start.29 = (bf16[200,768]{1,0:T(8,128)(2,1)}, bf16[200,768]{1,0:T(8,128)(2,1)}, u32[]{:S(2)}, u32[]{:S(2)}) collective-permute-start(bf16[200,768]{1,0:T(8,128)(2,1)} %get-tuple-element.97), channel_id=1, source_target_pairs={{0,1},{1,2},{2,3},{3,0},{4,5},{5,6},{6,7},{7,4},{8,9},{9,10},{10,1... | collective-permute-start | bytes 921608 | tf_op jit(solution)/shard_map/ppermute | solution.py:75
  447.6 10.3 %multiply_convert_fusion.2 = bf16[800,768]{1,0:T(8,128)(2,1)} fusion(f32[800,768]{1,0:T(8,128)S(1)} %copy-done.12, bf16[800,3072]{1,0:T(8,128)(2,1)} %copy-done.81, bf16[768,6144]{1,0:T(8,128)(2,1)} %all-gather.8.cloned.1.call-done, f32[800]{0:T(1024)S(1)} %mul.251, f32[768]{0:T(1024)S(1)} %copy-done.37), kind=kOutput, calls=%fused_computation.69 | convolution fusion | flops 3777331200 | bytes 13326464 | tf_op jit(solution)/shard_map/dot_general | solution.py:22
  460.1 13.2 %collective-permute-done.28 = bf16[200,768]{1,0:T(8,128)(2,1)} collective-permute-done((bf16[200,768]{1,0:T(8,128)(2,1)S(1)}, bf16[200,768]{1,0:T(8,128)(2,1)}, u32[]{:S(2)}, u32[]{:S(2)}) %collective-permute-start.28) | collective-permute-done | bytes 307232 | tf_op jit(solution)/shard_map/ppermute | solution.py:75
  473.4 5.3 convolution_add_fusion
  487.9 4.5 collective-permute-start.58
  499.0 5.2 collective-permute-start.50
  509.4 4.6 collective-permute-start.42
  516.3 4.6 collective-permute-start.59
  524.1 4.6 collective-permute-start.51
  530.1 4.6 collective-permute-start.43
  536.1 4.6 collective-permute-start.60
  542.1 4.6 collective-permute-start.52
  550.8 5.9 collective-permute-start.61
  559.5 4.5 collective-permute-start.44
  564.7 4.3 collective-permute-start.53
  575.2 4.6 collective-permute-start.45
  582.8 5.2 collective-permute-done.30
  588.0 3.9 collective-permute-start.34
  592.0 3.8 collective-permute-done.34
  597.2 9.2 %collective-permute-done.31 = bf16[96,1024]{0,1:T(8,128)(2,1)S(1)} collective-permute-done((bf16[96,1024]{0,1:T(8,128)(2,1)S(1)}, bf16[96,1024]{0,1:T(8,128)(2,1)S(1)}, u32[]{:S(2)}, u32[]{:S(2)}) %collective-permute-start.31) | collective-permute-done | bytes 196640 | tf_op jit(solution)/shard_map/ppermute | solution.py:64
  606.4 4.3 collective-permute-start.35
  617.0 4.5 collective-permute-done.32
  621.6 3.8 collective-permute-start.36
  629.3 4.4 collective-permute-start.37
  (536 shorter events, 200.4 us)
Async XLA Ops:
  7.2 129.1 %all-gather.4.cloned.1.call-start = ((), (), s32[]{:S(2)}) async-start(), calls=%async_computation.4 | async-start | bytes 7077888 | tf_op jit(solution)/shard_map/all_gather | solution.py:273
  9.3 17.7 %collective-permute-start.12 = (bf16[96,768]{0,1:T(8,128)(2,1)S(1)}, bf16[96,768]{0,1:T(8,128)(2,1)S(1)}, u32[]{:S(2)}, u32[]{:S(2)}) collective-permute-start(bf16[96,768]{0,1:T(8,128)(2,1)S(1)} %pad_maximum_fusion.9), channel_id=1, source_target_pairs={{0,1},{1,2},{2,3},{4,5},{5,6},{6,7},{8,9},{9,10},{10,11},{12,13},{... | collective-permute-start | bytes 442376 | tf_op jit(solution)/shard_map/ppermute | solution.py:40
  16.0 21.1 %collective-permute-start.3 = (bf16[96,1024]{0,1:T(8,128)(2,1)S(1)}, bf16[96,1024]{0,1:T(8,128)(2,1)S(1)}, u32[]{:S(2)}, u32[]{:S(2)}) collective-permute-start(bf16[96,1024]{0,1:T(8,128)(2,1)S(1)} %pad_maximum_fusion.8), channel_id=1, source_target_pairs={{0,1},{1,2},{2,3},{4,5},{5,6},{6,7},{8,9},{9,10},{10,11},{12,13},{... | collective-permute-start | bytes 589832 | tf_op jit(solution)/shard_map/ppermute | solution.py:40
  17.3 21.1 %collective-permute-start.6 = (bf16[96,1024]{0,1:T(8,128)(2,1)S(1)}, bf16[96,1024]{0,1:T(8,128)(2,1)S(1)}, u32[]{:S(2)}, u32[]{:S(2)}) collective-permute-start(bf16[96,1024]{0,1:T(8,128)(2,1)S(1)} %pad_maximum_fusion.8), channel_id=1, source_target_pairs={{1,0},{2,1},{3,2},{5,4},{6,5},{7,6},{9,8},{10,9},{11,10},{13,12},{... | collective-permute-start | bytes 589832 | tf_op jit(solution)/shard_map/ppermute | solution.py:41
  22.5 9.5 %collective-permute-start.15 = (bf16[96,768]{0,1:T(8,128)(2,1)S(1)}, bf16[96,768]{0,1:T(8,128)(2,1)}, u32[]{:S(2)}, u32[]{:S(2)}) collective-permute-start(bf16[96,768]{0,1:T(8,128)(2,1)S(1)} %pad_maximum_fusion.9), channel_id=1, source_target_pairs={{1,0},{2,1},{3,2},{5,4},{6,5},{7,6},{9,8},{10,9},{11,10},{13,12},{... | collective-permute-start | bytes 442376 | tf_op jit(solution)/shard_map/ppermute | solution.py:41
  27.0 15.9 %collective-permute-start.13 = (bf16[96,768]{0,1:T(8,128)(2,1)S(1)}, bf16[96,768]{0,1:T(8,128)(2,1)}, u32[]{:S(2)}, u32[]{:S(2)}) collective-permute-start(bf16[96,768]{0,1:T(8,128)(2,1)S(1)} %collective-permute-done.12), channel_id=1, source_target_pairs={{0,1},{1,2},{2,3},{4,5},{5,6},{6,7},{8,9},{9,10},{10,11},{12,13},{... | collective-permute-start | bytes 442376 | tf_op jit(solution)/shard_map/ppermute | solution.py:40
  31.9 13.1 %collective-permute-start.16 = (bf16[96,768]{0,1:T(8,128)(2,1)}, bf16[96,768]{0,1:T(8,128)(2,1)}, u32[]{:S(2)}, u32[]{:S(2)}) collective-permute-start(bf16[96,768]{0,1:T(8,128)(2,1)} %collective-permute-done.15), channel_id=1, source_target_pairs={{1,0},{2,1},{3,2},{5,4},{6,5},{7,6},{9,8},{10,9},{11,10},{13,12},{... | collective-permute-start | bytes 442376 | tf_op jit(solution)/shard_map/ppermute | solution.py:41
  37.1 12.7 %collective-permute-start.4 = (bf16[96,1024]{0,1:T(8,128)(2,1)S(1)}, bf16[96,1024]{0,1:T(8,128)(2,1)S(1)}, u32[]{:S(2)}, u32[]{:S(2)}) collective-permute-start(bf16[96,1024]{0,1:T(8,128)(2,1)S(1)} %collective-permute-done.3), channel_id=1, source_target_pairs={{0,1},{1,2},{2,3},{4,5},{5,6},{6,7},{8,9},{9,10},{10,11},{12,13},{... | collective-permute-start | bytes 589832 | tf_op jit(solution)/shard_map/ppermute | solution.py:40
  38.4 12.7 %collective-permute-start.7 = (bf16[96,1024]{0,1:T(8,128)(2,1)S(1)}, bf16[96,1024]{0,1:T(8,128)(2,1)S(1)}, u32[]{:S(2)}, u32[]{:S(2)}) collective-permute-start(bf16[96,1024]{0,1:T(8,128)(2,1)S(1)} %collective-permute-done.6), channel_id=1, source_target_pairs={{1,0},{2,1},{3,2},{5,4},{6,5},{7,6},{9,8},{10,9},{11,10},{13,12},{... | collective-permute-start | bytes 589832 | tf_op jit(solution)/shard_map/ppermute | solution.py:41
  43.0 12.7 %collective-permute-start.14 = (bf16[96,768]{0,1:T(8,128)(2,1)}, bf16[96,768]{0,1:T(8,128)(2,1)}, u32[]{:S(2)}, u32[]{:S(2)}) collective-permute-start(bf16[96,768]{0,1:T(8,128)(2,1)} %collective-permute-done.13), channel_id=1, source_target_pairs={{0,1},{1,2},{2,3},{4,5},{5,6},{6,7},{8,9},{9,10},{10,11},{12,13},{... | collective-permute-start | bytes 442376 | tf_op jit(solution)/shard_map/ppermute | solution.py:40
  45.1 13.9 %collective-permute-start.17 = (bf16[96,768]{0,1:T(8,128)(2,1)}, bf16[96,768]{0,1:T(8,128)(2,1)S(1)}, u32[]{:S(2)}, u32[]{:S(2)}) collective-permute-start(bf16[96,768]{0,1:T(8,128)(2,1)} %collective-permute-done.16), channel_id=1, source_target_pairs={{1,0},{2,1},{3,2},{5,4},{6,5},{7,6},{9,8},{10,9},{11,10},{13,12},{... | collective-permute-start | bytes 442376 | tf_op jit(solution)/shard_map/ppermute | solution.py:41
  49.8 16.5 %collective-permute-start.5 = (bf16[96,1024]{0,1:T(8,128)(2,1)S(1)}, bf16[96,1024]{0,1:T(8,128)(2,1)S(1)}, u32[]{:S(2)}, u32[]{:S(2)}) collective-permute-start(bf16[96,1024]{0,1:T(8,128)(2,1)S(1)} %collective-permute-done.4), channel_id=1, source_target_pairs={{0,1},{1,2},{2,3},{4,5},{5,6},{6,7},{8,9},{9,10},{10,11},{12,13},{... | collective-permute-start | bytes 589832 | tf_op jit(solution)/shard_map/ppermute | solution.py:40
  51.1 15.4 %collective-permute-start.8 = (bf16[96,1024]{0,1:T(8,128)(2,1)S(1)}, bf16[96,1024]{0,1:T(8,128)(2,1)S(1)}, u32[]{:S(2)}, u32[]{:S(2)}) collective-permute-start(bf16[96,1024]{0,1:T(8,128)(2,1)S(1)} %collective-permute-done.7), channel_id=1, source_target_pairs={{1,0},{2,1},{3,2},{5,4},{6,5},{7,6},{9,8},{10,9},{11,10},{13,12},{... | collective-permute-start | bytes 589832 | tf_op jit(solution)/shard_map/ppermute | solution.py:41
  74.2 146.3 %all-gather.6.cloned.1.call-start = ((), (), s32[]{:S(2)}) async-start(), calls=%async_computation.5 | async-start | bytes 5308416 | tf_op jit(solution)/shard_map/all_gather | solution.py:273
  76.6 171.3 %all-gather.8.cloned.1.call-start = ((), (), s32[]{:S(2)}) async-start(), calls=%async_computation.6 | async-start | bytes 10616832 | tf_op jit(solution)/shard_map/all_gather | solution.py:273
  76.7 8.6 %collective-permute-start.18 = (bf16[96,1536]{1,0:T(8,128)(2,1)S(1)}, bf16[96,1536]{1,0:T(8,128)(2,1)S(1)}, u32[]{:S(2)}, u32[]{:S(2)}) collective-permute-start(bf16[96,1536]{1,0:T(8,128)(2,1)S(1)} %pad_maximum_fusion.7), channel_id=1, source_target_pairs={{0,1},{1,2},{2,3},{4,5},{5,6},{6,7},{8,9},{9,10},{10,11},{12,13},{... | collective-permute-start | bytes 884744 | tf_op jit(solution)/shard_map/ppermute | solution.py:40
  78.0 8.8 %collective-permute-start.21 = (bf16[96,1536]{1,0:T(8,128)(2,1)S(1)}, bf16[96,1536]{1,0:T(8,128)(2,1)S(1)}, u32[]{:S(2)}, u32[]{:S(2)}) collective-permute-start(bf16[96,1536]{1,0:T(8,128)(2,1)S(1)} %pad_maximum_fusion.7), channel_id=1, source_target_pairs={{1,0},{2,1},{3,2},{5,4},{6,5},{7,6},{9,8},{10,9},{11,10},{13,12},{... | collective-permute-start | bytes 884744 | tf_op jit(solution)/shard_map/ppermute | solution.py:41
  85.3 9.3 %collective-permute-start.19 = (bf16[96,1536]{1,0:T(8,128)(2,1)S(1)}, bf16[96,1536]{1,0:T(8,128)(2,1)S(1)}, u32[]{:S(2)}, u32[]{:S(2)}) collective-permute-start(bf16[96,1536]{1,0:T(8,128)(2,1)S(1)} %collective-permute-done.18), channel_id=1, source_target_pairs={{0,1},{1,2},{2,3},{4,5},{5,6},{6,7},{8,9},{9,10},{10,11},{12,13},{... | collective-permute-start | bytes 884744 | tf_op jit(solution)/shard_map/ppermute | solution.py:40
  86.7 9.3 %collective-permute-start.22 = (bf16[96,1536]{1,0:T(8,128)(2,1)S(1)}, bf16[96,1536]{1,0:T(8,128)(2,1)S(1)}, u32[]{:S(2)}, u32[]{:S(2)}) collective-permute-start(bf16[96,1536]{1,0:T(8,128)(2,1)S(1)} %collective-permute-done.21), channel_id=1, source_target_pairs={{1,0},{2,1},{3,2},{5,4},{6,5},{7,6},{9,8},{10,9},{11,10},{13,12},{... | collective-permute-start | bytes 884744 | tf_op jit(solution)/shard_map/ppermute | solution.py:41
  94.5 8.6 %collective-permute-start.20 = (bf16[96,1536]{1,0:T(8,128)(2,1)S(1)}, bf16[96,1536]{1,0:T(8,128)(2,1)S(1)}, u32[]{:S(2)}, u32[]{:S(2)}) collective-permute-start(bf16[96,1536]{1,0:T(8,128)(2,1)S(1)} %collective-permute-done.19), channel_id=1, source_target_pairs={{0,1},{1,2},{2,3},{4,5},{5,6},{6,7},{8,9},{9,10},{10,11},{12,13},{... | collective-permute-start | bytes 884744 | tf_op jit(solution)/shard_map/ppermute | solution.py:40
  96.0 8.6 %collective-permute-start.23 = (bf16[96,1536]{1,0:T(8,128)(2,1)S(1)}, bf16[96,1536]{1,0:T(8,128)(2,1)S(1)}, u32[]{:S(2)}, u32[]{:S(2)}) collective-permute-start(bf16[96,1536]{1,0:T(8,128)(2,1)S(1)} %collective-permute-done.22), channel_id=1, source_target_pairs={{1,0},{2,1},{3,2},{5,4},{6,5},{7,6},{9,8},{10,9},{11,10},{13,12},{... | collective-permute-start | bytes 884744 | tf_op jit(solution)/shard_map/ppermute | solution.py:41
  106.3 375.2 %reduce-scatter.11.cloned.1.call-start = ((), (), s32[]{:S(2)}) async-start(), calls=%async_computation.10 | async-start | bytes 5308416 | tf_op jit(solution)/shard_map/reduce_scatter | solution.py:437
  111.7 11.9 %collective-permute-start.2 = (bf16[200,768]{1,0:T(8,128)(2,1)S(1)}, bf16[200,768]{1,0:T(8,128)(2,1)S(1)}, u32[]{:S(2)}, u32[]{:S(2)}) collective-permute-start(bf16[200,768]{1,0:T(8,128)(2,1)S(1)} %get-tuple-element.109), channel_id=1, source_target_pairs={{0,3},{1,0},{2,1},{3,2},{4,7},{5,4},{6,5},{7,6},{8,11},{9,8},{10,9... | collective-permute-start | bytes 921608 | tf_op jit(solution)/shard_map/ppermute | solution.py:75
  114.2 17.3 %collective-permute-start.1 = (bf16[200,768]{1,0:T(8,128)(2,1)S(1)}, bf16[200,768]{1,0:T(8,128)(2,1)S(1)}, u32[]{:S(2)}, u32[]{:S(2)}) collective-permute-start(bf16[200,768]{1,0:T(8,128)(2,1)S(1)} %get-tuple-element.110), channel_id=1, source_target_pairs={{0,2},{1,3},{2,0},{3,1},{4,6},{5,7},{6,4},{7,5},{8,10},{9,11},{10,... | collective-permute-start | bytes 921608 | tf_op jit(solution)/shard_map/ppermute | solution.py:75
  116.8 14.7 %collective-permute-start = (bf16[200,768]{1,0:T(8,128)(2,1)S(1)}, bf16[200,768]{1,0:T(8,128)(2,1)S(1)}, u32[]{:S(2)}, u32[]{:S(2)}) collective-permute-start(bf16[200,768]{1,0:T(8,128)(2,1)S(1)} %get-tuple-element.111), channel_id=1, source_target_pairs={{0,1},{1,2},{2,3},{3,0},{4,5},{5,6},{6,7},{7,4},{8,9},{9,10},{10,1... | collective-permute-start | bytes 921608 | tf_op jit(solution)/shard_map/ppermute | solution.py:75
  181.4 14.9 %collective-permute-start.11 = (bf16[200,768]{1,0:T(8,128)(2,1)}, bf16[200,768]{1,0:T(8,128)(2,1)}, u32[]{:S(2)}, u32[]{:S(2)}) collective-permute-start(bf16[200,768]{1,0:T(8,128)(2,1)} %get-tuple-element.105), channel_id=1, source_target_pairs={{0,1},{1,2},{2,3},{3,0},{4,5},{5,6},{6,7},{7,4},{8,9},{9,10},{10,1... | collective-permute-start | bytes 921608 | tf_op jit(solution)/shard_map/ppermute | solution.py:75
  188.3 26.2 %collective-permute-start.10 = (bf16[200,768]{1,0:T(8,128)(2,1)}, bf16[200,768]{1,0:T(8,128)(2,1)}, u32[]{:S(2)}, u32[]{:S(2)}) collective-permute-start(bf16[200,768]{1,0:T(8,128)(2,1)} %get-tuple-element.106), channel_id=1, source_target_pairs={{0,2},{1,3},{2,0},{3,1},{4,6},{5,7},{6,4},{7,5},{8,10},{9,11},{10,... | collective-permute-start | bytes 921608 | tf_op jit(solution)/shard_map/ppermute | solution.py:75
  188.6 25.9 %collective-permute-start.9 = (bf16[200,768]{1,0:T(8,128)(2,1)S(1)}, bf16[200,768]{1,0:T(8,128)(2,1)}, u32[]{:S(2)}, u32[]{:S(2)}) collective-permute-start(bf16[200,768]{1,0:T(8,128)(2,1)S(1)} %get-tuple-element.107), channel_id=1, source_target_pairs={{0,3},{1,0},{2,1},{3,2},{4,7},{5,4},{6,5},{7,6},{8,11},{9,8},{10,9... | collective-permute-start | bytes 921608 | tf_op jit(solution)/shard_map/ppermute | solution.py:75
  266.9 225.6 %reduce-scatter.9.cloned.1.call-start = ((), (), s32[]{:S(2)}) async-start(), calls=%async_computation.9 | async-start | bytes 5308416 | tf_op jit(solution)/shard_map/reduce_scatter | solution.py:437
  287.2 217.0 %reduce-scatter.7.cloned.1.call-start = ((), (), s32[]{:S(2)}) async-start(), calls=%async_computation.8 | async-start | bytes 5308416 | tf_op jit(solution)/shard_map/reduce_scatter | solution.py:437
  338.2 232.9 %reduce-scatter.5.cloned.1.call-start = ((), (), s32[]{:S(2)}) async-start(), calls=%async_computation.7 | async-start | bytes 7077888 | tf_op jit(solution)/shard_map/reduce_scatter | solution.py:437
  345.6 12.1 %collective-permute-start.26 = (bf16[200,768]{1,0:T(8,128)(2,1)S(1)}, bf16[200,768]{1,0:T(8,128)(2,1)S(1)}, u32[]{:S(2)}, u32[]{:S(2)}) collective-permute-start(bf16[200,768]{1,0:T(8,128)(2,1)S(1)} %get-tuple-element.101), channel_id=1, source_target_pairs={{0,3},{1,0},{2,1},{3,2},{4,7},{5,4},{6,5},{7,6},{8,11},{9,8},{10,9... | collective-permute-start | bytes 921608 | tf_op jit(solution)/shard_map/ppermute | solution.py:75
  345.6 21.4 %collective-permute-start.25 = (bf16[200,768]{1,0:T(8,128)(2,1)S(1)}, bf16[200,768]{1,0:T(8,128)(2,1)}, u32[]{:S(2)}, u32[]{:S(2)}) collective-permute-start(bf16[200,768]{1,0:T(8,128)(2,1)S(1)} %get-tuple-element.102), channel_id=1, source_target_pairs={{0,2},{1,3},{2,0},{3,1},{4,6},{5,7},{6,4},{7,5},{8,10},{9,11},{10,... | collective-permute-start | bytes 921608 | tf_op jit(solution)/shard_map/ppermute | solution.py:75
  346.5 20.5 %collective-permute-start.24 = (bf16[200,768]{1,0:T(8,128)(2,1)S(1)}, bf16[200,768]{1,0:T(8,128)(2,1)}, u32[]{:S(2)}, u32[]{:S(2)}) collective-permute-start(bf16[200,768]{1,0:T(8,128)(2,1)S(1)} %get-tuple-element.103), channel_id=1, source_target_pairs={{0,1},{1,2},{2,3},{3,0},{4,5},{5,6},{6,7},{7,4},{8,9},{9,10},{10,1... | collective-permute-start | bytes 921608 | tf_op jit(solution)/shard_map/ppermute | solution.py:75
  437.8 22.3 %collective-permute-start.29 = (bf16[200,768]{1,0:T(8,128)(2,1)}, bf16[200,768]{1,0:T(8,128)(2,1)}, u32[]{:S(2)}, u32[]{:S(2)}) collective-permute-start(bf16[200,768]{1,0:T(8,128)(2,1)} %get-tuple-element.97), channel_id=1, source_target_pairs={{0,1},{1,2},{2,3},{3,0},{4,5},{5,6},{6,7},{7,4},{8,9},{9,10},{10,1... | collective-permute-start | bytes 921608 | tf_op jit(solution)/shard_map/ppermute | solution.py:75
  447.0 26.4 %collective-permute-start.28 = (bf16[200,768]{1,0:T(8,128)(2,1)S(1)}, bf16[200,768]{1,0:T(8,128)(2,1)}, u32[]{:S(2)}, u32[]{:S(2)}) collective-permute-start(bf16[200,768]{1,0:T(8,128)(2,1)S(1)} %get-tuple-element.98), channel_id=1, source_target_pairs={{0,2},{1,3},{2,0},{3,1},{4,6},{5,7},{6,4},{7,5},{8,10},{9,11},{10,... | collective-permute-start | bytes 921608 | tf_op jit(solution)/shard_map/ppermute | solution.py:75
  447.0 26.4 %collective-permute-start.27 = (bf16[200,768]{1,0:T(8,128)(2,1)S(1)}, bf16[200,768]{1,0:T(8,128)(2,1)}, u32[]{:S(2)}, u32[]{:S(2)}) collective-permute-start(bf16[200,768]{1,0:T(8,128)(2,1)S(1)} %get-tuple-element.99), channel_id=1, source_target_pairs={{0,3},{1,0},{2,1},{3,2},{4,7},{5,4},{6,5},{7,6},{8,11},{9,8},{10,9... | collective-permute-start | bytes 921608 | tf_op jit(solution)/shard_map/ppermute | solution.py:75
  485.9 23.5 %collective-permute-start.54 = (bf16[96,1,768]{2,0,1:T(8,128)(2,1)}, bf16[96,1,768]{2,0,1:T(8,128)(2,1)}, u32[]{:S(2)}, u32[]{:S(2)}) collective-permute-start(bf16[96,1,768]{2,0,1:T(8,128)(2,1)} %select_bitcast_fusion.5), channel_id=1, source_target_pairs={{0,1},{1,2},{2,3},{4,5},{5,6},{6,7},{8,9},{9,10},{10,11},{12,13},{... | collective-permute-start | bytes 442376 | tf_op jit(solution)/shard_map/ppermute | solution.py:64
  487.9 27.1 %collective-permute-start.58 = (bf16[96,1,768]{2,0,1:T(8,128)(2,1)}, bf16[96,1,768]{2,0,1:T(8,128)(2,1)S(1)}, u32[]{:S(2)}, u32[]{:S(2)}) collective-permute-start(bf16[96,1,768]{2,0,1:T(8,128)(2,1)} %select_bitcast_fusion.4), channel_id=1, source_target_pairs={{1,0},{2,1},{3,2},{5,4},{6,5},{7,6},{9,8},{10,9},{11,10},{13,12},{... | collective-permute-start | bytes 442376 | tf_op jit(solution)/shard_map/ppermute | solution.py:64
  497.7 18.5 %collective-permute-start.46 = (bf16[96,1,768]{2,0,1:T(8,128)(2,1)}, bf16[96,1,768]{2,0,1:T(8,128)(2,1)}, u32[]{:S(2)}, u32[]{:S(2)}) collective-permute-start(bf16[96,1,768]{2,0,1:T(8,128)(2,1)} %select_bitcast_fusion.7), channel_id=1, source_target_pairs={{0,1},{1,2},{2,3},{4,5},{5,6},{6,7},{8,9},{9,10},{10,11},{12,13},{... | collective-permute-start | bytes 442376 | tf_op jit(solution)/shard_map/ppermute | solution.py:64
  499.0 22.8 %collective-permute-start.50 = (bf16[96,1,768]{2,0,1:T(8,128)(2,1)}, bf16[96,1,768]{2,0,1:T(8,128)(2,1)}, u32[]{:S(2)}, u32[]{:S(2)}) collective-permute-start(bf16[96,1,768]{2,0,1:T(8,128)(2,1)} %select_bitcast_fusion.6), channel_id=1, source_target_pairs={{1,0},{2,1},{3,2},{5,4},{6,5},{7,6},{9,8},{10,9},{11,10},{13,12},{... | collective-permute-start | bytes 442376 | tf_op jit(solution)/shard_map/ppermute | solution.py:64
  508.0 16.1 %collective-permute-start.38 = (bf16[96,768]{0,1:T(8,128)(2,1)S(1)}, bf16[96,768]{0,1:T(8,128)(2,1)S(1)}, u32[]{:S(2)}, u32[]{:S(2)}) collective-permute-start(bf16[96,768]{0,1:T(8,128)(2,1)S(1)} %get-tuple-element.118), channel_id=1, source_target_pairs={{0,1},{1,2},{2,3},{4,5},{5,6},{6,7},{8,9},{9,10},{10,11},{12,13},{... | collective-permute-start | bytes 442376 | tf_op jit(solution)/shard_map/ppermute | solution.py:64
  509.4 19.3 %collective-permute-start.42 = (bf16[96,768]{0,1:T(8,128)(2,1)S(1)}, bf16[96,768]{0,1:T(8,128)(2,1)S(1)}, u32[]{:S(2)}, u32[]{:S(2)}) collective-permute-start(bf16[96,768]{0,1:T(8,128)(2,1)S(1)} %get-tuple-element.119), channel_id=1, source_target_pairs={{1,0},{2,1},{3,2},{5,4},{6,5},{7,6},{9,8},{10,9},{11,10},{13,12},{... | collective-permute-start | bytes 442376 | tf_op jit(solution)/shard_map/ppermute | solution.py:64
  514.9 15.2 %collective-permute-start.55 = (bf16[96,1,768]{2,0,1:T(8,128)(2,1)S(1)}, bf16[96,1,768]{2,0,1:T(8,128)(2,1)S(1)}, u32[]{:S(2)}, u32[]{:S(2)}) collective-permute-start(bf16[96,1,768]{2,0,1:T(8,128)(2,1)S(1)} %add_convert_fusion.12), channel_id=1, source_target_pairs={{0,1},{1,2},{2,3},{4,5},{5,6},{6,7},{8,9},{9,10},{10,11},{12,13},{... | collective-permute-start | bytes 442376 | tf_op jit(solution)/shard_map/ppermute | solution.py:64
  516.3 18.4 %collective-permute-start.59 = (bf16[96,1,768]{2,0,1:T(8,128)(2,1)S(1)}, bf16[96,1,768]{2,0,1:T(8,128)(2,1)S(1)}, u32[]{:S(2)}, u32[]{:S(2)}) collective-permute-start(bf16[96,1,768]{2,0,1:T(8,128)(2,1)S(1)} %add_convert_fusion.11), channel_id=1, source_target_pairs={{1,0},{2,1},{3,2},{5,4},{6,5},{7,6},{9,8},{10,9},{11,10},{13,12},{... | collective-permute-start | bytes 442376 | tf_op jit(solution)/shard_map/ppermute | solution.py:64
  521.8 14.3 %collective-permute-start.47 = (bf16[96,1,768]{2,0,1:T(8,128)(2,1)S(1)}, bf16[96,1,768]{2,0,1:T(8,128)(2,1)S(1)}, u32[]{:S(2)}, u32[]{:S(2)}) collective-permute-start(bf16[96,1,768]{2,0,1:T(8,128)(2,1)S(1)} %add_convert_fusion.14), channel_id=1, source_target_pairs={{0,1},{1,2},{2,3},{4,5},{5,6},{6,7},{8,9},{9,10},{10,11},{12,13},{... | collective-permute-start | bytes 442376 | tf_op jit(solution)/shard_map/ppermute | solution.py:64
  524.1 16.6 %collective-permute-start.51 = (bf16[96,1,768]{2,0,1:T(8,128)(2,1)S(1)}, bf16[96,1,768]{2,0,1:T(8,128)(2,1)S(1)}, u32[]{:S(2)}, u32[]{:S(2)}) collective-permute-start(bf16[96,1,768]{2,0,1:T(8,128)(2,1)S(1)} %add_convert_fusion.13), channel_id=1, source_target_pairs={{1,0},{2,1},{3,2},{5,4},{6,5},{7,6},{9,8},{10,9},{11,10},{13,12},{... | collective-permute-start | bytes 442376 | tf_op jit(solution)/shard_map/ppermute | solution.py:64
  528.7 13.3 %collective-permute-start.39 = (bf16[96,768]{0,1:T(8,128)(2,1)S(1)}, bf16[96,768]{0,1:T(8,128)(2,1)S(1)}, u32[]{:S(2)}, u32[]{:S(2)}) collective-permute-start(bf16[96,768]{0,1:T(8,128)(2,1)S(1)} %add_convert_fusion.10), channel_id=1, source_target_pairs={{0,1},{1,2},{2,3},{4,5},{5,6},{6,7},{8,9},{9,10},{10,11},{12,13},{... | collective-permute-start | bytes 442376 | tf_op jit(solution)/shard_map/ppermute | solution.py:64
  530.1 27.2 %collective-permute-start.43 = (bf16[96,768]{0,1:T(8,128)(2,1)S(1)}, bf16[96,768]{0,1:T(8,128)(2,1)S(1)}, u32[]{:S(2)}, u32[]{:S(2)}) collective-permute-start(bf16[96,768]{0,1:T(8,128)(2,1)S(1)} %add_convert_fusion.9), channel_id=1, source_target_pairs={{1,0},{2,1},{3,2},{5,4},{6,5},{7,6},{9,8},{10,9},{11,10},{13,12},{... | collective-permute-start | bytes 442376 | tf_op jit(solution)/shard_map/ppermute | solution.py:64
  534.8 12.0 %collective-permute-start.56 = (bf16[96,1,768]{2,0,1:T(8,128)(2,1)S(1)}, bf16[96,1,768]{2,0,1:T(8,128)(2,1)S(1)}, u32[]{:S(2)}, u32[]{:S(2)}) collective-permute-start(bf16[96,1,768]{2,0,1:T(8,128)(2,1)S(1)} %get-tuple-element.130), channel_id=1, source_target_pairs={{0,1},{1,2},{2,3},{4,5},{5,6},{6,7},{8,9},{9,10},{10,11},{12,13},{... | collective-permute-start | bytes 442376 | tf_op jit(solution)/shard_map/ppermute | solution.py:64
  536.1 12.7 %collective-permute-start.60 = (bf16[96,1,768]{2,0,1:T(8,128)(2,1)S(1)}, bf16[96,1,768]{2,0,1:T(8,128)(2,1)S(1)}, u32[]{:S(2)}, u32[]{:S(2)}) collective-permute-start(bf16[96,1,768]{2,0,1:T(8,128)(2,1)S(1)} %get-tuple-element.131), channel_id=1, source_target_pairs={{1,0},{2,1},{3,2},{5,4},{6,5},{7,6},{9,8},{10,9},{11,10},{13,12},{... | collective-permute-start | bytes 442376 | tf_op jit(solution)/shard_map/ppermute | solution.py:64
  540.8 10.0 %collective-permute-start.48 = (bf16[96,1,768]{2,0,1:T(8,128)(2,1)S(1)}, bf16[96,1,768]{2,0,1:T(8,128)(2,1)S(1)}, u32[]{:S(2)}, u32[]{:S(2)}) collective-permute-start(bf16[96,1,768]{2,0,1:T(8,128)(2,1)S(1)} %get-tuple-element.132), channel_id=1, source_target_pairs={{0,1},{1,2},{2,3},{4,5},{5,6},{6,7},{8,9},{9,10},{10,11},{12,13},{... | collective-permute-start | bytes 442376 | tf_op jit(solution)/shard_map/ppermute | solution.py:64
  542.1 21.9 %collective-permute-start.52 = (bf16[96,1,768]{2,0,1:T(8,128)(2,1)S(1)}, bf16[96,1,768]{2,0,1:T(8,128)(2,1)S(1)}, u32[]{:S(2)}, u32[]{:S(2)}) collective-permute-start(bf16[96,1,768]{2,0,1:T(8,128)(2,1)S(1)} %get-tuple-element.133), channel_id=1, source_target_pairs={{1,0},{2,1},{3,2},{5,4},{6,5},{7,6},{9,8},{10,9},{11,10},{13,12},{... | collective-permute-start | bytes 442376 | tf_op jit(solution)/shard_map/ppermute | solution.py:64
  546.8 11.9 %collective-permute-start.40 = (bf16[96,768]{0,1:T(8,128)(2,1)S(1)}, bf16[96,768]{0,1:T(8,128)(2,1)S(1)}, u32[]{:S(2)}, u32[]{:S(2)}) collective-permute-start(bf16[96,768]{0,1:T(8,128)(2,1)S(1)} %fusion.91), channel_id=1, source_target_pairs={{0,1},{1,2},{2,3},{4,5},{5,6},{6,7},{8,9},{9,10},{10,11},{12,13},{... | collective-permute-start | bytes 442376 | tf_op jit(solution)/shard_map/ppermute | solution.py:64
  548.8 26.4 %collective-permute-start.57 = (bf16[96,1,768]{2,0,1:T(8,128)(2,1)}, bf16[96,1,768]{2,0,1:T(8,128)(2,1)}, u32[]{:S(2)}, u32[]{:S(2)}) collective-permute-start(bf16[96,1,768]{2,0,1:T(8,128)(2,1)} %fusion.97), channel_id=1, source_target_pairs={{0,1},{1,2},{2,3},{4,5},{5,6},{6,7},{8,9},{9,10},{10,11},{12,13},{... | collective-permute-start | bytes 442376 | tf_op jit(solution)/shard_map/ppermute | solution.py:66
  550.8 29.0 %collective-permute-start.61 = (bf16[96,1,768]{2,0,1:T(8,128)(2,1)}, bf16[96,1,768]{2,0,1:T(8,128)(2,1)}, u32[]{:S(2)}, u32[]{:S(2)}) collective-permute-start(bf16[96,1,768]{2,0,1:T(8,128)(2,1)} %fusion.95), channel_id=1, source_target_pairs={{1,0},{2,1},{3,2},{5,4},{6,5},{7,6},{9,8},{10,9},{11,10},{13,12},{... | collective-permute-start | bytes 442376 | tf_op jit(solution)/shard_map/ppermute | solution.py:66
  557.3 53.4 %collective-permute-start.49 = (bf16[96,1,768]{2,0,1:T(8,128)(2,1)}, bf16[96,1,768]{2,0,1:T(8,128)(2,1)}, u32[]{:S(2)}, u32[]{:S(2)}) collective-permute-start(bf16[96,1,768]{2,0,1:T(8,128)(2,1)} %fusion.103), channel_id=1, source_target_pairs={{0,1},{1,2},{2,3},{4,5},{5,6},{6,7},{8,9},{9,10},{10,11},{12,13},{... | collective-permute-start | bytes 442376 | tf_op jit(solution)/shard_map/ppermute | solution.py:66
  559.5 9.5 %collective-permute-start.44 = (bf16[96,768]{0,1:T(8,128)(2,1)S(1)}, bf16[96,768]{0,1:T(8,128)(2,1)S(1)}, u32[]{:S(2)}, u32[]{:S(2)}) collective-permute-start(bf16[96,768]{0,1:T(8,128)(2,1)S(1)} %get-tuple-element.117), channel_id=1, source_target_pairs={{1,0},{2,1},{3,2},{5,4},{6,5},{7,6},{9,8},{10,9},{11,10},{13,12},{... | collective-permute-start | bytes 442376 | tf_op jit(solution)/shard_map/ppermute | solution.py:64
  564.7 47.3 %collective-permute-start.53 = (bf16[96,1,768]{2,0,1:T(8,128)(2,1)}, bf16[96,1,768]{2,0,1:T(8,128)(2,1)}, u32[]{:S(2)}, u32[]{:S(2)}) collective-permute-start(bf16[96,1,768]{2,0,1:T(8,128)(2,1)} %fusion.101), channel_id=1, source_target_pairs={{1,0},{2,1},{3,2},{5,4},{6,5},{7,6},{9,8},{10,9},{11,10},{13,12},{... | collective-permute-start | bytes 442376 | tf_op jit(solution)/shard_map/ppermute | solution.py:66
  569.0 56.4 %collective-permute-start.41 = (bf16[96,768]{0,1:T(8,128)(2,1)}, bf16[96,768]{0,1:T(8,128)(2,1)}, u32[]{:S(2)}, u32[]{:S(2)}) collective-permute-start(bf16[96,768]{0,1:T(8,128)(2,1)} %get-tuple-element.116), channel_id=1, source_target_pairs={{0,1},{1,2},{2,3},{4,5},{5,6},{6,7},{8,9},{9,10},{10,11},{12,13},{... | collective-permute-start | bytes 442376 | tf_op jit(solution)/shard_map/ppermute | solution.py:66
  575.2 50.3 %collective-permute-start.45 = (bf16[96,768]{0,1:T(8,128)(2,1)}, bf16[96,768]{0,1:T(8,128)(2,1)S(1)}, u32[]{:S(2)}, u32[]{:S(2)}) collective-permute-start(bf16[96,768]{0,1:T(8,128)(2,1)} %fusion.90), channel_id=1, source_target_pairs={{1,0},{2,1},{3,2},{5,4},{6,5},{7,6},{9,8},{10,9},{11,10},{13,12},{... | collective-permute-start | bytes 442376 | tf_op jit(solution)/shard_map/ppermute | solution.py:66
  595.8 10.6 %collective-permute-start.31 = (bf16[96,1024]{0,1:T(8,128)(2,1)S(1)}, bf16[96,1024]{0,1:T(8,128)(2,1)S(1)}, u32[]{:S(2)}, u32[]{:S(2)}) collective-permute-start(bf16[96,1024]{0,1:T(8,128)(2,1)S(1)} %add_convert_fusion.8), channel_id=1, source_target_pairs={{0,1},{1,2},{2,3},{4,5},{5,6},{6,7},{8,9},{9,10},{10,11},{12,13},{... | collective-permute-start | bytes 589832 | tf_op jit(solution)/shard_map/ppermute | solution.py:64
  606.4 10.6 %collective-permute-start.35 = (bf16[96,1024]{0,1:T(8,128)(2,1)S(1)}, bf16[96,1024]{0,1:T(8,128)(2,1)S(1)}, u32[]{:S(2)}, u32[]{:S(2)}) collective-permute-start(bf16[96,1024]{0,1:T(8,128)(2,1)S(1)} %add_convert_fusion.7), channel_id=1, source_target_pairs={{1,0},{2,1},{3,2},{5,4},{6,5},{7,6},{9,8},{10,9},{11,10},{13,12},{... | collective-permute-start | bytes 589832 | tf_op jit(solution)/shard_map/ppermute | solution.py:64
  610.8 10.7 %collective-permute-start.32 = (bf16[96,1024]{0,1:T(8,128)(2,1)S(1)}, bf16[96,1024]{0,1:T(8,128)(2,1)S(1)}, u32[]{:S(2)}, u32[]{:S(2)}) collective-permute-start(bf16[96,1024]{0,1:T(8,128)(2,1)S(1)} %fusion.86), channel_id=1, source_target_pairs={{0,1},{1,2},{2,3},{4,5},{5,6},{6,7},{8,9},{9,10},{10,11},{12,13},{... | collective-permute-start | bytes 589832 | tf_op jit(solution)/shard_map/ppermute | solution.py:64
  (94 other events, 804.7 us)
Sparse Core Ops, SparseCore 0:
  74.3 46.4 all-gather.3
  123.3 39.0 all-gather.5
  164.3 58.8 all-gather.7
  267.0 55.5 reduce-scatter.10
  326.2 53.8 reduce-scatter.8
  383.4 53.9 reduce-scatter.6
  441.2 61.7 reduce-scatter.4

commit v2 on v1

v2 whole, which is shorter than its diff:
```python
from functools import partial

import jax
import jax.numpy as jnp
from jax import lax
from jax.experimental import pallas as pl
from jax.experimental.pallas import tpu as pltpu
from jax.sharding import PartitionSpec as P

FRAMES = 8
EPS = 1e-06
LOW = jnp.bfloat16
F32 = jnp.float32
NEG = -1e30


def dot_nn(left, right):
    return lax.dot_general(left, right, (((1,), (0,)), ((), ())), preferred_element_type=F32)


def dot_nt(left, right):
    return lax.dot_general(left, right, (((1,), (1,)), ((), ())), preferred_element_type=F32)


def dot_tn(left, right):
    return lax.dot_general(left, right, (((0,), (0,)), ((), ())), preferred_element_type=F32)


def line_shift(block, step):
    count = lax.axis_size("tensor")
    return lax.ppermute(block, "tensor", [(i, (i + step) % count) for i in range(count)])


def line_gather(block):
    return [block] + [line_shift(block, k) for k in range(1, lax.axis_size("tensor"))]


def line_order(back):
    count = lax.axis_size("tensor")
    ring = jnp.stack([back[(-j) % count] for j in range(count)] * 2)
    return lax.dynamic_slice_in_dim(ring, count - lax.axis_index("tensor"), count, axis=0)


def line_scatter(blocks):
    count = lax.axis_size("tensor")
    place = lax.axis_index("tensor")
    parts = []
    for k in range(count):
        ahead = lax.dynamic_index_in_dim(
            blocks, lax.rem(place + k, count), axis=0, keepdims=False
        )
        parts.append(ahead if k == 0 else line_shift(ahead, k))
    return parts


def line_total(parts):
    total = parts[0].astype(F32)
    for part in parts[1:]:
        total = total + part.astype(F32)
    return total


def swap_blocks(blocks, sign):
    count = lax.axis_size("tensor")
    moved = [blocks[0]]
    for k in range(1, count):
        pairs = [(i, (i + sign * k) % count) for i in range(count)]
        moved.append(lax.ppermute(blocks[k], "tensor", pairs))
    return jnp.concatenate(moved, axis=0)


def pair_sides(values, first):
    wide = values.astype(F32)
    zero = jnp.zeros_like(wide)
    both = [jnp.where(first, wide, zero), jnp.where(first, zero, wide)]
    return jnp.concatenate(both, axis=0).astype(LOW)


def key_mask(rows, group, keys):
    key = lax.broadcasted_iota(jnp.int32, (2, rows, rows), 1)
    query = lax.broadcasted_iota(jnp.int32, (2, rows, rows), 2)
    if keys is not None:
        return key < keys
    return (key // group) == (query // group)


def pair_probs(query, key_sides, mask, rows):
    scores = dot_nt(key_sides, query).reshape(2, rows, rows)
    scores = jnp.where(mask, scores, NEG)
    grown = jnp.exp(scores - jnp.max(scores, axis=1, keepdims=True))
    return grown * (1.0 / jnp.sum(grown, axis=1, keepdims=True))


def attend_kernel(group, keys, width, mixed_ref, out_ref):
    rows = out_ref.shape[-2]
    mask = key_mask(rows, group, keys)
    first = lax.broadcasted_iota(jnp.int32, (rows, 128), 1) < 64
    for at in range(0, width, 128):
        query = mixed_ref[:, at : at + 128] * LOW(0.125)
        key = pair_sides(mixed_ref[:, width + at : width + at + 128], first)
        value = pair_sides(mixed_ref[:, 2 * width + at : 2 * width + at + 128], first)
        probs = pair_probs(query, key, mask, rows).reshape(2 * rows, rows)
        out_ref[:, at : at + 128] = dot_tn(probs.astype(LOW), value).astype(LOW)


def attend_back_kernel(group, keys, width, mixed_ref, grad_ref, out_ref, sums_ref):
    rows = grad_ref.shape[-2]
    mask = key_mask(rows, group, keys)
    first = lax.broadcasted_iota(jnp.int32, (rows, 128), 1) < 64

    @pl.when(pl.program_id(0) == 0)
    def clear():
        sums_ref[...] = jnp.zeros_like(sums_ref)

    for at in range(0, width, 128):
        query = mixed_ref[:, at : at + 128] * LOW(0.125)
        key = pair_sides(mixed_ref[:, width + at : width + at + 128], first)
        value = pair_sides(mixed_ref[:, 2 * width + at : 2 * width + at + 128], first)
        grad = grad_ref[:, at : at + 128]
        probs = pair_probs(query, key, mask, rows)
        grad_probs = dot_nt(value, grad).reshape(2, rows, rows)
        inner = jnp.sum(grad_probs * probs, axis=1, keepdims=True)
        grad_scores = (probs * (grad_probs - inner)).reshape(2 * rows, rows).astype(LOW)
        probs_low = probs.reshape(2 * rows, rows).astype(LOW)
        dq = (dot_tn(grad_scores, key) * 0.125).astype(LOW)
        dk = dot_nn(grad_scores, query)
        dv = dot_nn(probs_low, grad)
        dk = jnp.where(first, dk[:rows], dk[rows:]).astype(LOW)
        dv = jnp.where(first, dv[:rows], dv[rows:]).astype(LOW)
        out_ref[:, at : at + 128] = dq
        out_ref[:, width + at : width + at + 128] = dk
        out_ref[:, 2 * width + at : 2 * width + at + 128] = dv
        for part, value in ((0, dq), (2, dv)):
            start = part * width + at
            total = jnp.sum(value.astype(F32), axis=0, keepdims=True)
            sums_ref[:, start : start + 128] = sums_ref[:, start : start + 128] + total


def attend(mixed, blocks, rows, group, keys):
    width = mixed.shape[1] // 3
    out = pl.pallas_call(
        partial(attend_kernel, group, keys, width),
        grid=(blocks,),
        in_specs=[pl.BlockSpec((None, rows, 3 * width), lambda i: (i, 0, 0))],
        out_specs=pl.BlockSpec((None, rows, width), lambda i: (i, 0, 0)),
        out_shape=jax.ShapeDtypeStruct((blocks, rows, width), LOW),
        compiler_params=pltpu.CompilerParams(vmem_limit_bytes=32 << 20),
        cost_estimate=pl.CostEstimate(
            flops=8_000_000_000, bytes_accessed=8 * blocks * rows * width, transcendentals=0
        ),
        name="attend",
    )(mixed.reshape(blocks, rows, 3 * width))
    return out.reshape(blocks * rows, width)


def attend_back(mixed, grad, blocks, rows, group, keys):
    width = grad.shape[1]
    out, sums = pl.pallas_call(
        partial(attend_back_kernel, group, keys, width),
        grid=(blocks,),
        in_specs=[
            pl.BlockSpec((None, rows, 3 * width), lambda i: (i, 0, 0)),
            pl.BlockSpec((None, rows, width), lambda i: (i, 0, 0)),
        ],
        out_specs=[
            pl.BlockSpec((None, rows, 3 * width), lambda i: (i, 0, 0)),
            pl.BlockSpec((1, 3 * width), lambda i: (0, 0)),
        ],
        out_shape=[
            jax.ShapeDtypeStruct((blocks, rows, 3 * width), LOW),
            jax.ShapeDtypeStruct((1, 3 * width), F32),
        ],
        compiler_params=pltpu.CompilerParams(vmem_limit_bytes=32 << 20),
        cost_estimate=pl.CostEstimate(
            flops=18_000_000_000, bytes_accessed=14 * blocks * rows * width, transcendentals=0
        ),
        name="attend_back",
    )(mixed.reshape(blocks, rows, 3 * width), grad.reshape(blocks, rows, width))
    return out.reshape(blocks * rows, 3 * width), sums[0]


def norm_stats(rows):
    centred = rows - jnp.mean(rows, axis=-1, keepdims=True)
    scale = lax.rsqrt(jnp.mean(centred * centred, axis=-1, keepdims=True) + EPS)
    return centred * scale, scale


def norm_low(rows, gain, shift):
    return (norm_stats(rows)[0] * gain + shift).astype(LOW)


def norm_back(grad, rows, gain):
    unit, scale = norm_stats(rows)
    scaled = grad * gain
    mean_plain = jnp.mean(scaled, axis=-1, keepdims=True)
    mean_unit = jnp.mean(scaled * unit, axis=-1, keepdims=True)
    back = (scaled - mean_plain - unit * mean_unit) * scale
    return back, jnp.sum(grad * unit, axis=0), jnp.sum(grad, axis=0)


def column_sums(rows):
    return jnp.sum(rows.astype(F32), axis=0)


def together(*values):
    return lax.optimization_barrier(values)


def shards(
    clips,
    clip_live,
    qkv_weight,
    proj_weight,
    fc1_weight,
    fc2_weight,
    attn_bias,
    fc1_bias,
    norm_params,
    tfc_weight,
    out_bias,
    cotangent,
):
    tp = lax.axis_size("tensor")
    place = lax.axis_index("tensor")
    slots, tokens, width = clips.shape
    part = qkv_weight.shape[3]
    drow = qkv_weight.shape[1]
    srow = tfc_weight.shape[0]
    hidden_part = fc1_weight.shape[1]
    frames = FRAMES // tp
    patches = tokens // frames
    share = patches // tp
    padded = -(-patches // 8) * 8
    images = slots * frames
    rows_f = images * padded
    group_rows = images * share
    block_rows = -(-group_rows // 8) * 8
    rows_t = slots * share * FRAMES

    small = jnp.concatenate(
        [
            norm_params.reshape(6, srow).T,
            out_bias.T,
            attn_bias.reshape(4, srow).T,
            fc1_bias.reshape(tp, srow).T,
        ],
        axis=1,
    )
    small_cols = small.shape[1]
    shared_cols = width + 256
    shared = jnp.concatenate(
        [tfc_weight, jnp.pad(small, ((0, 0), (0, 256 - small_cols)))], axis=1
    ).reshape(drow, shared_cols // tp)

    def branch_rows(both):
        qkv = both[:, :, : 3 * part].reshape(tp, drow, 3, part)
        proj = both[:, :, 3 * part : 4 * part]
        return [
            qkv.transpose(1, 2, 0, 3).reshape(drow, 3 * width),
            proj.transpose(1, 0, 2).reshape(drow, width),
        ]

    def spread(rows):
        return lax.all_gather(rows, "dp", axis=0, tiled=True)

    def cut(rows):
        return [rows[k * block_rows : (k + 1) * block_rows] for k in range(tp)]

    def pick_rows(columns):
        dims = (tp, block_rows, images, columns)
        shift, row, image, patch = (lax.broadcasted_iota(jnp.int32, dims, d) for d in range(4))
        target = lax.rem(place + shift, tp)
        found = ((row // share) == image) & ((row % share) + target * share == patch)
        return (found & (row < group_rows)).astype(LOW).reshape(tp * block_rows, images * columns)

    pick = pick_rows(padded)
    pick_plain = pick_rows(patches)
    dims = (rows_t, tp, block_rows)
    row, shift, sent = (lax.broadcasted_iota(jnp.int32, dims, d) for d in range(3))
    frame = row % FRAMES
    merge = ((frame // frames) == lax.rem(place - shift + tp, tp)) & (
        ((row // (FRAMES * share)) * frames + frame % frames) * share + (row // FRAMES) % share
        == sent
    )
    merge = merge.astype(LOW).reshape(rows_t, tp * block_rows)

    time_own = jnp.concatenate(
        [qkv_weight[0].reshape(drow, 3 * part), proj_weight[0].T, shared], axis=1
    )
    space_own = jnp.concatenate([qkv_weight[1].reshape(drow, 3 * part), proj_weight[1].T], axis=1)
    mlp_own = jnp.concatenate([fc1_weight, fc2_weight.T], axis=1)
    sent_x = dot_nn(pick_plain, clips.reshape(slots * tokens, width)).astype(LOW)
    time_back = line_gather(time_own)
    *time_back, sent_x = together(*time_back, sent_x)
    came_x = swap_blocks(cut(sent_x), 1)
    space_own, sent_x = together(space_own, sent_x)
    space_back = line_gather(space_own)
    gathered = line_order(time_back)
    shared_rows = gathered[:, :, 4 * part :].reshape(drow, shared_cols)
    time_all = spread(jnp.concatenate(branch_rows(gathered) + [shared_rows], axis=1))
    mlp_own, came_x = together(mlp_own, came_x)
    mlp_back = line_gather(mlp_own)
    space_all = spread(jnp.concatenate(branch_rows(line_order(space_back)), axis=1))
    qkv_w = (time_all[:, : 3 * width], space_all[:, : 3 * width])
    proj_w = (time_all[:, 3 * width : 4 * width], space_all[:, 3 * width :])
    tfc_w = time_all[:, 4 * width : 5 * width]
    small_all = time_all[:, 5 * width : 5 * width + small_cols].astype(F32).T
    norms = small_all[:6].reshape(3, 2, width)
    out_b = small_all[6:10]
    dp = width // drow
    heads_local = attn_bias.shape[2]
    attn_b = (
        small_all[10:14]
        .reshape(2, 2, dp, tp, heads_local, -1)
        .transpose(0, 1, 3, 4, 2, 5)
        .reshape(2, 2, width)
    )
    hidden_b = (
        small_all[14 : 14 + tp].reshape(tp, dp, tp, srow).transpose(2, 1, 0, 3).reshape(-1)
    )
    bias_rows = [
        jnp.concatenate([attn_b[b, 0], jnp.zeros((width,), F32), attn_b[b, 1]]) for b in (0, 1)
    ]

    def to_patches(rows):
        sent = dot_nn(pick, rows).astype(LOW)
        return dot_nn(merge, swap_blocks(cut(sent), 1))

    def to_frames(rows):
        sent = dot_tn(merge, rows).astype(LOW)
        return dot_tn(pick, swap_blocks(cut(sent), -1))

    def pad_rows(values):
        shaped = values.reshape(images, patches, width)
        return jnp.pad(shaped, ((0, 0), (0, padded - patches), (0, 0))).reshape(rows_f, width)

    def drop_rows(values):
        return values.reshape(images, padded, width)[:, :patches].reshape(slots, tokens, width)

    inputs_low = pad_rows(clips)
    live = jnp.repeat(clip_live.astype(F32), frames * padded)[:, None]

    def qkv_of(normed, b):
        return (dot_nn(normed, qkv_w[b]) + bias_rows[b]).astype(LOW)

    time_blocks = 1
    while rows_t // time_blocks > 128 or rows_t % (8 * time_blocks):
        time_blocks += 1
    time_core = (time_blocks, rows_t // time_blocks, FRAMES, None)
    space_core = (images, padded, None, patches)

    inputs_t = dot_nn(merge, came_x)
    n1 = norm_low(inputs_t, norms[0, 0], norms[0, 1])
    mixed_t = qkv_of(n1, 0)
    heads_t = attend(mixed_t, *time_core)
    *mlp_back, heads_t = together(*mlp_back, heads_t)
    gathered = line_order(mlp_back)
    mlp_all = spread(
        jnp.concatenate(
            [
                gathered[:, :, :hidden_part].transpose(1, 0, 2).reshape(drow, tp * hidden_part),
                gathered[:, :, hidden_part:].transpose(1, 0, 2).reshape(drow, tp * hidden_part),
            ],
            axis=1,
        )
    )
    fc1_w = mlp_all[:, : tp * hidden_part]
    fc2_w = mlp_all[:, tp * hidden_part :]
    summed = (dot_nt(heads_t, proj_w[0]) + out_b[0]).astype(LOW)
    moved = (dot_nn(summed, tfc_w) + out_b[1]).astype(LOW)
    first = inputs_low.astype(F32) + to_frames(moved)
    n2 = norm_low(first, norms[1, 0], norms[1, 1])
    mixed_s = qkv_of(n2, 1)
    heads_s = attend(mixed_s, *space_core)
    second = first + dot_nt(heads_s, proj_w[1]) + out_b[2]
    n3 = norm_low(second, norms[2, 0], norms[2, 1])
    hidden = dot_nn(n3, fc1_w) + hidden_b
    cdf = 0.5 * (1.0 + lax.erf(hidden * (2.0**-0.5)))
    active = (hidden * cdf).astype(LOW)
    slope = (cdf + hidden * jnp.exp(-0.5 * hidden * hidden) * 0.3989422804014327).astype(LOW)
    result = second + dot_nt(active, fc2_w) + out_b[3]
    outputs = drop_rows((result * live).astype(LOW))

    grad_result = pad_rows(cotangent).astype(F32) * live
    grad_low = grad_result.astype(LOW)
    grad_fc2 = dot_tn(grad_low, active).astype(LOW)
    grad_hidden = (dot_nn(grad_low, fc2_w) * slope.astype(F32)).astype(LOW)
    grad_fc1 = dot_tn(n3, grad_hidden).astype(LOW)
    grad_n3 = dot_nt(grad_hidden, fc1_w)
    back, gain_m, shift_m = norm_back(grad_n3, second, norms[2, 0])
    grad_second = grad_result + back

    def branch_back(low, mixed, heads, normed, b, core):
        grad_proj = dot_tn(low, heads).astype(LOW)
        grad_heads = dot_nn(low, proj_w[b]).astype(LOW)
        grad_mixed, sums = attend_back(mixed, grad_heads, *core)
        grad_qkv = dot_tn(normed, grad_mixed).astype(LOW)
        grad_normed = dot_nt(grad_mixed, qkv_w[b])
        return grad_normed, grad_qkv, grad_proj, sums

    def collect(rows):
        return lax.psum_scatter(rows, "dp", scatter_dimension=0, tiled=True)

    def split_cols(rows, pieces):
        return rows.reshape(drow, pieces, tp, -1).transpose(2, 0, 1, 3)

    def branch_blocks(rows):
        return jnp.concatenate(
            [
                split_cols(rows[:, : 3 * width], 3).reshape(tp, drow, 3 * part),
                split_cols(rows[:, 3 * width : 4 * width], 1).reshape(tp, drow, part),
            ],
            axis=2,
        )

    fc2_rows = collect(grad_fc2)
    fc1_rows = collect(grad_fc1)
    low_s = grad_second.astype(LOW)
    grad_n2, qkv_s, proj_s, sums_s = branch_back(low_s, mixed_s, heads_s, n2, 1, space_core)
    space_rows = collect(jnp.concatenate([qkv_s, proj_s], axis=1))
    back, gain_s, shift_s = norm_back(grad_n2, first, norms[1, 0])
    grad_first = grad_second + back
    plain_first = drop_rows(grad_first).reshape(slots * tokens, width)
    low_f = to_patches(grad_first.astype(LOW)).astype(LOW)
    grad_tfc = dot_tn(summed, low_f).astype(LOW)
    low_t = dot_nt(low_f, tfc_w).astype(LOW)
    fc1_rows, fc2_rows, low_t = together(fc1_rows, fc2_rows, low_t)
    fc1_parts = line_scatter(split_cols(fc1_rows, 1).reshape(tp, drow, hidden_part))
    fc2_parts = line_scatter(split_cols(fc2_rows, 1).reshape(tp, drow, hidden_part))
    grad_n1, qkv_t, proj_t, sums_t = branch_back(low_t, mixed_t, heads_t, n1, 0, time_core)
    *fc1_parts, grad_n1 = together(*fc1_parts, grad_n1)
    *fc2_parts, grad_n1 = together(*fc2_parts, grad_n1)
    back, gain_t, shift_t = norm_back(grad_n1, inputs_t, norms[0, 0])
    sent_back = dot_tn(merge, back.astype(LOW)).astype(LOW)
    came_back = swap_blocks(cut(sent_back), -1)

    feature = jnp.stack(
        [
            gain_t,
            shift_t,
            gain_s,
            shift_s,
            gain_m,
            shift_m,
            column_sums(low_t),
            column_sums(low_f),
            column_sums(low_s),
            column_sums(grad_low),
        ]
    )
    attn_sums = jnp.stack(
        [sums_t[:width], sums_t[2 * width :], sums_s[:width], sums_s[2 * width :]]
    )
    attn_sums = (
        attn_sums.reshape(4, tp, heads_local, dp, -1).transpose(0, 3, 1, 2, 4).reshape(4, width)
    )
    hidden_sums = (
        column_sums(grad_hidden).reshape(tp, dp, tp, srow).transpose(2, 1, 0, 3).reshape(tp, width)
    )
    small_grad = jnp.concatenate([feature, attn_sums, hidden_sums]).astype(LOW)
    small_grad = jnp.pad(small_grad, ((0, 256 - small_cols), (0, 0))).T

    time_rows = collect(jnp.concatenate([qkv_t, proj_t, grad_tfc, small_grad], axis=1))
    space_rows, sent_back = together(space_rows, sent_back)
    space_done = line_total(line_scatter(branch_blocks(space_rows)))
    grad_clips = (plain_first + dot_tn(pick_plain, came_back)).reshape(slots, tokens, width)
    shared_back = time_rows[:, 4 * width :].reshape(tp, srow, shared_cols)
    time_done = line_total(
        line_scatter(
            jnp.concatenate(
                [branch_blocks(time_rows), shared_back.reshape(tp, drow, shared_cols // tp)],
                axis=2,
            )
        )
    )
    grad_qkv = jnp.stack([time_done[:, : 3 * part], space_done[:, : 3 * part]]).reshape(
        2, drow, 3, part
    )
    grad_proj = jnp.stack([time_done[:, 3 * part : 4 * part].T, space_done[:, 3 * part :].T])
    shared_done = time_done[:, 4 * part :].reshape(srow, shared_cols)
    smalls = shared_done[:, width : width + small_cols].T
    return (
        outputs,
        grad_clips,
        grad_qkv,
        grad_proj,
        line_total(fc1_parts),
        line_total(fc2_parts).T,
        smalls[10:14].reshape(attn_bias.shape),
        smalls[14 : 14 + tp].reshape(fc1_bias.shape),
        smalls[:6].reshape(3, 2, srow),
        shared_done[:, :width],
        smalls[6:10],
    )


def solution(mesh):
    return jax.shard_map(
        shards,
        mesh=mesh,
        in_specs=(
            P("dp", "tensor", None),
            P("dp"),
            P(None, "dp", None, "tensor"),
            P(None, "tensor", "dp"),
            P("dp", "tensor"),
            P("tensor", "dp"),
            P(None, None, "tensor", "dp"),
            P("tensor", "dp"),
            P(None, None, ("dp", "tensor")),
            P(("dp", "tensor"), None),
            P(None, ("dp", "tensor")),
            P("dp", "tensor", None),
        ),
        out_specs=(
            P("dp", "tensor", None),
            P("dp", "tensor", None),
            P(None, "dp", None, "tensor"),
            P(None, "tensor", "dp"),
            P("dp", "tensor"),
            P("tensor", "dp"),
            P(None, None, "tensor", "dp"),
            P("tensor", "dp"),
            P(None, None, ("dp", "tensor")),
            P(("dp", "tensor"), None),
            P(None, ("dp", "tensor")),
        ),
        check_vma=False,
    )
```

time: 662 us -> 513 us (0.77)
  starting transfers between devices: 176 us -> 56.2 us
  Pallas kernels: 90.9 us -> 38.7 us
  waiting for transfers between devices: 104 us -> 130 us
  other arithmetic: 60.6 us -> 41.4 us
  local copies, waits for them, and re-layouts: 62.7 us -> 80.5 us
    ppermute x50 -> x21, starting transfers between devices: 147 us -> 24.1 us  [line_shift(): lax.ppermute(block, 'tensor', [(i, (i + step) % count) for i in range(cou...]
    pallas_call x2, Pallas kernels: 40 us -> 11.1 us  [attend(): pl.pallas_call(partial(attend_kernel, group, keys, width), grid=(blocks,)...]
    reduce_scatter x4, waiting for transfers between devices: 0.03 us -> 25.7 us  [collect(): return lax.psum_scatter(rows, 'dp', scatter_dimension=0, tiled=True)]
    pallas_call x2, Pallas kernels: 50.9 us -> 27.6 us  [attend_back(): pl.pallas_call(partial(attend_back_kernel, group, keys, width), grid=(blo...]
    ppermute x12, waiting for transfers between devices: 58.1 us -> 38.6 us  [swap_blocks(): moved.append(lax.ppermute(blocks[k], 'tensor', pairs))]
    ppermute x50 -> x21, waiting for transfers between devices: 45.2 us -> 59 us  [line_shift(): lax.ppermute(block, 'tensor', [(i, (i + step) % count) for i in range(cou...]
    unnamed x23 -> x3, other arithmetic: 12.9 us -> 1.32 us
    convert_element_type x20 -> x0, other arithmetic: 8.22 us -> none  [line_scatter(): held = (parts[k].astype(F32) + arrived.astype(F32)).astype(LOW)]
  transfers between devices with their start and end apart: 69 -> 40, of which waited for: 22 -> 15; matrix products, arithmetic and copies ran while one was open for 34% -> 41% of each run, Pallas kernels for 14% -> 8%
where the time goes in v2:
time: 513 us; the launch traced here: 504 us
  matrix products  140 us (27%)
  waiting for transfers between devices  130 us (25%)
  local copies, waits for them, and re-layouts  80.5 us (16%)
  starting transfers between devices  56.2 us (11%)
  other arithmetic  41.4 us (8%)
  Pallas kernels  38.7 us (8%)
  between operations  17.5 us (3%)
    ppermute x21, waiting for transfers between devices, line_shift(): lax.ppermute(block, 'tensor', [(i, (i + step) % count) for i in range(cou...  59 us
    dot_general x11, matrix products, dot_tn(): lax.dot_general(left, right, (((0,), (0,)), ((), ())), preferred_element_...  55.6 us
    dot_general x10, matrix products, dot_nn(): lax.dot_general(left, right, (((1,), (0,)), ((), ())), preferred_element_...  49.1 us
    ppermute x12, waiting for transfers between devices, swap_blocks(): moved.append(lax.ppermute(blocks[k], 'tensor', pairs))  38.6 us
    dot_general x7, matrix products, dot_nt(): lax.dot_general(left, right, (((1,), (1,)), ((), ())), preferred_element_...  35.2 us
    ppermute x12, starting transfers between devices, swap_blocks(): moved.append(lax.ppermute(blocks[k], 'tensor', pairs))  31.8 us
    pallas_call x2, Pallas kernels, attend_back(): pl.pallas_call(partial(attend_back_kernel, group, keys, width), grid=(blo...  27.6 us
    reduce_scatter x4, waiting for transfers between devices, collect(): return lax.psum_scatter(rows, 'dp', scatter_dimension=0, tiled=True)  25.7 us
  transfers between devices with their start and end apart: 40, of which 15 were waited for; matrix products, arithmetic and copies ran while one was open for 41% of the time, Pallas kernels for 8%

profile of v2, /device:TPU:24, one launch (start us, length us, event | category | flops | bytes accessed | tf_op | source)
XLA Modules:
  0.0 504.1 jit_solution(14303848814073442950)
XLA Ops:
  14.5 1.9 collective-permute-start.1
  17.9 4.1 convolution_convert_fusion.8
  22.9 16.4 %collective-permute-done.1 = bf16[96,1024]{0,1:T(8,128)(2,1)S(1)} collective-permute-done((bf16[96,1024]{0,1:T(8,128)(2,1)S(1)}, bf16[96,1024]{0,1:T(8,128)(2,1)S(1)}, u32[]{:S(2)}, u32[]{:S(2)}) %collective-permute-start.1) | collective-permute-done | bytes 196640 | tf_op jit(solution)/shard_map/ppermute | solution.py:31
  46.2 3.7 fusion.119.clone.4
  51.3 3.0 collective-permute-start.14
  56.9 2.8 collective-permute-done.12
  59.6 18.9 %collective-permute-start.5 = (bf16[200,768]{1,0:T(8,128)(2,1)S(1)}, bf16[200,768]{1,0:T(8,128)(2,1)S(1)}, u32[]{:S(2)}, u32[]{:S(2)}) collective-permute-start(bf16[200,768]{1,0:T(8,128)(2,1)S(1)} %get-tuple-element.175), channel_id=1, source_target_pairs={{0,3},{1,0},{2,1},{3,2},{4,7},{5,4},{6,5},{7,6},{8,11},{9,8},{10,9... | collective-permute-start | bytes 921608 | tf_op jit(solution)/shard_map/ppermute | solution.py:68
  83.3 12.5 %collective-permute-done.4 = bf16[200,768]{1,0:T(8,128)(2,1)S(1)} collective-permute-done((bf16[200,768]{1,0:T(8,128)(2,1)}, bf16[200,768]{1,0:T(8,128)(2,1)S(1)}, u32[]{:S(2)}, u32[]{:S(2)}) %collective-permute-start.4) | collective-permute-done | bytes 307232 | tf_op jit(solution)/shard_map/ppermute | solution.py:68
  97.3 2.4 collective-permute-start.8
  99.8 2.7 fusion.127
  112.1 5.7 %add_convert_fusion.1 = bf16[784,2304]{1,0:T(8,128)(2,1)S(1)} fusion(f32[2304]{0:T(1024)S(1)} %get-tuple-element.202, bf16[768,4096]{1,0:T(8,128)(2,1)} %all-gather.4.cloned.1.call-done, f32[784,768]{1,0:T(8,128)S(1)} %get-tuple-element.204, f32[768]{0:T(1024)S(1)} %get-tuple-element.148, f32[768]{0:T(1024)S(1)} %get-tuple-element.149, ...), kind=kOutput, calls=%fused_computation.10 | convolution fusion | flops 2781155328 | bytes 9582656 | tf_op jit(solution)/shard_map/dot_general | solution.py:18
  117.9 4.6 attend.2
  131.7 2.4 add_convert_fusion.5
  135.3 4.4 convolution_convert_fusion.7
  150.3 8.0 %collective-permute-done.10 = bf16[200,768]{1,0:T(8,128)(2,1)} collective-permute-done((bf16[200,768]{1,0:T(8,128)(2,1)}, bf16[200,768]{1,0:T(8,128)(2,1)}, u32[]{:S(2)}, u32[]{:S(2)}) %collective-permute-start.10) | collective-permute-done | bytes 307232 | tf_op jit(solution)/shard_map/ppermute | solution.py:68
  158.2 6.2 %collective-permute-done.11 = bf16[200,768]{1,0:T(8,128)(2,1)} collective-permute-done((bf16[200,768]{1,0:T(8,128)(2,1)}, bf16[200,768]{1,0:T(8,128)(2,1)}, u32[]{:S(2)}, u32[]{:S(2)}) %collective-permute-start.11) | collective-permute-done | bytes 307232 | tf_op jit(solution)/shard_map/ppermute | solution.py:68
  164.4 4.3 fusion.128
  170.6 6.0 %add_convert_fusion = bf16[800,2304]{1,0:T(8,128)(2,1)S(1)} fusion(f32[2304]{0:T(1024)S(1)} %copy-done.76, bf16[768,3072]{1,0:T(8,128)(2,1)} %all-gather.6.cloned.1.call-done, f32[800,768]{1,0:T(8,128)} %copy-done.12, f32[768]{0:T(1024)S(1)} %copy-done.114, f32[768]{0:T(1024)S(1)} %copy-done.68, f32[800]{0:T(1024)S(1)} %add_rsqrt_fusion.1, ...), kind=kOutput, calls=%fused_computation.9 | convolution fusion | flops 2837913600 | bytes 9704704 | tf_op jit(solution)/shard_map/dot_general | solution.py:18
  176.7 6.5 %attend.3 = bf16[4,200,768]{2,1,0:T(8,128)(2,1)S(1)} custom-call(bf16[4,200,2304]{2,1,0:T(8,128)(2,1)S(1)} %bitcast.204), custom_call_target="tpu_custom_call" | custom-call | flops 8000000000 | bytes 4915200 | tf_op jit(solution)/shard_map/attend/pallas_call | solution.py:141
  183.2 2.6 fusion.129
  187.7 6.6 %all-gather.8.cloned.1.call-done = bf16[768,6144]{1,0:T(8,128)(2,1)} async-done(((bf16[96,6144]{1,0:T(8,128)(2,1)}), bf16[768,6144]{1,0:T(8,128)(2,1)}) %all-gather.8.cloned.1.call-update) | async-done | bytes 9437200 | tf_op jit(solution)/shard_map/all_gather | solution.py:264
  194.3 9.0 %multiply_convert_fusion.1 = (bf16[800,3072]{1,0:T(8,128)(2,1)}, f32[800,3072]{1,0:T(8,128)S(1)}) fusion(f32[3072]{0:T(1024)S(1)} %add.370, bf16[768,6144]{1,0:T(8,128)(2,1)} %all-gather.8.cloned.1.call-done, f32[800,768]{1,0:T(8,128)} %copy-done.8, f32[768]{0:T(1024)S(1)} %copy-done.115, f32[768]{0:T(1024)S(1)} %copy-done.69, f32[800]{0:T(1024)S(1)} %add_rsqrt_fusion, ...), kind=kOutput, calls=%fused_computation.7 | convolution fusion | flops 3792691200 | bytes 21946624 | tf_op jit(solution)/shard_map/dot_general | solution.py:18
  203.3 9.3 %fusion.131 = (bf16[3072]{0:T(1024)(128)(2,1)S(1)}, bf16[800,3072]{1,0:T(8,128)(2,1)S(1)}) fusion(f32[800,3072]{1,0:T(8,128)S(1)} %get-tuple-element.210, f32[3072]{0:T(1024)S(1)} %add.370, bf16[800,768]{1,0:T(8,128)(2,1)S(1)} %copy-done.20, bf16[768,6144]{1,0:T(8,128)(2,1)S(1)} %copy-done.134), kind=kOutput, calls=%fused_computation.319 | convolution fusion | flops 3809276928 | bytes 20711424 | tf_op jit(solution)/shard_map/dot_general | solution.py:18
  212.6 2.2 copy-done.136
  214.8 7.7 %convolution_convert_fusion.3 = bf16[768,3072]{1,0:T(8,128)(2,1)} fusion(bf16[800,3072]{1,0:T(8,128)(2,1)S(1)} %get-tuple-element.216, f32[800,768]{1,0:T(8,128)S(1)} %copy-done.9, f32[768]{0:T(1024)S(1)} %copy-done.115, f32[768]{0:T(1024)S(1)} %copy-done.69, f32[800]{0:T(1024)S(1)} %add_rsqrt_fusion, f32[800]{0:T(1024)S(1)} %broadcast_multiply_fusion.4), kind=kOutput, calls=%fused_computation.19 | convolution fusion | flops 3780304896 | bytes 12103936 | tf_op jit(solution)/shard_map/dot_general | solution.py:26
  223.8 10.3 %multiply_reduce_fusion = (bf16[768]{0:T(1024)(128)(2,1)S(1)}, f32[800]{0:T(1024)S(1)}, f32[800]{0:T(1024)S(1)}, bf16[768]{0:T(1024)(128)(2,1)S(1)}, f32[800,768]{1,0:T(8,128)}) fusion(f32[800,768]{1,0:T(8,128)} %copy-done.8, f32[800]{0:T(1024)S(1)} %add_rsqrt_fusion, f32[800]{0:T(1024)S(1)} %broadcast_multiply_fusion.4, f32[768]{0:T(1024)S(1)} %copy-done.69, ...), kind=kOutput, calls=%fused_computation.71 | convolution fusion | flops 3780400128 | bytes 14567936 | tf_op jit(solution)/shard_map/dot_general | solution.py:22
  234.1 9.6 %convolution_convert_fusion.2 = bf16[768,3072]{1,0:T(8,128)(2,1)} fusion(bf16[800,768]{1,0:T(8,128)(2,1)S(1)} %copy-done.21, bf16[800,3072]{1,0:T(8,128)(2,1)} %get-tuple-element.209), kind=kOutput, calls=%fused_computation.18 | convolution fusion | flops 3777232896 | bytes 10862592 | tf_op jit(solution)/shard_map/dot_general | solution.py:26
  243.8 4.2 convert_reduce_fusion
  248.0 3.3 convolution_convert_fusion.6
  251.4 14.3 %attend_back.2 = (bf16[4,200,2304]{2,1,0:T(8,128)(2,1)S(1)}, f32[1,2304]{1,0:T(1,128)S(1)}) custom-call(bf16[4,200,2304]{2,1,0:T(8,128)(2,1)S(1)} %bitcast.205, bf16[4,200,768]{2,1,0:T(8,128)(2,1)S(1)} %bitcast.214), custom_call_target="tpu_custom_call" | custom-call | flops 17999998976 | bytes 8601600 | tf_op jit(solution)/shard_map/attend_back/pallas_call | solution.py:158
  265.7 3.6 multiply_reduce_fusion.1
  270.7 3.0 convolution_convert_fusion.5
  279.8 3.3 convolution_convert_fusion.12
  283.3 4.6 convolution_convert_fusion
  287.9 2.8 pad_maximum_fusion.1
  290.9 12.0 %collective-permute-done.16 = bf16[200,768]{1,0:T(8,128)(2,1)S(1)} collective-permute-done((bf16[200,768]{1,0:T(8,128)(2,1)S(1)}, bf16[200,768]{1,0:T(8,128)(2,1)S(1)}, u32[]{:S(2)}, u32[]{:S(2)}) %collective-permute-start.16) | collective-permute-done | bytes 307232 | tf_op jit(solution)/shard_map/ppermute | solution.py:68
  303.0 3.4 fusion.130
  307.0 2.5 convolution_convert_fusion.10
  309.5 2.5 convolution_convert_fusion.13
  312.0 22.1 %reduce-scatter.7.cloned.1.call-done = bf16[96,3072]{1,0:T(8,128)(2,1)} async-done(((bf16[768,3072]{1,0:T(8,128)(2,1)}), bf16[96,3072]{1,0:T(8,128)(2,1)}) %reduce-scatter.7.cloned.1.call-update) | async-done | bytes 589840 | tf_op jit(solution)/shard_map/reduce_scatter | solution.py:402
  334.1 1.8 reshape.385
  344.2 3.5 collective-permute-start.18
  348.3 2.6 convolution_convert_fusion.9
  350.9 2.5 convolution_convert_fusion.14
  353.5 13.3 %attend_back.3 = (bf16[7,112,2304]{2,1,0:T(8,128)(2,1)S(1)}, f32[1,2304]{1,0:T(1,128)S(1)}) custom-call(bf16[7,112,2304]{2,1,0:T(8,128)(2,1)S(1)} %bitcast.209, bf16[7,112,768]{2,1,0:T(8,128)(2,1)S(1)} %bitcast.217), custom_call_target="tpu_custom_call" | custom-call | flops 17999998976 | bytes 8429568 | tf_op jit(solution)/shard_map/attend_back/pallas_call | solution.py:158
  366.9 5.7 %convolution_convert_fusion.1 = bf16[768,2304]{1,0:T(8,128)(2,1)} fusion(bf16[784,2304]{1,0:T(8,128)(2,1)S(1)} %bitcast.210, f32[784,768]{1,0:T(8,128)S(1)} %copy-done.18, f32[768]{0:T(1024)S(1)} %copy-done.113, f32[768]{0:T(1024)S(1)} %copy-done.67, f32[784]{0:T(1024)S(1)} %copy-done.65, f32[784]{0:T(1024)S(1)} %copy-done.35), kind=kOutput, calls=%fused_computation.17 | convolution fusion | flops 2779312128 | bytes 9572480 | tf_op jit(solution)/shard_map/dot_general | solution.py:26
  372.6 4.4 fusion.15
  379.7 2.1 reduce.1
  385.3 2.7 multiply_reduce_fusion.6
  388.5 6.4 %pad_maximum_fusion = bf16[768,4096]{1,0:T(8,128)(2,1)} fusion(bf16[768,256]{1,0:T(8,128)(2,1)S(1)} %pad_bitcast_fusion, bf16[768,768]{1,0:T(8,128)(2,1)} %convolution_convert_fusion.13, bf16[768,768]{1,0:T(8,128)(2,1)} %convolution_convert_fusion.14, bf16[768,2304]{1,0:T(8,128)(2,1)} %convolution_convert_fusion.1), kind=kLoop, calls=%fused_computation.15 | loop fusion | flops 25165824 | bytes 12582912 | tf_op jit(solution)/shard_map/concatenate | solution.py:463
  395.0 3.0 reshape_reshape.6
  398.0 9.4 %multiply_convert_fusion.3 = bf16[800,768]{1,0:T(8,128)(2,1)} fusion(f32[800,768]{1,0:T(8,128)S(1)} %copy-done.10, bf16[800,3072]{1,0:T(8,128)(2,1)} %get-tuple-element.209, bf16[768,6144]{1,0:T(8,128)(2,1)} %all-gather.8.cloned.1.call-done, f32[800]{0:T(1024)S(1)} %copy-done.37, f32[768]{0:T(1024)S(1)} %copy-done.77), kind=kOutput, calls=%fused_computation.77 | convolution fusion | flops 3777331200 | bytes 13326464 | tf_op jit(solution)/shard_map/dot_general | solution.py:22
  407.4 2.3 reshape.379
  409.8 5.8 %convolution_convert_fusion.4 = bf16[800,768]{1,0:T(8,128)(2,1)S(1)} fusion(f32[784,768]{1,0:T(8,128)} %fusion.15, f32[784,768]{1,0:T(8,128)} %copy-done.17, f32[784]{0:T(1024)S(1)} %broadcast_multiply_fusion.6, f32[784]{0:T(1024)S(1)} %broadcast_multiply_fusion.7, f32[768]{0:T(1024)S(1)} %copy-done.67, f32[784]{0:T(1024)S(1)} %copy-done.65, ...), kind=kOutput, calls=%fused_computation.97 | convolution fusion | flops 993271296 | bytes 6092880 | tf_op jit(solution)/shard_map/dot_general | solution.py:26
  418.5 2.3 collective-permute-start.30
  422.9 2.3 collective-permute-start.24
  425.3 2.0 collective-permute-start.25
  427.3 1.8 add_bitcast_fusion
  429.1 1.8 convert_add_fusion.3
  431.5 21.2 %collective-permute-done.31 = bf16[96,768]{0,1:T(8,128)(2,1)S(1)} collective-permute-done((bf16[96,768]{0,1:T(8,128)(2,1)S(1)}, bf16[96,768]{0,1:T(8,128)(2,1)S(1)}, u32[]{:S(2)}, u32[]{:S(2)}) %collective-permute-start.31) | collective-permute-done | bytes 147488 | tf_op jit(solution)/shard_map/ppermute | solution.py:31
  453.6 3.6 reduce-scatter.9.cloned.1.call-done
  463.3 1.7 copy.238
  469.1 5.2 %convolution_add_fusion = f32[784,768]{1,0:T(8,128)} fusion(f32[784,768]{1,0:T(8,128)S(1)} %copy-done.19, bf16[200,768]{1,0:T(8,128)(2,1)} %collective-permute-done.26, bf16[200,768]{1,0:T(8,128)(2,1)} %collective-permute-done.25, bf16[200,768]{1,0:T(8,128)(2,1)} %collective-permute-done.24, bf16[200,768]{1,0:T(8,128)(2,1)S(1)} %copy-done.29, ...), kind=kOutput, calls=%fused_computation.102 | convolution fusion | flops 976422912 | bytes 6074368 | tf_op jit(solution)/shard_map/dot_general | solution.py:26
  474.8 16.4 %collective-permute-done.28 = bf16[96,1024]{0,1:T(8,128)(2,1)S(1)} collective-permute-done((bf16[96,1024]{0,1:T(8,128)(2,1)S(1)}, bf16[96,1024]{0,1:T(8,128)(2,1)S(1)}, u32[]{:S(2)}, u32[]{:S(2)}) %collective-permute-start.28) | collective-permute-done | bytes 196640 | tf_op jit(solution)/shard_map/ppermute | solution.py:31
  (586 shorter events, 107.6 us)
Async XLA Ops:
  7.2 96.7 %all-gather.4.cloned.1.call-start = ((), (), s32[]{:S(2)}) async-start(), calls=%async_computation.4 | async-start | bytes 7077888 | tf_op jit(solution)/shard_map/all_gather | solution.py:264
  14.4 8.5 %collective-permute-start = (bf16[96,1024]{0,1:T(8,128)(2,1)S(1)}, bf16[96,1024]{0,1:T(8,128)(2,1)S(1)}, u32[]{:S(2)}, u32[]{:S(2)}) collective-permute-start(bf16[96,1024]{0,1:T(8,128)(2,1)S(1)} %pad_maximum_fusion.9), channel_id=1, source_target_pairs={{0,1},{1,2},{2,3},{3,0},{4,5},{5,6},{6,7},{7,4},{8,9},{9,10},{10,1... | collective-permute-start | bytes 589832 | tf_op jit(solution)/shard_map/ppermute | solution.py:31
  14.5 24.8 %collective-permute-start.1 = (bf16[96,1024]{0,1:T(8,128)(2,1)S(1)}, bf16[96,1024]{0,1:T(8,128)(2,1)S(1)}, u32[]{:S(2)}, u32[]{:S(2)}) collective-permute-start(bf16[96,1024]{0,1:T(8,128)(2,1)S(1)} %pad_maximum_fusion.9), channel_id=1, source_target_pairs={{0,2},{1,3},{2,0},{3,1},{4,6},{5,7},{6,4},{7,5},{8,10},{9,11},{10,... | collective-permute-start | bytes 589832 | tf_op jit(solution)/shard_map/ppermute | solution.py:31
  16.4 22.9 %collective-permute-start.2 = (bf16[96,1024]{0,1:T(8,128)(2,1)S(1)}, bf16[96,1024]{0,1:T(8,128)(2,1)S(1)}, u32[]{:S(2)}, u32[]{:S(2)}) collective-permute-start(bf16[96,1024]{0,1:T(8,128)(2,1)S(1)} %pad_maximum_fusion.9), channel_id=1, source_target_pairs={{0,3},{1,0},{2,1},{3,2},{4,7},{5,4},{6,5},{7,6},{8,11},{9,8},{10,9... | collective-permute-start | bytes 589832 | tf_op jit(solution)/shard_map/ppermute | solution.py:31
  45.5 125.1 %all-gather.6.cloned.1.call-start = ((), (), s32[]{:S(2)}) async-start(), calls=%async_computation.5 | async-start | bytes 5308416 | tf_op jit(solution)/shard_map/all_gather | solution.py:264
  45.7 88.4 %copy-start.32 = (s32[800]{0:T(1024)}, s32[800]{0:T(1024)S(1)}, u32[]{:S(2)}) copy-start(s32[800]{0:T(1024)S(1)} %add.336) | copy-start | bytes 9604
  49.9 9.7 %collective-permute-start.12 = (bf16[96,768]{0,1:T(8,128)(2,1)S(1)}, bf16[96,768]{0,1:T(8,128)(2,1)S(1)}, u32[]{:S(2)}, u32[]{:S(2)}) collective-permute-start(bf16[96,768]{0,1:T(8,128)(2,1)S(1)} %pad_maximum_fusion.10), channel_id=1, source_target_pairs={{0,3},{1,0},{2,1},{3,2},{4,7},{5,4},{6,5},{7,6},{8,11},{9,8},{10,9... | collective-permute-start | bytes 442376 | tf_op jit(solution)/shard_map/ppermute | solution.py:31
  49.9 28.7 %collective-permute-start.13 = (bf16[96,768]{0,1:T(8,128)(2,1)S(1)}, bf16[96,768]{0,1:T(8,128)(2,1)S(1)}, u32[]{:S(2)}, u32[]{:S(2)}) collective-permute-start(bf16[96,768]{0,1:T(8,128)(2,1)S(1)} %pad_maximum_fusion.10), channel_id=1, source_target_pairs={{0,2},{1,3},{2,0},{3,1},{4,6},{5,7},{6,4},{7,5},{8,10},{9,11},{10,... | collective-permute-start | bytes 442376 | tf_op jit(solution)/shard_map/ppermute | solution.py:31
  51.3 27.3 %collective-permute-start.14 = (bf16[96,768]{0,1:T(8,128)(2,1)S(1)}, bf16[96,768]{0,1:T(8,128)(2,1)S(1)}, u32[]{:S(2)}, u32[]{:S(2)}) collective-permute-start(bf16[96,768]{0,1:T(8,128)(2,1)S(1)} %pad_maximum_fusion.10), channel_id=1, source_target_pairs={{0,1},{1,2},{2,3},{3,0},{4,5},{5,6},{6,7},{7,4},{8,9},{9,10},{10,1... | collective-permute-start | bytes 442376 | tf_op jit(solution)/shard_map/ppermute | solution.py:31
  55.3 28.1 %collective-permute-start.3 = (bf16[200,768]{1,0:T(8,128)(2,1)}, bf16[200,768]{1,0:T(8,128)(2,1)S(1)}, u32[]{:S(2)}, u32[]{:S(2)}) collective-permute-start(bf16[200,768]{1,0:T(8,128)(2,1)} %get-tuple-element.177), channel_id=1, source_target_pairs={{0,1},{1,2},{2,3},{3,0},{4,5},{5,6},{6,7},{7,4},{8,9},{9,10},{10,1... | collective-permute-start | bytes 921608 | tf_op jit(solution)/shard_map/ppermute | solution.py:68
  55.4 40.4 %collective-permute-start.4 = (bf16[200,768]{1,0:T(8,128)(2,1)}, bf16[200,768]{1,0:T(8,128)(2,1)S(1)}, u32[]{:S(2)}, u32[]{:S(2)}) collective-permute-start(bf16[200,768]{1,0:T(8,128)(2,1)} %get-tuple-element.176), channel_id=1, source_target_pairs={{0,2},{1,3},{2,0},{3,1},{4,6},{5,7},{6,4},{7,5},{8,10},{9,11},{10,... | collective-permute-start | bytes 921608 | tf_op jit(solution)/shard_map/ppermute | solution.py:68
  59.6 36.1 %collective-permute-start.5 = (bf16[200,768]{1,0:T(8,128)(2,1)S(1)}, bf16[200,768]{1,0:T(8,128)(2,1)S(1)}, u32[]{:S(2)}, u32[]{:S(2)}) collective-permute-start(bf16[200,768]{1,0:T(8,128)(2,1)S(1)} %get-tuple-element.175), channel_id=1, source_target_pairs={{0,3},{1,0},{2,1},{3,2},{4,7},{5,4},{6,5},{7,6},{8,11},{9,8},{10,9... | collective-permute-start | bytes 921608 | tf_op jit(solution)/shard_map/ppermute | solution.py:68
  83.2 111.1 %all-gather.8.cloned.1.call-start = ((), (), s32[]{:S(2)}) async-start(), calls=%async_computation.6 | async-start | bytes 10616832 | tf_op jit(solution)/shard_map/all_gather | solution.py:264
  95.9 26.6 %collective-permute-start.6 = (bf16[96,1536]{1,0:T(8,128)(2,1)S(1)}, bf16[96,1536]{1,0:T(8,128)(2,1)}, u32[]{:S(2)}, u32[]{:S(2)}) collective-permute-start(bf16[96,1536]{1,0:T(8,128)(2,1)S(1)} %pad_maximum_fusion.8), channel_id=1, source_target_pairs={{0,1},{1,2},{2,3},{3,0},{4,5},{5,6},{6,7},{7,4},{8,9},{9,10},{10,1... | collective-permute-start | bytes 884744 | tf_op jit(solution)/shard_map/ppermute | solution.py:31
  95.9 26.7 %collective-permute-start.7 = (bf16[96,1536]{1,0:T(8,128)(2,1)S(1)}, bf16[96,1536]{1,0:T(8,128)(2,1)}, u32[]{:S(2)}, u32[]{:S(2)}) collective-permute-start(bf16[96,1536]{1,0:T(8,128)(2,1)S(1)} %pad_maximum_fusion.8), channel_id=1, source_target_pairs={{0,2},{1,3},{2,0},{3,1},{4,6},{5,7},{6,4},{7,5},{8,10},{9,11},{10,... | collective-permute-start | bytes 884744 | tf_op jit(solution)/shard_map/ppermute | solution.py:31
  97.3 25.3 %collective-permute-start.8 = (bf16[96,1536]{1,0:T(8,128)(2,1)S(1)}, bf16[96,1536]{1,0:T(8,128)(2,1)}, u32[]{:S(2)}, u32[]{:S(2)}) collective-permute-start(bf16[96,1536]{1,0:T(8,128)(2,1)S(1)} %pad_maximum_fusion.8), channel_id=1, source_target_pairs={{0,3},{1,0},{2,1},{3,2},{4,7},{5,4},{6,5},{7,6},{8,11},{9,8},{10,9... | collective-permute-start | bytes 884744 | tf_op jit(solution)/shard_map/ppermute | solution.py:31
  130.3 181.7 %reduce-scatter.5.cloned.1.call-start = ((), (), s32[]{:S(2)}) async-start(), calls=%async_computation.7 | async-start | bytes 5308416 | tf_op jit(solution)/shard_map/reduce_scatter | solution.py:402
  140.6 17.6 %collective-permute-start.10 = (bf16[200,768]{1,0:T(8,128)(2,1)}, bf16[200,768]{1,0:T(8,128)(2,1)}, u32[]{:S(2)}, u32[]{:S(2)}) collective-permute-start(bf16[200,768]{1,0:T(8,128)(2,1)} %get-tuple-element.172), channel_id=1, source_target_pairs={{0,2},{1,3},{2,0},{3,1},{4,6},{5,7},{6,4},{7,5},{8,10},{9,11},{10,... | collective-permute-start | bytes 921608 | tf_op jit(solution)/shard_map/ppermute | solution.py:68
  142.2 22.2 %collective-permute-start.11 = (bf16[200,768]{1,0:T(8,128)(2,1)}, bf16[200,768]{1,0:T(8,128)(2,1)}, u32[]{:S(2)}, u32[]{:S(2)}) collective-permute-start(bf16[200,768]{1,0:T(8,128)(2,1)} %get-tuple-element.171), channel_id=1, source_target_pairs={{0,1},{1,2},{2,3},{3,0},{4,5},{5,6},{6,7},{7,4},{8,9},{9,10},{10,1... | collective-permute-start | bytes 921608 | tf_op jit(solution)/shard_map/ppermute | solution.py:68
  143.1 21.3 %collective-permute-start.9 = (bf16[200,768]{1,0:T(8,128)(2,1)S(1)}, bf16[200,768]{1,0:T(8,128)(2,1)}, u32[]{:S(2)}, u32[]{:S(2)}) collective-permute-start(bf16[200,768]{1,0:T(8,128)(2,1)S(1)} %get-tuple-element.173), channel_id=1, source_target_pairs={{0,3},{1,0},{2,1},{3,2},{4,7},{5,4},{6,5},{7,6},{8,11},{9,8},{10,9... | collective-permute-start | bytes 921608 | tf_op jit(solution)/shard_map/ppermute | solution.py:68
  146.0 97.8 %copy-start.36 = (f32[800]{0:T(1024)}, f32[800]{0:T(1024)S(1)}, u32[]{:S(2)}) copy-start(f32[800]{0:T(1024)S(1)} %mul.263) | copy-start | bytes 9604
  147.4 17.0 %copy-start.39 = (s32[800]{0:T(1024)S(1)}, s32[800]{0:T(1024)}, u32[]{:S(2)}) copy-start(s32[800]{0:T(1024)} %copy-done.38) | copy-start | bytes 9604
  147.4 17.0 %copy-start.92 = (s32[800]{0:T(1024)S(1)}, s32[800]{0:T(1024)}, u32[]{:S(2)}) copy-start(s32[800]{0:T(1024)} %copy-done.91) | copy-start | bytes 9604
  148.6 15.9 %copy-start.22 = (bf16[4,200,768]{2,1,0:T(8,128)(2,1)S(1)}, bf16[4,200,768]{2,1,0:T(8,128)(2,1)}, u32[]{:S(2)}) copy-start(bf16[4,200,768]{2,1,0:T(8,128)(2,1)} %pad.15) | copy-start | bytes 3686404
  222.5 111.6 %reduce-scatter.7.cloned.1.call-start = ((), (), s32[]{:S(2)}) async-start(), calls=%async_computation.8 | async-start | bytes 5308416 | tf_op jit(solution)/shard_map/reduce_scatter | solution.py:402
  243.8 171.9 %reduce-scatter.11.cloned.1.call-start = ((), (), s32[]{:S(2)}) async-start(), calls=%async_computation.10 | async-start | bytes 5308416 | tf_op jit(solution)/shard_map/reduce_scatter | solution.py:402
  248.0 21.4 %copy-start.16 = (f32[800,768]{1,0:T(8,128)}, f32[800,768]{1,0:T(8,128)S(1)}, u32[]{:S(2)}) copy-start(f32[800,768]{1,0:T(8,128)S(1)} %get-tuple-element.159) | copy-start | bytes 7372804
  248.0 17.7 %slice-start.4 = ((s8[4718592]{0:T(1024)(128)(4,1)}), s8[4194304]{0:T(1024)(128)(4,1)S(1)}, s32[]{:S(2)}) async-start(s8[4718592]{0:T(1024)(128)(4,1)} %bitcast.255), calls=%async_computation.15 | async-start | bytes 8388608
  251.4 14.3 %copy-start.14 = (f32[800,768]{1,0:T(8,128)S(1)}, f32[800,768]{1,0:T(8,128)}, u32[]{:S(2)}) copy-start(f32[800,768]{1,0:T(8,128)} %copy-done.12) | copy-start | bytes 7372804
  251.4 14.3 %slice-start.5 = ((s8[4718592]{0:T(1024)(128)(4,1)}), s8[524288]{0:T(1024)(128)(4,1)S(1)}, s32[]{:S(2)}) async-start(s8[4718592]{0:T(1024)(128)(4,1)} %bitcast.255), calls=%async_computation.16 | async-start | bytes 1048576
  273.7 17.2 %collective-permute-start.15 = (bf16[200,768]{1,0:T(8,128)(2,1)S(1)}, bf16[200,768]{1,0:T(8,128)(2,1)S(1)}, u32[]{:S(2)}, u32[]{:S(2)}) collective-permute-start(bf16[200,768]{1,0:T(8,128)(2,1)S(1)} %get-tuple-element.169), channel_id=1, source_target_pairs={{0,1},{1,2},{2,3},{3,0},{4,5},{5,6},{6,7},{7,4},{8,9},{9,10},{10,1... | collective-permute-start | bytes 921608 | tf_op jit(solution)/shard_map/ppermute | solution.py:68
  274.4 28.5 %collective-permute-start.16 = (bf16[200,768]{1,0:T(8,128)(2,1)S(1)}, bf16[200,768]{1,0:T(8,128)(2,1)S(1)}, u32[]{:S(2)}, u32[]{:S(2)}) collective-permute-start(bf16[200,768]{1,0:T(8,128)(2,1)S(1)} %get-tuple-element.168), channel_id=1, source_target_pairs={{0,2},{1,3},{2,0},{3,1},{4,6},{5,7},{6,4},{7,5},{8,10},{9,11},{10,... | collective-permute-start | bytes 921608 | tf_op jit(solution)/shard_map/ppermute | solution.py:68
  275.8 27.2 %collective-permute-start.17 = (bf16[200,768]{1,0:T(8,128)(2,1)S(1)}, bf16[200,768]{1,0:T(8,128)(2,1)}, u32[]{:S(2)}, u32[]{:S(2)}) collective-permute-start(bf16[200,768]{1,0:T(8,128)(2,1)S(1)} %get-tuple-element.167), channel_id=1, source_target_pairs={{0,3},{1,0},{2,1},{3,2},{4,7},{5,4},{6,5},{7,6},{8,11},{9,8},{10,9... | collective-permute-start | bytes 921608 | tf_op jit(solution)/shard_map/ppermute | solution.py:68
  290.8 12.2 %copy-start.61 = (s32[784]{0:T(1024)S(1)}, s32[784]{0:T(1024)}, u32[]{:S(2)}) copy-start(s32[784]{0:T(1024)} %copy-done.59) | copy-start | bytes 9412
  290.8 12.2 %copy-start.64 = (s32[784]{0:T(1024)S(1)}, s32[784]{0:T(1024)}, u32[]{:S(2)}) copy-start(s32[784]{0:T(1024)} %copy-done.62) | copy-start | bytes 9412
  290.8 12.2 %copy-start.81 = (pred[800]{0:T(1024)(128)(4,1)S(1)}, pred[800]{0:T(1024)(128)(4,1)}, u32[]{:S(2)}) copy-start(pred[800]{0:T(1024)(128)(4,1)} %copy-done.79) | copy-start | bytes 2404
  290.8 12.2 %copy-start.85 = (pred[784]{0:T(1024)(128)(4,1)S(1)}, pred[784]{0:T(1024)(128)(4,1)}, u32[]{:S(2)}) copy-start(pred[784]{0:T(1024)(128)(4,1)} %copy-done.83) | copy-start | bytes 2356
  290.8 12.2 %copy-start.89 = (pred[784]{0:T(1024)(128)(4,1)S(1)}, pred[784]{0:T(1024)(128)(4,1)}, u32[]{:S(2)}) copy-start(pred[784]{0:T(1024)(128)(4,1)} %copy-done.87) | copy-start | bytes 2356
  290.8 12.2 %copy-start.118 = (pred[784]{0:T(1024)(128)(4,1)S(1)}, pred[784]{0:T(1024)(128)(4,1)}, u32[]{:S(2)}) copy-start(pred[784]{0:T(1024)(128)(4,1)} %copy-done.116) | copy-start | bytes 2356
  290.9 166.3 %reduce-scatter.9.cloned.1.call-start = ((), (), s32[]{:S(2)}) async-start(), calls=%async_computation.9 | async-start | bytes 7077888 | tf_op jit(solution)/shard_map/reduce_scatter | solution.py:402
  309.5 41.4 %copy-start.24 = (bf16[784,768]{1,0:T(8,128)(2,1)}, bf16[784,768]{1,0:T(8,128)(2,1)S(1)}, u32[]{:S(2)}) copy-start(bf16[784,768]{1,0:T(8,128)(2,1)S(1)} %convolution_convert_fusion.10) | copy-start | bytes 3612676
  337.9 39.8 %collective-permute-start.21 = (bf16[96,768]{1,0:T(8,128)(2,1)}, bf16[96,768]{1,0:T(8,128)(2,1)S(1)}, u32[]{:S(2)}, u32[]{:S(2)}) collective-permute-start(bf16[96,768]{1,0:T(8,128)(2,1)} %bitcast.194), channel_id=1, source_target_pairs={{0,1},{1,2},{2,3},{3,0},{4,5},{5,6},{6,7},{7,4},{8,9},{9,10},{10,1... | collective-permute-start | bytes 442376 | tf_op jit(solution)/shard_map/ppermute | solution.py:31
  339.1 45.4 %collective-permute-start.22 = (bf16[96,768]{1,0:T(8,128)(2,1)}, bf16[96,768]{1,0:T(8,128)(2,1)}, u32[]{:S(2)}, u32[]{:S(2)}) collective-permute-start(bf16[96,768]{1,0:T(8,128)(2,1)} %bitcast.193), channel_id=1, source_target_pairs={{0,2},{1,3},{2,0},{3,1},{4,6},{5,7},{6,4},{7,5},{8,10},{9,11},{10,... | collective-permute-start | bytes 442376 | tf_op jit(solution)/shard_map/ppermute | solution.py:31
  341.2 43.3 %collective-permute-start.23 = (bf16[96,768]{1,0:T(8,128)(2,1)}, bf16[96,768]{1,0:T(8,128)(2,1)}, u32[]{:S(2)}, u32[]{:S(2)}) collective-permute-start(bf16[96,768]{1,0:T(8,128)(2,1)} %bitcast.192), channel_id=1, source_target_pairs={{0,3},{1,0},{2,1},{3,2},{4,7},{5,4},{6,5},{7,6},{8,11},{9,8},{10,9... | collective-permute-start | bytes 442376 | tf_op jit(solution)/shard_map/ppermute | solution.py:31
  344.2 40.4 %collective-permute-start.18 = (bf16[96,768]{1,0:T(8,128)(2,1)}, bf16[96,768]{1,0:T(8,128)(2,1)S(1)}, u32[]{:S(2)}, u32[]{:S(2)}) collective-permute-start(bf16[96,768]{1,0:T(8,128)(2,1)} %bitcast.198), channel_id=1, source_target_pairs={{0,1},{1,2},{2,3},{3,0},{4,5},{5,6},{6,7},{7,4},{8,9},{9,10},{10,1... | collective-permute-start | bytes 442376 | tf_op jit(solution)/shard_map/ppermute | solution.py:31
  348.3 36.2 %collective-permute-start.19 = (bf16[96,768]{1,0:T(8,128)(2,1)}, bf16[96,768]{1,0:T(8,128)(2,1)}, u32[]{:S(2)}, u32[]{:S(2)}) collective-permute-start(bf16[96,768]{1,0:T(8,128)(2,1)} %bitcast.197), channel_id=1, source_target_pairs={{0,2},{1,3},{2,0},{3,1},{4,6},{5,7},{6,4},{7,5},{8,10},{9,11},{10,... | collective-permute-start | bytes 442376 | tf_op jit(solution)/shard_map/ppermute | solution.py:31
  350.9 21.7 %slice-start.2 = ((s8[6291456]{0:T(1024)(128)(4,1)}), s8[4194304]{0:T(1024)(128)(4,1)S(1)}, s32[]{:S(2)}) async-start(s8[6291456]{0:T(1024)(128)(4,1)} %bitcast.250), calls=%async_computation.13 | async-start | bytes 8388608
  353.4 13.4 %copy-start.18 = (f32[784,768]{1,0:T(8,128)S(1)}, f32[784,768]{1,0:T(8,128)}, u32[]{:S(2)}) copy-start(f32[784,768]{1,0:T(8,128)} %copy-done.17) | copy-start | bytes 7225348
  353.4 13.4 %copy-start.35 = (f32[784]{0:T(1024)S(1)}, f32[784]{0:T(1024)}, u32[]{:S(2)}) copy-start(f32[784]{0:T(1024)} %copy-done.34) | copy-start | bytes 9412
  353.4 13.4 %copy-start.65 = (f32[784]{0:T(1024)S(1)}, f32[784]{0:T(1024)}, u32[]{:S(2)}) copy-start(f32[784]{0:T(1024)} %add_rsqrt_fusion.2) | copy-start | bytes 9412
  353.4 13.4 %copy-start.67 = (f32[768]{0:T(1024)S(1)}, f32[768]{0:T(1024)}, u32[]{:S(2)}) copy-start(f32[768]{0:T(1024)} %copy-done.66) | copy-start | bytes 9220
  353.5 13.4 %copy-start.113 = (f32[768]{0:T(1024)S(1)}, f32[768]{0:T(1024)}, u32[]{:S(2)}) copy-start(f32[768]{0:T(1024)} %copy-done.112) | copy-start | bytes 9220
  353.5 19.1 %slice-start.3 = ((s8[6291456]{0:T(1024)(128)(4,1)}), s8[2097152]{0:T(1024)(128)(4,1)S(1)}, s32[]{:S(2)}) async-start(s8[6291456]{0:T(1024)(128)(4,1)} %bitcast.250), calls=%async_computation.14 | async-start | bytes 4194304
  377.7 7.6 %collective-permute-start.20 = (bf16[96,768]{1,0:T(8,128)(2,1)}, bf16[96,768]{1,0:T(8,128)(2,1)}, u32[]{:S(2)}, u32[]{:S(2)}) collective-permute-start(bf16[96,768]{1,0:T(8,128)(2,1)} %bitcast.196), channel_id=1, source_target_pairs={{0,3},{1,0},{2,1},{3,2},{4,7},{5,4},{6,5},{7,6},{8,11},{9,8},{10,9... | collective-permute-start | bytes 442376 | tf_op jit(solution)/shard_map/ppermute | solution.py:31
  418.5 12.4 %collective-permute-start.30 = (bf16[96,768]{0,1:T(8,128)(2,1)S(1)}, bf16[96,768]{0,1:T(8,128)(2,1)S(1)}, u32[]{:S(2)}, u32[]{:S(2)}) collective-permute-start(bf16[96,768]{0,1:T(8,128)(2,1)S(1)} %get-tuple-element.181), channel_id=1, source_target_pairs={{0,1},{1,2},{2,3},{3,0},{4,5},{5,6},{6,7},{7,4},{8,9},{9,10},{10,1... | collective-permute-start | bytes 442376 | tf_op jit(solution)/shard_map/ppermute | solution.py:31
  420.8 31.9 %collective-permute-start.31 = (bf16[96,768]{0,1:T(8,128)(2,1)S(1)}, bf16[96,768]{0,1:T(8,128)(2,1)S(1)}, u32[]{:S(2)}, u32[]{:S(2)}) collective-permute-start(bf16[96,768]{0,1:T(8,128)(2,1)S(1)} %get-tuple-element.182), channel_id=1, source_target_pairs={{0,2},{1,3},{2,0},{3,1},{4,6},{5,7},{6,4},{7,5},{8,10},{9,11},{10,... | collective-permute-start | bytes 442376 | tf_op jit(solution)/shard_map/ppermute | solution.py:31
  421.9 30.8 %collective-permute-start.32 = (bf16[96,768]{0,1:T(8,128)(2,1)S(1)}, bf16[96,768]{0,1:T(8,128)(2,1)S(1)}, u32[]{:S(2)}, u32[]{:S(2)}) collective-permute-start(bf16[96,768]{0,1:T(8,128)(2,1)S(1)} %get-tuple-element.183), channel_id=1, source_target_pairs={{0,3},{1,0},{2,1},{3,2},{4,7},{5,4},{6,5},{7,6},{8,11},{9,8},{10,9... | collective-permute-start | bytes 442376 | tf_op jit(solution)/shard_map/ppermute | solution.py:31
  422.9 45.5 %collective-permute-start.24 = (bf16[200,768]{1,0:T(8,128)(2,1)}, bf16[200,768]{1,0:T(8,128)(2,1)}, u32[]{:S(2)}, u32[]{:S(2)}) collective-permute-start(bf16[200,768]{1,0:T(8,128)(2,1)} %get-tuple-element.165), channel_id=1, source_target_pairs={{0,3},{1,0},{2,1},{3,2},{4,7},{5,4},{6,5},{7,6},{8,11},{9,8},{10,9... | collective-permute-start | bytes 921608 | tf_op jit(solution)/shard_map/ppermute | solution.py:68
  425.3 43.7 %collective-permute-start.25 = (bf16[200,768]{1,0:T(8,128)(2,1)}, bf16[200,768]{1,0:T(8,128)(2,1)}, u32[]{:S(2)}, u32[]{:S(2)}) collective-permute-start(bf16[200,768]{1,0:T(8,128)(2,1)} %get-tuple-element.164), channel_id=1, source_target_pairs={{0,2},{1,3},{2,0},{3,1},{4,6},{5,7},{6,4},{7,5},{8,10},{9,11},{10,... | collective-permute-start | bytes 921608 | tf_op jit(solution)/shard_map/ppermute | solution.py:68
  430.9 38.1 %collective-permute-start.26 = (bf16[200,768]{1,0:T(8,128)(2,1)}, bf16[200,768]{1,0:T(8,128)(2,1)}, u32[]{:S(2)}, u32[]{:S(2)}) collective-permute-start(bf16[200,768]{1,0:T(8,128)(2,1)} %get-tuple-element.163), channel_id=1, source_target_pairs={{0,1},{1,2},{2,3},{3,0},{4,5},{5,6},{6,7},{7,4},{8,9},{9,10},{10,1... | collective-permute-start | bytes 921608 | tf_op jit(solution)/shard_map/ppermute | solution.py:68
  466.3 8.5 %collective-permute-start.27 = (bf16[96,1024]{0,1:T(8,128)(2,1)S(1)}, bf16[96,1024]{0,1:T(8,128)(2,1)S(1)}, u32[]{:S(2)}, u32[]{:S(2)}) collective-permute-start(bf16[96,1024]{0,1:T(8,128)(2,1)S(1)} %get-tuple-element.178), channel_id=1, source_target_pairs={{0,1},{1,2},{2,3},{3,0},{4,5},{5,6},{6,7},{7,4},{8,9},{9,10},{10,1... | collective-permute-start | bytes 589832 | tf_op jit(solution)/shard_map/ppermute | solution.py:31
  466.9 24.4 %collective-permute-start.28 = (bf16[96,1024]{0,1:T(8,128)(2,1)S(1)}, bf16[96,1024]{0,1:T(8,128)(2,1)S(1)}, u32[]{:S(2)}, u32[]{:S(2)}) collective-permute-start(bf16[96,1024]{0,1:T(8,128)(2,1)S(1)} %get-tuple-element.180), channel_id=1, source_target_pairs={{0,2},{1,3},{2,0},{3,1},{4,6},{5,7},{6,4},{7,5},{8,10},{9,11},{10,... | collective-permute-start | bytes 589832 | tf_op jit(solution)/shard_map/ppermute | solution.py:31
  468.4 22.9 %collective-permute-start.29 = (bf16[96,1024]{0,1:T(8,128)(2,1)S(1)}, bf16[96,1024]{0,1:T(8,128)(2,1)S(1)}, u32[]{:S(2)}, u32[]{:S(2)}) collective-permute-start(bf16[96,1024]{0,1:T(8,128)(2,1)S(1)} %get-tuple-element.179), channel_id=1, source_target_pairs={{0,3},{1,0},{2,1},{3,2},{4,7},{5,4},{6,5},{7,6},{8,11},{9,8},{10,9... | collective-permute-start | bytes 589832 | tf_op jit(solution)/shard_map/ppermute | solution.py:31
  474.3 21.0 %copy-start.28 = (f32[1,192,96]{2,1,0:T(8,128)S(1)}, f32[1,192,96]{2,1,0:T(8,128)}, u32[]{:S(2)}) copy-start(f32[1,192,96]{2,1,0:T(8,128)} %slice_bitcast_fusion) | copy-start | bytes 221188
  (121 other events, 590.6 us)
Sparse Core Ops, SparseCore 0:
  45.6 46.4 all-gather.3
  94.6 38.9 all-gather.5
  135.5 58.8 all-gather.7
  222.6 53.8 reduce-scatter.4
  280.2 53.8 reduce-scatter.6
  337.4 53.9 reduce-scatter.10
  395.2 61.9 reduce-scatter.8

commit v3 on v2

--- a/solution.py
+++ b/solution.py
@@ -37,8 +37,10 @@
 
 def line_order(back):
     count = lax.axis_size("tensor")
-    ring = jnp.stack([back[(-j) % count] for j in range(count)] * 2)
-    return lax.dynamic_slice_in_dim(ring, count - lax.axis_index("tensor"), count, axis=0)
+    place = lax.axis_index("tensor")
+    return [
+        lax.select_n(lax.rem(place - j + count, count), *back) for j in range(count)
+    ]
 
 
 def line_scatter(blocks):
@@ -67,6 +69,64 @@
         pairs = [(i, (i + sign * k) % count) for i in range(count)]
         moved.append(lax.ppermute(blocks[k], "tensor", pairs))
     return jnp.concatenate(moved, axis=0)
+
+
+def flip(block, mask):
+    count = lax.axis_size("dp")
+    return lax.ppermute(block, "dp", [(i, i ^ mask) for i in range(count)])
+
+
+def is_square():
+    return lax.axis_size("dp") == 8
+
+
+def place_kernel(me_ref, *refs):
+    pieces, out_ref = refs[:-1], refs[-1]
+    for mask, piece in enumerate(pieces):
+        out_ref[me_ref[0] ^ mask] = piece[...]
+
+
+def place_pieces(pieces):
+    shape = (len(pieces),) + pieces[0].shape
+    whole = pl.BlockSpec(memory_space=pltpu.VMEM)
+    out = pl.pallas_call(
+        place_kernel,
+        in_specs=[pl.BlockSpec(memory_space=pltpu.SMEM)] + [whole] * len(pieces),
+        out_specs=whole,
+        out_shape=jax.ShapeDtypeStruct(shape, pieces[0].dtype),
+        compiler_params=pltpu.CompilerParams(vmem_limit_bytes=24 << 20),
+        cost_estimate=pl.CostEstimate(
+            flops=0, bytes_accessed=32 * pieces[0].size, transcendentals=0
+        ),
+        name="place_pieces",
+    )(lax.axis_index("dp").astype(jnp.int32).reshape(1), *pieces)
+    return out.reshape(-1, shape[2])
+
+
+def chip_scatter(arrays):
+    if not is_square():
+        joined = jnp.concatenate(arrays, axis=1)
+        return lax.psum_scatter(joined, "dp", scatter_dimension=0, tiled=True)
+    me = lax.axis_index("dp")
+    core, chip = me & 1, me >> 1
+    height = arrays[0].shape[0] // 8
+
+    def half(which):
+        parts = [
+            lax.dynamic_index_in_dim(
+                item.reshape(4, 2, height, -1), which, axis=1, keepdims=False
+            )
+            for item in arrays
+        ]
+        return jnp.concatenate(parts, axis=2)
+
+    arrived = flip(half(1 - core), 1)
+    kept = (half(core).astype(F32) + arrived.astype(F32)).astype(LOW)
+    total = lax.dynamic_index_in_dim(kept, chip, axis=0, keepdims=False).astype(F32)
+    for mask in (1, 2, 3):
+        away = lax.dynamic_index_in_dim(kept, chip ^ mask, axis=0, keepdims=False)
+        total = total + flip(away, 2 * mask).astype(F32)
+    return total.astype(LOW)
 
 
 def pair_sides(values, first):
@@ -237,28 +297,38 @@
     block_rows = -(-group_rows // 8) * 8
     rows_t = slots * share * FRAMES
 
+    dp = width // drow
+    heads_local = attn_bias.shape[2]
     small = jnp.concatenate(
+        [norm_params.reshape(6, srow).T, out_bias.T, attn_bias.reshape(4, srow).T], axis=1
+    )
+    shared_cols = width + 256
+    shared = jnp.concatenate(
         [
-            norm_params.reshape(6, srow).T,
-            out_bias.T,
-            attn_bias.reshape(4, srow).T,
-            fc1_bias.reshape(tp, srow).T,
+            tfc_weight,
+            jnp.pad(small, ((0, 0), (0, 128 - small.shape[1]))),
+            jnp.pad(fc1_bias, ((0, srow - 1), (0, 128 - drow))),
         ],
         axis=1,
-    )
-    small_cols = small.shape[1]
-    shared_cols = width + 256
-    shared = jnp.concatenate(
-        [tfc_weight, jnp.pad(small, ((0, 0), (0, 256 - small_cols)))], axis=1
     ).reshape(drow, shared_cols // tp)
 
-    def branch_rows(both):
-        qkv = both[:, :, : 3 * part].reshape(tp, drow, 3, part)
-        proj = both[:, :, 3 * part : 4 * part]
-        return [
-            qkv.transpose(1, 2, 0, 3).reshape(drow, 3 * width),
-            proj.transpose(1, 0, 2).reshape(drow, width),
+    def branch_rows(pieces):
+        parts = [
+            piece[:, k * part : (k + 1) * part] for k in range(4) for piece in line_order(pieces)
         ]
+        return jnp.concatenate(parts, axis=1)
+
+    dims = (dp, tp, heads_local, srow // heads_local, width)
+    at_dp, at_place, at_head, at_lane = (
+        lax.broadcasted_iota(jnp.int32, dims, d) for d in range(4)
+    )
+    column = lax.broadcasted_iota(jnp.int32, dims, 4)
+    lanes = srow // heads_local
+    head_order = ((at_place * heads_local + at_head) * dp + at_dp) * lanes + at_lane == column
+    row = lax.broadcasted_iota(jnp.int32, (width, width), 0)
+    column = lax.broadcasted_iota(jnp.int32, (width, width), 1)
+    orders = jnp.concatenate([row == column, head_order.reshape(width, width)], axis=1)
+    orders = orders.astype(LOW)
 
     def spread(rows):
         return lax.all_gather(rows, "dp", axis=0, tiled=True)
@@ -288,36 +358,32 @@
         [qkv_weight[0].reshape(drow, 3 * part), proj_weight[0].T, shared], axis=1
     )
     space_own = jnp.concatenate([qkv_weight[1].reshape(drow, 3 * part), proj_weight[1].T], axis=1)
-    mlp_own = jnp.concatenate([fc1_weight, fc2_weight.T], axis=1)
+    fc2_own = fc2_weight.T
     sent_x = dot_nn(pick_plain, clips.reshape(slots * tokens, width)).astype(LOW)
     time_back = line_gather(time_own)
-    *time_back, sent_x = together(*time_back, sent_x)
-    came_x = swap_blocks(cut(sent_x), 1)
-    space_own, sent_x = together(space_own, sent_x)
+    *time_back, held_x = together(*time_back, sent_x)
+    came_x = swap_blocks(cut(held_x)[:1] + cut(sent_x)[1:], 1)
+    space_own, held_x = together(space_own, sent_x)
     space_back = line_gather(space_own)
-    gathered = line_order(time_back)
-    shared_rows = gathered[:, :, 4 * part :].reshape(drow, shared_cols)
-    time_all = spread(jnp.concatenate(branch_rows(gathered) + [shared_rows], axis=1))
-    mlp_own, came_x = together(mlp_own, came_x)
-    mlp_back = line_gather(mlp_own)
-    space_all = spread(jnp.concatenate(branch_rows(line_order(space_back)), axis=1))
+    shared_rows = jnp.concatenate(
+        [piece[:, 4 * part :].reshape(srow, shared_cols) for piece in line_order(time_back)]
+    )
+    time_all = spread(jnp.concatenate([branch_rows(time_back), shared_rows], axis=1))
+    fc1_own, came_x = together(fc1_weight, came_x)
+    fc1_back = line_gather(fc1_own)
+    fc2_own, time_all = together(fc2_own, time_all)
+    fc2_back = line_gather(fc2_own)
+    space_all = spread(branch_rows(space_back))
+    fc1_w = spread(jnp.concatenate(line_order(fc1_back), axis=1))
     qkv_w = (time_all[:, : 3 * width], space_all[:, : 3 * width])
     proj_w = (time_all[:, 3 * width : 4 * width], space_all[:, 3 * width :])
     tfc_w = time_all[:, 4 * width : 5 * width]
-    small_all = time_all[:, 5 * width : 5 * width + small_cols].astype(F32).T
-    norms = small_all[:6].reshape(3, 2, width)
-    out_b = small_all[6:10]
-    dp = width // drow
-    heads_local = attn_bias.shape[2]
-    attn_b = (
-        small_all[10:14]
-        .reshape(2, 2, dp, tp, heads_local, -1)
-        .transpose(0, 1, 3, 4, 2, 5)
-        .reshape(2, 2, width)
-    )
-    hidden_b = (
-        small_all[14 : 14 + tp].reshape(tp, dp, tp, srow).transpose(2, 1, 0, 3).reshape(-1)
-    )
+    small_all = dot_tn(time_all[:, 5 * width : 5 * width + 16], orders)
+    norms = small_all[:6, :width].reshape(3, 2, width)
+    out_b = small_all[6:10, :width]
+    attn_b = small_all[10:14, width:].reshape(2, 2, width)
+    hidden_b = time_all[:, 5 * width + 128 : 5 * width + 128 + drow].reshape(dp, tp, srow, drow)
+    hidden_b = hidden_b[:, :, 0].transpose(1, 0, 2).reshape(-1).astype(F32)
     bias_rows = [
         jnp.concatenate([attn_b[b, 0], jnp.zeros((width,), F32), attn_b[b, 1]]) for b in (0, 1)
     ]
@@ -325,10 +391,6 @@
     def to_patches(rows):
         sent = dot_nn(pick, rows).astype(LOW)
         return dot_nn(merge, swap_blocks(cut(sent), 1))
-
-    def to_frames(rows):
-        sent = dot_tn(merge, rows).astype(LOW)
-        return dot_tn(pick, swap_blocks(cut(sent), -1))
 
     def pad_rows(values):
         shaped = values.reshape(images, patches, width)
@@ -353,24 +415,17 @@
     n1 = norm_low(inputs_t, norms[0, 0], norms[0, 1])
     mixed_t = qkv_of(n1, 0)
     heads_t = attend(mixed_t, *time_core)
-    *mlp_back, heads_t = together(*mlp_back, heads_t)
-    gathered = line_order(mlp_back)
-    mlp_all = spread(
-        jnp.concatenate(
-            [
-                gathered[:, :, :hidden_part].transpose(1, 0, 2).reshape(drow, tp * hidden_part),
-                gathered[:, :, hidden_part:].transpose(1, 0, 2).reshape(drow, tp * hidden_part),
-            ],
-            axis=1,
-        )
-    )
-    fc1_w = mlp_all[:, : tp * hidden_part]
-    fc2_w = mlp_all[:, tp * hidden_part :]
+    *fc2_back, heads_t = together(*fc2_back, heads_t)
     summed = (dot_nt(heads_t, proj_w[0]) + out_b[0]).astype(LOW)
     moved = (dot_nn(summed, tfc_w) + out_b[1]).astype(LOW)
-    first = inputs_low.astype(F32) + to_frames(moved)
+    came_f = swap_blocks(cut(dot_tn(merge, moved).astype(LOW)), -1)
+    first = inputs_low.astype(F32) + dot_tn(pick, came_f)
     n2 = norm_low(first, norms[1, 0], norms[1, 1])
     mixed_s = qkv_of(n2, 1)
+    *fc2_back, mixed_s = together(*fc2_back, mixed_s)
+    fc2_rows = jnp.concatenate(line_order(fc2_back), axis=1)
+    if is_square():
+        fc2_chips = [fc2_rows] + [flip(fc2_rows, mask) for mask in (2, 4, 6)]
     heads_s = attend(mixed_s, *space_core)
     second = first + dot_nt(heads_s, proj_w[1]) + out_b[2]
     n3 = norm_low(second, norms[2, 0], norms[2, 1])
@@ -378,25 +433,32 @@
     cdf = 0.5 * (1.0 + lax.erf(hidden * (2.0**-0.5)))
     active = (hidden * cdf).astype(LOW)
     slope = (cdf + hidden * jnp.exp(-0.5 * hidden * hidden) * 0.3989422804014327).astype(LOW)
-    result = second + dot_nt(active, fc2_w) + out_b[3]
-    outputs = drop_rows((result * live).astype(LOW))
+    if is_square():
+        *fc2_chips, active = together(*fc2_chips, active)
+        fc2_pairs = [flip(piece, 1) for piece in fc2_chips]
+        fc2_w = place_pieces([piece for pair in zip(fc2_chips, fc2_pairs) for piece in pair])
+    else:
+        fc2_w = spread(fc2_rows)
 
     grad_result = pad_rows(cotangent).astype(F32) * live
     grad_low = grad_result.astype(LOW)
     grad_fc2 = dot_tn(grad_low, active).astype(LOW)
+    grad_fc2, grad_low = together(grad_fc2, grad_low)
     grad_hidden = (dot_nn(grad_low, fc2_w) * slope.astype(F32)).astype(LOW)
     grad_fc1 = dot_tn(n3, grad_hidden).astype(LOW)
+    grad_fc1, grad_hidden = together(grad_fc1, grad_hidden)
     grad_n3 = dot_nt(grad_hidden, fc1_w)
     back, gain_m, shift_m = norm_back(grad_n3, second, norms[2, 0])
     grad_second = grad_result + back
 
-    def branch_back(low, mixed, heads, normed, b, core):
-        grad_proj = dot_tn(low, heads).astype(LOW)
+    def branch_back(low, mixed, normed, b, core, held):
         grad_heads = dot_nn(low, proj_w[b]).astype(LOW)
         grad_mixed, sums = attend_back(mixed, grad_heads, *core)
+        held, grad_mixed = together(held, grad_mixed)
+        parts = line_scatter(blocks_of(held, 1))
         grad_qkv = dot_tn(normed, grad_mixed).astype(LOW)
         grad_normed = dot_nt(grad_mixed, qkv_w[b])
-        return grad_normed, grad_qkv, grad_proj, sums
+        return grad_normed, grad_qkv, sums, parts
 
     def collect(rows):
         return lax.psum_scatter(rows, "dp", scatter_dimension=0, tiled=True)
@@ -404,32 +466,28 @@
     def split_cols(rows, pieces):
         return rows.reshape(drow, pieces, tp, -1).transpose(2, 0, 1, 3)
 
-    def branch_blocks(rows):
-        return jnp.concatenate(
-            [
-                split_cols(rows[:, : 3 * width], 3).reshape(tp, drow, 3 * part),
-                split_cols(rows[:, 3 * width : 4 * width], 1).reshape(tp, drow, part),
-            ],
-            axis=2,
-        )
+    def blocks_of(rows, pieces):
+        return split_cols(rows, pieces).reshape(tp, drow, rows.shape[1] // tp)
 
     fc2_rows = collect(grad_fc2)
     fc1_rows = collect(grad_fc1)
     low_s = grad_second.astype(LOW)
-    grad_n2, qkv_s, proj_s, sums_s = branch_back(low_s, mixed_s, heads_s, n2, 1, space_core)
-    space_rows = collect(jnp.concatenate([qkv_s, proj_s], axis=1))
+    proj_s = dot_tn(low_s, heads_s).astype(LOW)
+    grad_n2, qkv_s, sums_s, fc2_parts = branch_back(low_s, mixed_s, n2, 1, space_core, fc2_rows)
     back, gain_s, shift_s = norm_back(grad_n2, first, norms[1, 0])
     grad_first = grad_second + back
     plain_first = drop_rows(grad_first).reshape(slots * tokens, width)
     low_f = to_patches(grad_first.astype(LOW)).astype(LOW)
     grad_tfc = dot_tn(summed, low_f).astype(LOW)
     low_t = dot_nt(low_f, tfc_w).astype(LOW)
-    fc1_rows, fc2_rows, low_t = together(fc1_rows, fc2_rows, low_t)
-    fc1_parts = line_scatter(split_cols(fc1_rows, 1).reshape(tp, drow, hidden_part))
-    fc2_parts = line_scatter(split_cols(fc2_rows, 1).reshape(tp, drow, hidden_part))
-    grad_n1, qkv_t, proj_t, sums_t = branch_back(low_t, mixed_t, heads_t, n1, 0, time_core)
-    *fc1_parts, grad_n1 = together(*fc1_parts, grad_n1)
-    *fc2_parts, grad_n1 = together(*fc2_parts, grad_n1)
+    proj_t = dot_tn(low_t, heads_t).astype(LOW)
+    middle_rows = jnp.concatenate([qkv_s, proj_s, proj_t, grad_tfc], axis=1)
+    middle_rows, low_t = together(middle_rows, low_t)
+    middle_rows = collect(middle_rows)
+    grad_n1, qkv_t, sums_t, fc1_parts = branch_back(low_t, mixed_t, n1, 0, time_core, fc1_rows)
+    active, grad_n1 = together(active, grad_n1)
+    result = second + dot_nt(active, fc2_w) + out_b[3]
+    outputs = drop_rows((result * live).astype(LOW))
     back, gain_t, shift_t = norm_back(grad_n1, inputs_t, norms[0, 0])
     sent_back = dot_tn(merge, back.astype(LOW)).astype(LOW)
     came_back = swap_blocks(cut(sent_back), -1)
@@ -451,34 +509,42 @@
     attn_sums = jnp.stack(
         [sums_t[:width], sums_t[2 * width :], sums_s[:width], sums_s[2 * width :]]
     )
-    attn_sums = (
-        attn_sums.reshape(4, tp, heads_local, dp, -1).transpose(0, 3, 1, 2, 4).reshape(4, width)
-    )
-    hidden_sums = (
-        column_sums(grad_hidden).reshape(tp, dp, tp, srow).transpose(2, 1, 0, 3).reshape(tp, width)
-    )
-    small_grad = jnp.concatenate([feature, attn_sums, hidden_sums]).astype(LOW)
-    small_grad = jnp.pad(small_grad, ((0, 256 - small_cols), (0, 0))).T
-
-    time_rows = collect(jnp.concatenate([qkv_t, proj_t, grad_tfc, small_grad], axis=1))
-    space_rows, sent_back = together(space_rows, sent_back)
-    space_done = line_total(line_scatter(branch_blocks(space_rows)))
+    rows = jnp.concatenate(
+        [
+            jnp.pad(feature, ((0, 0), (0, width))),
+            jnp.pad(attn_sums, ((0, 128 - 14), (width, 0))),
+        ]
+    ).astype(LOW)
+    hidden_sums = column_sums(grad_hidden).reshape(tp, dp, 1, drow).transpose(1, 0, 2, 3)
+    hidden_sums = jnp.pad(hidden_sums, ((0, 0), (0, 0), (0, srow - 1), (0, 128 - drow)))
+    last_rows = chip_scatter(
+        [qkv_t, dot_nt(orders, rows).astype(LOW), hidden_sums.reshape(width, 128).astype(LOW)]
+    )
+    last_rows, came_back = together(last_rows, came_back)
+    middle = jnp.concatenate(
+        [
+            blocks_of(middle_rows[:, : 3 * width], 3),
+            blocks_of(middle_rows[:, 3 * width : 4 * width], 1),
+            blocks_of(middle_rows[:, 4 * width : 5 * width], 1),
+            middle_rows[:, 5 * width :].reshape(tp, drow, part),
+        ],
+        axis=2,
+    )
+    middle = line_total(line_scatter(middle))
+    last = jnp.concatenate(
+        [
+            blocks_of(last_rows[:, : 3 * width], 3),
+            last_rows[:, 3 * width :].reshape(tp, drow, 256 // tp),
+        ],
+        axis=2,
+    )
+    last = line_total(line_scatter(last))
     grad_clips = (plain_first + dot_tn(pick_plain, came_back)).reshape(slots, tokens, width)
-    shared_back = time_rows[:, 4 * width :].reshape(tp, srow, shared_cols)
-    time_done = line_total(
-        line_scatter(
-            jnp.concatenate(
-                [branch_blocks(time_rows), shared_back.reshape(tp, drow, shared_cols // tp)],
-                axis=2,
-            )
-        )
-    )
-    grad_qkv = jnp.stack([time_done[:, : 3 * part], space_done[:, : 3 * part]]).reshape(
-        2, drow, 3, part
-    )
-    grad_proj = jnp.stack([time_done[:, 3 * part : 4 * part].T, space_done[:, 3 * part :].T])
-    shared_done = time_done[:, 4 * part :].reshape(srow, shared_cols)
-    smalls = shared_done[:, width : width + small_cols].T
+    grad_qkv = jnp.stack([last[:, : 3 * part], middle[:, : 3 * part]]).reshape(2, drow, 3, part)
+    grad_proj = jnp.stack([middle[:, 4 * part : 5 * part].T, middle[:, 3 * part : 4 * part].T])
+    grad_tfc = middle[:, 5 * part :].reshape(srow, width)
+    smalls = last[:, 3 * part :].reshape(srow, 256)
+    features = smalls[:, :14].T
     return (
         outputs,
         grad_clips,
@@ -486,11 +552,11 @@
         grad_proj,
         line_total(fc1_parts),
         line_total(fc2_parts).T,
-        smalls[10:14].reshape(attn_bias.shape),
-        smalls[14 : 14 + tp].reshape(fc1_bias.shape),
-        smalls[:6].reshape(3, 2, srow),
-        shared_done[:, :width],
-        smalls[6:10],
+        features[10:14].reshape(attn_bias.shape),
+        smalls[:1, 128 : 128 + drow],
+        features[:6].reshape(3, 2, srow),
+        grad_tfc,
+        features[6:10],
     )
 
 

time: 513 us -> 493 us (0.961)
  local copies, waits for them, and re-layouts: 80.5 us -> 63.2 us
  waiting for transfers between devices: 130 us -> 139 us
  other arithmetic: 41.4 us -> 33.7 us
    reduce_scatter x4 -> x3, waiting for transfers between devices: 25.7 us -> 0.01 us  [collect(): return lax.psum_scatter(rows, 'dp', scatter_dimension=0, tiled=True)]
    ppermute x12, waiting for transfers between devices: 38.6 us -> 57.2 us  [swap_blocks(): moved.append(lax.ppermute(blocks[k], 'tensor', pairs))]
    ppermute x12, starting transfers between devices: 31.8 us -> 14.6 us  [swap_blocks(): moved.append(lax.ppermute(blocks[k], 'tensor', pairs))]
    ppermute x0 -> x11, waiting for transfers between devices: none -> 15.4 us  [flip(): return lax.ppermute(block, 'dp', [(i, i ^ mask) for i in range(count)])]
    concatenate x8 -> x7, other arithmetic: 14.2 us -> 5.52 us  [the longest x1 3.37 us: shards(): middle_rows = jnp.concatenate([qkv_s, proj_s, proj_t, grad_tfc], axis=1)]
    ppermute x0 -> x11, starting transfers between devices: none -> 7.64 us  [flip(): return lax.ppermute(block, 'dp', [(i, i ^ mask) for i in range(count)])]
    ppermute x21 -> x24, waiting for transfers between devices: 59 us -> 66.4 us  [line_shift(): lax.ppermute(block, 'tensor', [(i, (i + step) % count) for i in range(cou...]
    ppermute x21 -> x24, starting transfers between devices: 24.1 us -> 31.4 us  [line_shift(): lax.ppermute(block, 'tensor', [(i, (i + step) % count) for i in range(cou...]
  transfers between devices with their start and end apart: 40 -> 53, of which waited for: 15 -> 17; matrix products, arithmetic and copies ran while one was open for 41% -> 42% of each run, Pallas kernels for 8% -> 8%
where the time goes in v3:
time: 493 us; the launch traced here: 484 us
  waiting for transfers between devices  139 us (28%)
  matrix products  135 us (27%)
  local copies, waits for them, and re-layouts  63.2 us (13%)
  starting transfers between devices  53.9 us (11%)
  Pallas kernels  40.7 us (8%)
  other arithmetic  33.7 us (7%)
  between operations  17.9 us (4%)
    ppermute x24, waiting for transfers between devices, line_shift(): lax.ppermute(block, 'tensor', [(i, (i + step) % count) for i in range(cou...  66.4 us
    ppermute x12, waiting for transfers between devices, swap_blocks(): moved.append(lax.ppermute(blocks[k], 'tensor', pairs))  57.2 us
    dot_general x12, matrix products, dot_tn(): lax.dot_general(left, right, (((0,), (0,)), ((), ())), preferred_element_...  51.8 us
    dot_general x10, matrix products, dot_nn(): lax.dot_general(left, right, (((1,), (0,)), ((), ())), preferred_element_...  50.4 us
    dot_general x8, matrix products, dot_nt(): lax.dot_general(left, right, (((1,), (1,)), ((), ())), preferred_element_...  33.2 us
    ppermute x24, starting transfers between devices, line_shift(): lax.ppermute(block, 'tensor', [(i, (i + step) % count) for i in range(cou...  31.4 us
    pallas_call x2, Pallas kernels, attend_back(): pl.pallas_call(partial(attend_back_kernel, group, keys, width), grid=(blo...  28 us
    unnamed x337, local copies, waits for them, and re-layouts  21.6 us
  transfers between devices with their start and end apart: 53, of which 17 were waited for; matrix products, arithmetic and copies ran while one was open for 42% of the time, Pallas kernels for 8%

profile of v3, /device:TPU:24, one launch (start us, length us, event | category | flops | bytes accessed | tf_op | source)
XLA Modules:
  0.0 483.8 jit_solution(11349656638391573621)
XLA Ops:
  16.0 4.1 convolution_convert_fusion.8
  21.0 16.4 %collective-permute-done.1 = bf16[96,1024]{0,1:T(8,128)(2,1)S(1)} collective-permute-done((bf16[96,1024]{0,1:T(8,128)(2,1)S(1)}, bf16[96,1024]{0,1:T(8,128)(2,1)S(1)}, u32[]{:S(2)}, u32[]{:S(2)}) %collective-permute-start.1) | collective-permute-done | bytes 196640 | tf_op jit(solution)/shard_map/ppermute | solution.py:31
  45.1 2.2 collective-permute-done.12
  47.3 9.3 %collective-permute-done.13 = bf16[96,768]{1,0:T(8,128)(2,1)S(1)} collective-permute-done((bf16[96,768]{1,0:T(8,128)(2,1)S(1)}, bf16[96,768]{1,0:T(8,128)(2,1)S(1)}, u32[]{:S(2)}, u32[]{:S(2)}) %collective-permute-start.13) | collective-permute-done | bytes 147488 | tf_op jit(solution)/shard_map/ppermute | solution.py:31
  63.5 2.0 fusion.142.clone.4
  68.0 18.5 %collective-permute-done.7 = bf16[200,768]{1,0:T(8,128)(2,1)} collective-permute-done((bf16[200,768]{1,0:T(8,128)(2,1)S(1)}, bf16[200,768]{1,0:T(8,128)(2,1)}, u32[]{:S(2)}, u32[]{:S(2)}) %collective-permute-start.7) | collective-permute-done | bytes 307232 | tf_op jit(solution)/shard_map/ppermute | solution.py:70
  95.2 8.0 %collective-permute-done.19 = bf16[96,768]{1,0:T(8,128)(2,1)S(1)} collective-permute-done((bf16[96,768]{1,0:T(8,128)(2,1)S(1)}, bf16[96,768]{1,0:T(8,128)(2,1)S(1)}, u32[]{:S(2)}, u32[]{:S(2)}) %collective-permute-start.19) | collective-permute-done | bytes 147488 | tf_op jit(solution)/shard_map/ppermute | solution.py:31
  107.0 2.1 collective-permute-start.5
  110.4 5.9 %add_convert_fusion.1 = bf16[784,2304]{1,0:T(8,128)(2,1)S(1)} fusion(f32[2304]{0:T(1024)S(1)} %get-tuple-element.261, bf16[768,4096]{1,0:T(8,128)(2,1)} %all-gather.4.cloned.1.call-done, f32[784,768]{1,0:T(8,128)} %copy-done.25, f32[768]{0:T(1024)S(1)} %get-tuple-element.150, f32[768]{0:T(1024)S(1)} %get-tuple-element.151, f32[784]{0:T(1024)S(1)} %add_rsqrt_fusion.2, ...), kind=kOutput, calls=%fused_computation.10 | convolution fusion | flops 2781155328 | bytes 9581696 | tf_op jit(solution)/shard_map/dot_general | solution.py:18
  116.4 4.6 attend.2
  121.8 2.2 add_convert_fusion.6
  124.1 4.7 convolution_convert_fusion.7
  129.7 2.8 collective-permute-start.10
  132.6 2.2 collective-permute-start.9
  139.1 13.9 %collective-permute-done.10 = bf16[200,768]{1,0:T(8,128)(2,1)} collective-permute-done((bf16[200,768]{1,0:T(8,128)(2,1)}, bf16[200,768]{1,0:T(8,128)(2,1)}, u32[]{:S(2)}, u32[]{:S(2)}) %collective-permute-start.10) | collective-permute-done | bytes 307232 | tf_op jit(solution)/shard_map/ppermute | solution.py:70
  153.0 4.9 %fusion.164 = (f32[800]{0:T(1024)S(1)}, f32[800,768]{1,0:T(8,128)S(1)}) fusion(bf16[200,768]{1,0:T(8,128)(2,1)} %collective-permute-done.11, bf16[200,768]{1,0:T(8,128)(2,1)} %collective-permute-done.10, bf16[200,768]{1,0:T(8,128)(2,1)} %collective-permute-done.9, bf16[200,768]{1,0:T(8,128)(2,1)S(1)} %get-tuple-element.171, s32[800]{0:T(1024)S(1)} %copy-done.62, ...), kind=kOutput, calls=%fused_computation.349 | convolution fusion | flops 997477632 | bytes 4947200 | tf_op jit(solution)/shard_map/dot_general | solution.py:26
  158.7 5.8 %add_convert_fusion = bf16[800,2304]{1,0:T(8,128)(2,1)S(1)} fusion(f32[2304]{0:T(1024)S(1)} %copy-done.97, bf16[768,3072]{1,0:T(8,128)(2,1)} %all-gather.6.cloned.1.call-done, f32[800,768]{1,0:T(8,128)S(1)} %get-tuple-element.265, f32[768]{0:T(1024)S(1)} %copy-done.135, f32[768]{0:T(1024)S(1)} %copy-done.90, f32[800]{0:T(1024)S(1)} %add_rsqrt_fusion.1, ...), kind=kOutput, calls=%fused_computation.9 | convolution fusion | flops 2837913600 | bytes 9704704 | tf_op jit(solution)/shard_map/dot_general | solution.py:18
  168.3 6.5 %attend.3 = bf16[4,200,768]{2,1,0:T(8,128)(2,1)S(1)} custom-call(bf16[4,200,2304]{2,1,0:T(8,128)(2,1)S(1)} %bitcast.176), custom_call_target="tpu_custom_call" | custom-call | flops 8000000000 | bytes 4915200 | tf_op jit(solution)/shard_map/attend/pallas_call | solution.py:201
  174.8 3.0 fusion.165
  179.8 10.4 %multiply_convert_fusion.1 = (bf16[800,3072]{1,0:T(8,128)(2,1)S(1)}, f32[800,3072]{1,0:T(8,128)}) fusion(f32[3072]{0:T(1024)S(1)} %copy-done.94, bf16[768,3072]{1,0:T(8,128)(2,1)} %all-gather.8.cloned.1.call-done, f32[800,768]{1,0:T(8,128)} %copy-done.16, f32[768]{0:T(1024)S(1)} %copy-done.137, f32[768]{0:T(1024)S(1)} %copy-done.92, ...), kind=kOutput, calls=%fused_computation.7 | convolution fusion | flops 3792691200 | bytes 21946624 | tf_op jit(solution)/shard_map/dot_general | solution.py:18
  190.2 4.3 collective-permute-done.17.refs_6_
  195.5 7.0 %convolution_convert_fusion.3 = bf16[768,3072]{1,0:T(8,128)(2,1)} fusion(bf16[800,768]{1,0:T(8,128)(2,1)S(1)} %copy-done.28, bf16[800,3072]{1,0:T(8,128)(2,1)S(1)} %get-tuple-element.88), kind=kOutput, calls=%fused_computation.19 | convolution fusion | flops 3777232896 | bytes 10862592 | tf_op jit(solution)/shard_map/dot_general | solution.py:26
  202.7 2.1 reduce.3
  207.8 10.4 %multiply_convert_fusion = bf16[800,3072]{1,0:T(8,128)(2,1)S(1)} fusion(bf16[800,768]{1,0:T(8,128)(2,1)S(1)} %copy-done.29, bf16[768,3072]{1,0:T(8,128)(2,1)S(1)} %bitcast.172, f32[800,3072]{1,0:T(8,128)} %get-tuple-element.269, f32[3072]{0:T(1024)S(1)} %copy-done.95), kind=kOutput, calls=%fused_computation.6 | convolution fusion | flops 3806822400 | bytes 20705280 | tf_op jit(solution)/shard_map/dot_general | solution.py:18
  218.2 2.2 copy-done.27
  220.5 7.6 %convolution_convert_fusion.2 = bf16[768,3072]{1,0:T(8,128)(2,1)} fusion(bf16[800,3072]{1,0:T(8,128)(2,1)S(1)} %multiply_convert_fusion, f32[800,768]{1,0:T(8,128)S(1)} %copy-done.17, f32[768]{0:T(1024)S(1)} %copy-done.138, f32[768]{0:T(1024)S(1)} %copy-done.93, f32[800]{0:T(1024)S(1)} %copy-done.87, f32[800]{0:T(1024)S(1)} %broadcast_multiply_fusion.4), kind=kOutput, calls=%fused_computation.18 | convolution fusion | flops 3780304896 | bytes 12103936 | tf_op jit(solution)/shard_map/dot_general | solution.py:26
  228.1 3.9 reduce.4
  232.0 8.4 %multiply_reduce_fusion = (bf16[768]{0:T(1024)(128)(2,1)S(1)}, f32[800]{0:T(1024)S(1)}, f32[800]{0:T(1024)S(1)}, bf16[768]{0:T(1024)(128)(2,1)S(1)}, f32[800,768]{1,0:T(8,128)S(1)}) fusion(f32[800,768]{1,0:T(8,128)S(1)} %copy-done.17, f32[800]{0:T(1024)S(1)} %copy-done.87, f32[800]{0:T(1024)S(1)} %broadcast_multiply_fusion.4, f32[768]{0:T(1024)S(1)} %copy-done.93, ...), kind=kOutput, calls=%fused_computation.66 | convolution fusion | flops 3780400128 | bytes 14567936 | tf_op jit(solution)/shard_map/dot_general | solution.py:22
  241.7 3.4 convolution_convert_fusion.6
  245.0 14.7 %attend_back.2 = (bf16[4,200,2304]{2,1,0:T(8,128)(2,1)S(1)}, f32[1,2304]{1,0:T(1,128)S(1)}) custom-call(bf16[4,200,2304]{2,1,0:T(8,128)(2,1)S(1)} %bitcast.177, bf16[4,200,768]{2,1,0:T(8,128)(2,1)S(1)} %bitcast.186), custom_call_target="tpu_custom_call" | custom-call | flops 17999998976 | bytes 8601600 | tf_op jit(solution)/shard_map/attend_back/pallas_call | solution.py:218
  261.8 4.2 convolution_convert_fusion.14
  270.7 5.7 %collective-permute-start.45 = (bf16[96,768]{1,0:T(8,128)(2,1)S(1)}, bf16[96,768]{1,0:T(8,128)(2,1)}, u32[]{:S(2)}, u32[]{:S(2)}) collective-permute-start(bf16[96,768]{1,0:T(8,128)(2,1)S(1)} %bitcast.214), channel_id=1, source_target_pairs={{0,2},{1,3},{2,0},{3,1},{4,6},{5,7},{6,4},{7,5},{8,10},{9,11},{10,... | collective-permute-start | bytes 442376 | tf_op jit(solution)/shard_map/ppermute | solution.py:31
  278.8 6.0 %multiply_reduce_fusion.1 = (bf16[768]{0:T(1024)(128)(2,1)S(1)}, f32[800]{0:T(1024)S(1)}, f32[800]{0:T(1024)S(1)}, bf16[768]{0:T(1024)(128)(2,1)S(1)}, f32[800,768]{1,0:T(8,128)S(1)}) fusion(f32[800,768]{1,0:T(8,128)S(1)} %copy-done.21, f32[800]{0:T(1024)S(1)} %copy-done.85, f32[800]{0:T(1024)S(1)} %broadcast_multiply_fusion.5, f32[768]{0:T(1024)S(1)} %copy-done.91, ...), kind=kOutput, calls=%fused_computation.67 | convolution fusion | flops 2836681728 | bytes 12159488 | tf_op jit(solution)/shard_map/dot_general | solution.py:22
  286.2 3.0 convolution_convert_fusion.5
  290.1 2.0 collective-permute-start.25
  292.7 5.8 %convolution_convert_fusion.1 = bf16[768,2304]{1,0:T(8,128)(2,1)} fusion(bf16[800,2304]{1,0:T(8,128)(2,1)S(1)} %bitcast.179, f32[800,768]{1,0:T(8,128)S(1)} %copy-done.21, f32[768]{0:T(1024)S(1)} %copy-done.136, f32[768]{0:T(1024)S(1)} %copy-done.91, f32[800]{0:T(1024)S(1)} %copy-done.85, f32[800]{0:T(1024)S(1)} %broadcast_multiply_fusion.5), kind=kOutput, calls=%fused_computation.17 | convolution fusion | flops 2835996672 | bytes 9695488 | tf_op jit(solution)/shard_map/dot_general | solution.py:26
  298.6 2.9 reshape_reshape.3
  303.3 15.3 %collective-permute-done.26 = bf16[200,768]{1,0:T(8,128)(2,1)} collective-permute-done((bf16[200,768]{1,0:T(8,128)(2,1)}, bf16[200,768]{1,0:T(8,128)(2,1)}, u32[]{:S(2)}, u32[]{:S(2)}) %collective-permute-start.26) | collective-permute-done | bytes 307232 | tf_op jit(solution)/shard_map/ppermute | solution.py:70
  318.7 3.5 fusion.166
  322.3 2.5 convolution_convert_fusion.10
  328.6 3.4 pad_maximum_fusion
  332.0 2.4 convolution_convert_fusion.9
  334.4 2.0 copy-done.6
  336.4 13.3 %attend_back.3 = (bf16[7,112,2304]{2,1,0:T(8,128)(2,1)S(1)}, f32[1,2304]{1,0:T(1,128)S(1)}) custom-call(bf16[7,112,2304]{2,1,0:T(8,128)(2,1)S(1)} %bitcast.181, bf16[7,112,768]{2,1,0:T(8,128)(2,1)S(1)} %bitcast.189), custom_call_target="tpu_custom_call" | custom-call | flops 17999998976 | bytes 8429568 | tf_op jit(solution)/shard_map/attend_back/pallas_call | solution.py:218
  352.6 2.0 reshape.403
  354.6 1.9 constant_dynamic-slice_fusion.7
  357.9 2.2 collective-permute-start.42
  360.8 2.1 collective-permute-start.43
  362.9 5.0 %fusion.8 = f32[784,768]{1,0:T(8,128)S(1)} fusion(bf16[784,2304]{1,0:T(8,128)(2,1)S(1)} %bitcast.182, bf16[768,4096]{1,0:T(8,128)(2,1)} %all-gather.4.cloned.1.call-done), kind=kOutput, calls=%fused_computation.33 | convolution fusion | flops 2774532096 | bytes 9560064 | tf_op jit(solution)/shard_map/dot_general | solution.py:22
  370.8 2.1 fusion.58
  373.2 4.4 convolution_convert_fusion
  379.7 3.2 convolution_convert_fusion.4
  384.0 2.1 collective-permute-start.33
  391.4 4.6 collective-permute-done.32
  397.3 4.0 multiply_convert_fusion.2
  402.5 2.0 fusion.96
  404.5 2.9 collective-permute-done.33
  407.3 2.3 pad_maximum_fusion.3
  410.1 10.6 %collective-permute-done.31 = bf16[96,2560]{1,0:T(8,128)(2,1)} collective-permute-done((bf16[96,2560]{1,0:T(8,128)(2,1)}, bf16[96,2560]{1,0:T(8,128)(2,1)}, u32[]{:S(2)}, u32[]{:S(2)}) %collective-permute-start.31) | collective-permute-done | bytes 491552 | tf_op jit(solution)/shard_map/ppermute | solution.py:76
  428.4 5.3 %convolution_add_fusion = f32[784,768]{1,0:T(8,128)} fusion(f32[784,768]{1,0:T(8,128)S(1)} %copy-done.31, bf16[800,768]{1,0:T(8,128)(2,1)} %pad_maximum_fusion.3, s32[784]{0:T(1024)S(1)} %copy-done.130, s32[800]{0:T(1024)S(1)} %copy-done.58, s32[800]{0:T(1024)S(1)} %copy-done.113, s32[800]{0:T(1024)S(1)} %copy-done.126, s32[800]{0:T(1024)S(1)} %copy-done.123, ...), kind=kOutput, calls=%fused_computation.100 | convolution fusion | flops 971507712 | bytes 6074368 | tf_op jit(solution)/shard_map/dot_general | solution.py:26
  433.7 7.9 %collective-permute-done.36 = bf16[96,640]{0,1:T(8,128)(2,1)S(1)} collective-permute-done((bf16[96,640]{0,1:T(8,128)(2,1)S(1)}, bf16[96,640]{0,1:T(8,128)(2,1)S(1)}, u32[]{:S(2)}, u32[]{:S(2)}) %collective-permute-start.36) | collective-permute-done | bytes 122912 | tf_op jit(solution)/shard_map/ppermute | solution.py:31
  447.6 1.9 collective-permute-start.40
  451.7 2.0 collective-permute-done.38
  453.7 20.0 %collective-permute-done.39 = bf16[96,1152]{0,1:T(8,128)(2,1)S(1)} collective-permute-done((bf16[96,1152]{0,1:T(8,128)(2,1)S(1)}, bf16[96,1152]{0,1:T(8,128)(2,1)S(1)}, u32[]{:S(2)}, u32[]{:S(2)}) %collective-permute-start.39) | collective-permute-done | bytes 221216 | tf_op jit(solution)/shard_map/ppermute | solution.py:31
  (649 shorter events, 111.7 us)
Async XLA Ops:
  7.2 97.1 %all-gather.4.cloned.1.call-start = ((), (), s32[]{:S(2)}) async-start(), calls=%async_computation.3 | async-start | bytes 7077888 | tf_op jit(solution)/shard_map/all_gather | solution.py:334
  12.5 8.5 %collective-permute-start = (bf16[96,1024]{0,1:T(8,128)(2,1)S(1)}, bf16[96,1024]{0,1:T(8,128)(2,1)S(1)}, u32[]{:S(2)}, u32[]{:S(2)}) collective-permute-start(bf16[96,1024]{0,1:T(8,128)(2,1)S(1)} %pad_maximum_fusion.8), channel_id=1, source_target_pairs={{0,1},{1,2},{2,3},{3,0},{4,5},{5,6},{6,7},{7,4},{8,9},{9,10},{10,1... | collective-permute-start | bytes 589832 | tf_op jit(solution)/shard_map/ppermute | solution.py:31
  12.6 24.8 %collective-permute-start.1 = (bf16[96,1024]{0,1:T(8,128)(2,1)S(1)}, bf16[96,1024]{0,1:T(8,128)(2,1)S(1)}, u32[]{:S(2)}, u32[]{:S(2)}) collective-permute-start(bf16[96,1024]{0,1:T(8,128)(2,1)S(1)} %pad_maximum_fusion.8), channel_id=1, source_target_pairs={{0,2},{1,3},{2,0},{3,1},{4,6},{5,7},{6,4},{7,5},{8,10},{9,11},{10,... | collective-permute-start | bytes 589832 | tf_op jit(solution)/shard_map/ppermute | solution.py:31
  14.5 22.9 %collective-permute-start.2 = (bf16[96,1024]{0,1:T(8,128)(2,1)S(1)}, bf16[96,1024]{0,1:T(8,128)(2,1)S(1)}, u32[]{:S(2)}, u32[]{:S(2)}) collective-permute-start(bf16[96,1024]{0,1:T(8,128)(2,1)S(1)} %pad_maximum_fusion.8), channel_id=1, source_target_pairs={{0,3},{1,0},{2,1},{3,2},{4,7},{5,4},{6,5},{7,6},{8,11},{9,8},{10,9... | collective-permute-start | bytes 589832 | tf_op jit(solution)/shard_map/ppermute | solution.py:31
  15.1 137.9 %copy-start.57 = (s32[800]{0:T(1024)}, s32[800]{0:T(1024)S(1)}, u32[]{:S(2)}) copy-start(s32[800]{0:T(1024)S(1)} %iota.280) | copy-start | bytes 9604
  20.3 38.1 %copy-start.35 = (bf16[800,768]{1,0:T(8,128)(2,1)}, bf16[800,768]{1,0:T(8,128)(2,1)S(1)}, u32[]{:S(2)}) copy-start(bf16[800,768]{1,0:T(8,128)(2,1)S(1)} %convolution_convert_fusion.8) | copy-start | bytes 3686404
  41.2 117.3 %all-gather.6.cloned.1.call-start = ((), (), s32[]{:S(2)}) async-start(), calls=%async_computation.4 | async-start | bytes 5308416 | tf_op jit(solution)/shard_map/all_gather | solution.py:334
  41.7 5.6 %collective-permute-start.12 = (bf16[96,768]{1,0:T(8,128)(2,1)S(1)}, bf16[96,768]{1,0:T(8,128)(2,1)S(1)}, u32[]{:S(2)}, u32[]{:S(2)}) collective-permute-start(bf16[96,768]{1,0:T(8,128)(2,1)S(1)} %pad_maximum_fusion.11), channel_id=1, source_target_pairs={{0,1},{1,2},{2,3},{3,0},{4,5},{5,6},{6,7},{7,4},{8,9},{9,10},{10,1... | collective-permute-start | bytes 442376 | tf_op jit(solution)/shard_map/ppermute | solution.py:31
  41.8 14.8 %collective-permute-start.13 = (bf16[96,768]{1,0:T(8,128)(2,1)S(1)}, bf16[96,768]{1,0:T(8,128)(2,1)S(1)}, u32[]{:S(2)}, u32[]{:S(2)}) collective-permute-start(bf16[96,768]{1,0:T(8,128)(2,1)S(1)} %pad_maximum_fusion.11), channel_id=1, source_target_pairs={{0,2},{1,3},{2,0},{3,1},{4,6},{5,7},{6,4},{7,5},{8,10},{9,11},{10,... | collective-permute-start | bytes 442376 | tf_op jit(solution)/shard_map/ppermute | solution.py:31
  43.2 13.4 %collective-permute-start.14 = (bf16[96,768]{1,0:T(8,128)(2,1)S(1)}, bf16[96,768]{1,0:T(8,128)(2,1)S(1)}, u32[]{:S(2)}, u32[]{:S(2)}) collective-permute-start(bf16[96,768]{1,0:T(8,128)(2,1)S(1)} %pad_maximum_fusion.11), channel_id=1, source_target_pairs={{0,3},{1,0},{2,1},{3,2},{4,7},{5,4},{6,5},{7,6},{8,11},{9,8},{10,9... | collective-permute-start | bytes 442376 | tf_op jit(solution)/shard_map/ppermute | solution.py:31
  58.3 121.4 %all-gather.8.cloned.1.call-start = ((), (), s32[]{:S(2)}) async-start(), calls=%async_computation.5 | async-start | bytes 5308416 | tf_op jit(solution)/shard_map/all_gather | solution.py:334
  58.4 9.6 %collective-permute-start.6 = (bf16[200,768]{1,0:T(8,128)(2,1)S(1)}, bf16[200,768]{1,0:T(8,128)(2,1)}, u32[]{:S(2)}, u32[]{:S(2)}) collective-permute-start(bf16[200,768]{1,0:T(8,128)(2,1)S(1)} %get-tuple-element.175), channel_id=1, source_target_pairs={{0,1},{1,2},{2,3},{3,0},{4,5},{5,6},{6,7},{7,4},{8,9},{9,10},{10,1... | collective-permute-start | bytes 921608 | tf_op jit(solution)/shard_map/ppermute | solution.py:70
  58.5 28.1 %collective-permute-start.7 = (bf16[200,768]{1,0:T(8,128)(2,1)S(1)}, bf16[200,768]{1,0:T(8,128)(2,1)}, u32[]{:S(2)}, u32[]{:S(2)}) collective-permute-start(bf16[200,768]{1,0:T(8,128)(2,1)S(1)} %get-tuple-element.177), channel_id=1, source_target_pairs={{0,2},{1,3},{2,0},{3,1},{4,6},{5,7},{6,4},{7,5},{8,10},{9,11},{10,... | collective-permute-start | bytes 921608 | tf_op jit(solution)/shard_map/ppermute | solution.py:70
  59.2 27.3 %collective-permute-start.8 = (bf16[200,768]{1,0:T(8,128)(2,1)S(1)}, bf16[200,768]{1,0:T(8,128)(2,1)}, u32[]{:S(2)}, u32[]{:S(2)}) collective-permute-start(bf16[200,768]{1,0:T(8,128)(2,1)S(1)} %get-tuple-element.176), channel_id=1, source_target_pairs={{0,3},{1,0},{2,1},{3,2},{4,7},{5,4},{6,5},{7,6},{8,11},{9,8},{10,9... | collective-permute-start | bytes 921608 | tf_op jit(solution)/shard_map/ppermute | solution.py:70
  61.4 62.7 %copy-start.59 = (s32[800]{0:T(1024)}, s32[800]{0:T(1024)S(1)}, u32[]{:S(2)}) copy-start(s32[800]{0:T(1024)S(1)} %rem.278) | copy-start | bytes 9604
  63.3 71.6 %copy-start.14 = (bf16[4,200,768]{2,1,0:T(8,128)(2,1)}, bf16[4,200,768]{2,1,0:T(8,128)(2,1)S(1)}, u32[]{:S(2)}) copy-start(bf16[4,200,768]{2,1,0:T(8,128)(2,1)S(1)} %pad.33) | copy-start | bytes 3686404
  63.3 24.5 %copy-start.139 = (pred[784]{0:T(1024)(128)(4,1)}, pred[784]{0:T(1024)(128)(4,1)S(1)}, u32[]{:S(2)}) copy-start(pred[784]{0:T(1024)(128)(4,1)S(1)} %fusion.121) | copy-start | bytes 2356
  63.4 24.5 %copy-start.101 = (pred[784]{0:T(1024)(128)(4,1)}, pred[784]{0:T(1024)(128)(4,1)S(1)}, u32[]{:S(2)}) copy-start(pred[784]{0:T(1024)(128)(4,1)S(1)} %get-tuple-element.276) | copy-start | bytes 2356
  63.4 24.5 %copy-start.104 = (pred[784]{0:T(1024)(128)(4,1)}, pred[784]{0:T(1024)(128)(4,1)S(1)}, u32[]{:S(2)}) copy-start(pred[784]{0:T(1024)(128)(4,1)S(1)} %get-tuple-element.277) | copy-start | bytes 2356
  63.4 24.5 %copy-start.64 = (s32[784]{0:T(1024)}, s32[784]{0:T(1024)S(1)}, u32[]{:S(2)}) copy-start(s32[784]{0:T(1024)S(1)} %get-tuple-element.282) | copy-start | bytes 9412
  66.1 38.1 %copy-start.39 = (pred[768,768]{1,0:T(32,128)(4,1)}, pred[768,768]{1,0:T(32,128)(4,1)S(1)}, u32[]{:S(2)}) copy-start(pred[768,768]{1,0:T(32,128)(4,1)S(1)} %get-tuple-element.280) | copy-start | bytes 1769476
  66.1 38.1 %copy-start.41 = (pred[768,768]{1,0:T(32,128)(4,1)}, pred[768,768]{1,0:T(32,128)(4,1)S(1)}, u32[]{:S(2)}) copy-start(pred[768,768]{1,0:T(32,128)(4,1)S(1)} %get-tuple-element.281) | copy-start | bytes 1769476
  87.9 7.2 %collective-permute-start.18 = (bf16[96,768]{1,0:T(8,128)(2,1)S(1)}, bf16[96,768]{1,0:T(8,128)(2,1)S(1)}, u32[]{:S(2)}, u32[]{:S(2)}) collective-permute-start(bf16[96,768]{1,0:T(8,128)(2,1)S(1)} %copy-done.45), channel_id=1, source_target_pairs={{0,1},{1,2},{2,3},{3,0},{4,5},{5,6},{6,7},{7,4},{8,9},{9,10},{10,1... | collective-permute-start | bytes 442376 | tf_op jit(solution)/shard_map/ppermute | solution.py:31
  88.0 15.2 %collective-permute-start.19 = (bf16[96,768]{1,0:T(8,128)(2,1)S(1)}, bf16[96,768]{1,0:T(8,128)(2,1)S(1)}, u32[]{:S(2)}, u32[]{:S(2)}) collective-permute-start(bf16[96,768]{1,0:T(8,128)(2,1)S(1)} %copy-done.45), channel_id=1, source_target_pairs={{0,2},{1,3},{2,0},{3,1},{4,6},{5,7},{6,4},{7,5},{8,10},{9,11},{10,... | collective-permute-start | bytes 442376 | tf_op jit(solution)/shard_map/ppermute | solution.py:31
  89.7 13.4 %collective-permute-start.20 = (bf16[96,768]{1,0:T(8,128)(2,1)S(1)}, bf16[96,768]{1,0:T(8,128)(2,1)S(1)}, u32[]{:S(2)}, u32[]{:S(2)}) collective-permute-start(bf16[96,768]{1,0:T(8,128)(2,1)S(1)} %copy-done.45), channel_id=1, source_target_pairs={{0,3},{1,0},{2,1},{3,2},{4,7},{5,4},{6,5},{7,6},{8,11},{9,8},{10,9... | collective-permute-start | bytes 442376 | tf_op jit(solution)/shard_map/ppermute | solution.py:31
  104.2 162.5 %reduce-scatter.6.cloned.1.call-start = ((), (), s32[]{:S(2)}) async-start(), calls=%async_computation.7 | async-start | bytes 5308416 | tf_op jit(solution)/shard_map/reduce_scatter | solution.py:464
  105.9 15.8 %collective-permute-start.3 = (bf16[96,768]{1,0:T(8,128)(2,1)S(1)}, bf16[96,768]{1,0:T(8,128)(2,1)S(1)}, u32[]{:S(2)}, u32[]{:S(2)}) collective-permute-start(bf16[96,768]{1,0:T(8,128)(2,1)S(1)} %bitcast.210), channel_id=1, source_target_pairs={{0,1},{1,2},{2,3},{3,0},{4,5},{5,6},{6,7},{7,4},{8,9},{9,10},{10,1... | collective-permute-start | bytes 442376 | tf_op jit(solution)/shard_map/ppermute | solution.py:31
  105.9 15.8 %collective-permute-start.4 = (bf16[96,768]{1,0:T(8,128)(2,1)S(1)}, bf16[96,768]{1,0:T(8,128)(2,1)S(1)}, u32[]{:S(2)}, u32[]{:S(2)}) collective-permute-start(bf16[96,768]{1,0:T(8,128)(2,1)S(1)} %bitcast.211), channel_id=1, source_target_pairs={{0,2},{1,3},{2,0},{3,1},{4,6},{5,7},{6,4},{7,5},{8,10},{9,11},{10,... | collective-permute-start | bytes 442376 | tf_op jit(solution)/shard_map/ppermute | solution.py:31
  107.0 14.7 %collective-permute-start.5 = (bf16[96,768]{1,0:T(8,128)(2,1)S(1)}, bf16[96,768]{1,0:T(8,128)(2,1)S(1)}, u32[]{:S(2)}, u32[]{:S(2)}) collective-permute-start(bf16[96,768]{1,0:T(8,128)(2,1)S(1)} %bitcast.212), channel_id=1, source_target_pairs={{0,3},{1,0},{2,1},{3,2},{4,7},{5,4},{6,5},{7,6},{8,11},{9,8},{10,9... | collective-permute-start | bytes 442376 | tf_op jit(solution)/shard_map/ppermute | solution.py:31
  129.7 23.3 %collective-permute-start.10 = (bf16[200,768]{1,0:T(8,128)(2,1)}, bf16[200,768]{1,0:T(8,128)(2,1)}, u32[]{:S(2)}, u32[]{:S(2)}) collective-permute-start(bf16[200,768]{1,0:T(8,128)(2,1)} %get-tuple-element.173), channel_id=1, source_target_pairs={{0,2},{1,3},{2,0},{3,1},{4,6},{5,7},{6,4},{7,5},{8,10},{9,11},{10,... | collective-permute-start | bytes 921608 | tf_op jit(solution)/shard_map/ppermute | solution.py:70
  132.5 20.5 %collective-permute-start.11 = (bf16[200,768]{1,0:T(8,128)(2,1)S(1)}, bf16[200,768]{1,0:T(8,128)(2,1)}, u32[]{:S(2)}, u32[]{:S(2)}) collective-permute-start(bf16[200,768]{1,0:T(8,128)(2,1)S(1)} %get-tuple-element.172), channel_id=1, source_target_pairs={{0,1},{1,2},{2,3},{3,0},{4,5},{5,6},{6,7},{7,4},{8,9},{9,10},{10,1... | collective-permute-start | bytes 921608 | tf_op jit(solution)/shard_map/ppermute | solution.py:70
  132.6 20.4 %collective-permute-start.9 = (bf16[200,768]{1,0:T(8,128)(2,1)S(1)}, bf16[200,768]{1,0:T(8,128)(2,1)}, u32[]{:S(2)}, u32[]{:S(2)}) collective-permute-start(bf16[200,768]{1,0:T(8,128)(2,1)S(1)} %get-tuple-element.174), channel_id=1, source_target_pairs={{0,3},{1,0},{2,1},{3,2},{4,7},{5,4},{6,5},{7,6},{8,11},{9,8},{10,9... | collective-permute-start | bytes 921608 | tf_op jit(solution)/shard_map/ppermute | solution.py:70
  164.7 25.5 %collective-permute-start.15 = (bf16[96,3072]{1,0:T(8,128)(2,1)S(1)}, bf16[96,3072]{1,0:T(8,128)(2,1)S(1)}, u32[]{:S(2)}, u32[]{:S(2)}) collective-permute-start(bf16[96,3072]{1,0:T(8,128)(2,1)S(1)} %pad_maximum_fusion.5.refs_0_), channel_id=1, source_target_pairs={{0,8},{4,12},{8,0},{12,4},{16,24},{20,28},{24,16},{28,20},{1,9},{5... | collective-permute-start | bytes 1769480 | tf_op jit(solution)/shard_map/ppermute | solution.py:76
  165.9 24.2 %collective-permute-start.16 = (bf16[96,3072]{1,0:T(8,128)(2,1)S(1)}, bf16[96,3072]{1,0:T(8,128)(2,1)S(1)}, u32[]{:S(2)}, u32[]{:S(2)}) collective-permute-start(bf16[96,3072]{1,0:T(8,128)(2,1)S(1)} %pad_maximum_fusion.5.refs_0_), channel_id=1, source_target_pairs={{0,16},{4,20},{8,24},{12,28},{16,0},{20,4},{24,8},{28,12},{1,17},{... | collective-permute-start | bytes 1769480 | tf_op jit(solution)/shard_map/ppermute | solution.py:76
  167.1 27.4 %collective-permute-start.17 = (bf16[96,3072]{1,0:T(8,128)(2,1)S(1)}, bf16[96,3072]{1,0:T(8,128)(2,1)S(1)}, u32[]{:S(2)}, u32[]{:S(2)}) collective-permute-start(bf16[96,3072]{1,0:T(8,128)(2,1)S(1)} %pad_maximum_fusion.5.refs_0_), channel_id=1, source_target_pairs={{0,24},{4,28},{8,16},{12,20},{16,8},{20,12},{24,0},{28,4},{1,25},{... | collective-permute-start | bytes 1769480 | tf_op jit(solution)/shard_map/ppermute | solution.py:76
  194.5 11.5 %collective-permute-start.21 = (bf16[96,3072]{1,0:T(8,128)(2,1)S(1)}, bf16[96,3072]{1,0:T(8,128)(2,1)S(1)}, u32[]{:S(2)}, u32[]{:S(2)}) collective-permute-start(bf16[96,3072]{1,0:T(8,128)(2,1)S(1)} %pad_maximum_fusion.5.refs_0_), channel_id=1, source_target_pairs={{0,4},{4,0},{8,12},{12,8},{16,20},{20,16},{24,28},{28,24},{1,5},{5... | collective-permute-start | bytes 1769480 | tf_op jit(solution)/shard_map/ppermute | solution.py:76
  194.5 11.5 %collective-permute-start.22 = (bf16[96,3072]{1,0:T(8,128)(2,1)S(1)}, bf16[96,3072]{1,0:T(8,128)(2,1)S(1)}, u32[]{:S(2)}, u32[]{:S(2)}) collective-permute-start(bf16[96,3072]{1,0:T(8,128)(2,1)S(1)} %collective-permute-done.15.refs_2_), channel_id=1, source_target_pairs={{0,4},{4,0},{8,12},{12,8},{16,20},{20,16},{24,28},{28,24},{1,5},{5... | collective-permute-start | bytes 1769480 | tf_op jit(solution)/shard_map/ppermute | solution.py:76
  195.0 11.0 %collective-permute-start.23 = (bf16[96,3072]{1,0:T(8,128)(2,1)S(1)}, bf16[96,3072]{1,0:T(8,128)(2,1)}, u32[]{:S(2)}, u32[]{:S(2)}) collective-permute-start(bf16[96,3072]{1,0:T(8,128)(2,1)S(1)} %collective-permute-done.16.refs_4_), channel_id=1, source_target_pairs={{0,4},{4,0},{8,12},{12,8},{16,20},{20,16},{24,28},{28,24},{1,5},{5... | collective-permute-start | bytes 1769480 | tf_op jit(solution)/shard_map/ppermute | solution.py:76
  195.0 11.0 %collective-permute-start.24 = (bf16[96,3072]{1,0:T(8,128)(2,1)S(1)}, bf16[96,3072]{1,0:T(8,128)(2,1)}, u32[]{:S(2)}, u32[]{:S(2)}) collective-permute-start(bf16[96,3072]{1,0:T(8,128)(2,1)S(1)} %collective-permute-done.17.refs_6_), channel_id=1, source_target_pairs={{0,4},{4,0},{8,12},{12,8},{16,20},{20,16},{24,28},{28,24},{1,5},{5... | collective-permute-start | bytes 1769480 | tf_op jit(solution)/shard_map/ppermute | solution.py:76
  202.6 150.0 %reduce-scatter.4.cloned.1.call-start = ((), (), s32[]{:S(2)}) async-start(), calls=%async_computation.6 | async-start | bytes 5308416 | tf_op jit(solution)/shard_map/reduce_scatter | solution.py:464
  266.0 176.5 %reduce-scatter.8.cloned.1.call-start = ((), (), s32[]{:S(2)}) async-start(), calls=%async_computation.8 | async-start | bytes 7962624 | tf_op jit(solution)/shard_map/reduce_scatter | solution.py:464
  269.8 22.4 %collective-permute-start.44 = (bf16[96,768]{1,0:T(8,128)(2,1)S(1)}, bf16[96,768]{1,0:T(8,128)(2,1)S(1)}, u32[]{:S(2)}, u32[]{:S(2)}) collective-permute-start(bf16[96,768]{1,0:T(8,128)(2,1)S(1)} %bitcast.215), channel_id=1, source_target_pairs={{0,1},{1,2},{2,3},{3,0},{4,5},{5,6},{6,7},{7,4},{8,9},{9,10},{10,1... | collective-permute-start | bytes 442376 | tf_op jit(solution)/shard_map/ppermute | solution.py:31
  270.7 30.8 %collective-permute-start.45 = (bf16[96,768]{1,0:T(8,128)(2,1)S(1)}, bf16[96,768]{1,0:T(8,128)(2,1)}, u32[]{:S(2)}, u32[]{:S(2)}) collective-permute-start(bf16[96,768]{1,0:T(8,128)(2,1)S(1)} %bitcast.214), channel_id=1, source_target_pairs={{0,2},{1,3},{2,0},{3,1},{4,6},{5,7},{6,4},{7,5},{8,10},{9,11},{10,... | collective-permute-start | bytes 442376 | tf_op jit(solution)/shard_map/ppermute | solution.py:31
  277.1 24.5 %collective-permute-start.46 = (bf16[96,768]{1,0:T(8,128)(2,1)}, bf16[96,768]{1,0:T(8,128)(2,1)}, u32[]{:S(2)}, u32[]{:S(2)}) collective-permute-start(bf16[96,768]{1,0:T(8,128)(2,1)} %bitcast.163), channel_id=1, source_target_pairs={{0,3},{1,0},{2,1},{3,2},{4,7},{5,4},{6,5},{7,6},{8,11},{9,8},{10,9... | collective-permute-start | bytes 442376 | tf_op jit(solution)/shard_map/ppermute | solution.py:31
  290.1 13.2 %collective-permute-start.25 = (bf16[200,768]{1,0:T(8,128)(2,1)}, bf16[200,768]{1,0:T(8,128)(2,1)}, u32[]{:S(2)}, u32[]{:S(2)}) collective-permute-start(bf16[200,768]{1,0:T(8,128)(2,1)} %get-tuple-element.170), channel_id=1, source_target_pairs={{0,1},{1,2},{2,3},{3,0},{4,5},{5,6},{6,7},{7,4},{8,9},{9,10},{10,1... | collective-permute-start | bytes 921608 | tf_op jit(solution)/shard_map/ppermute | solution.py:70
  292.1 26.5 %collective-permute-start.26 = (bf16[200,768]{1,0:T(8,128)(2,1)}, bf16[200,768]{1,0:T(8,128)(2,1)}, u32[]{:S(2)}, u32[]{:S(2)}) collective-permute-start(bf16[200,768]{1,0:T(8,128)(2,1)} %get-tuple-element.169), channel_id=1, source_target_pairs={{0,2},{1,3},{2,0},{3,1},{4,6},{5,7},{6,4},{7,5},{8,10},{9,11},{10,... | collective-permute-start | bytes 921608 | tf_op jit(solution)/shard_map/ppermute | solution.py:70
  292.1 26.5 %collective-permute-start.27 = (bf16[200,768]{1,0:T(8,128)(2,1)}, bf16[200,768]{1,0:T(8,128)(2,1)}, u32[]{:S(2)}, u32[]{:S(2)}) collective-permute-start(bf16[200,768]{1,0:T(8,128)(2,1)} %get-tuple-element.168), channel_id=1, source_target_pairs={{0,3},{1,0},{2,1},{3,2},{4,7},{5,4},{6,5},{7,6},{8,11},{9,8},{10,9... | collective-permute-start | bytes 921608 | tf_op jit(solution)/shard_map/ppermute | solution.py:70
  357.2 30.6 %collective-permute-start.41 = (bf16[96,768]{1,0:T(8,128)(2,1)}, bf16[96,768]{1,0:T(8,128)(2,1)}, u32[]{:S(2)}, u32[]{:S(2)}) collective-permute-start(bf16[96,768]{1,0:T(8,128)(2,1)} %bitcast.168), channel_id=1, source_target_pairs={{0,1},{1,2},{2,3},{3,0},{4,5},{5,6},{6,7},{7,4},{8,9},{9,10},{10,1... | collective-permute-start | bytes 442376 | tf_op jit(solution)/shard_map/ppermute | solution.py:31
  357.9 31.7 %collective-permute-start.42 = (bf16[96,768]{1,0:T(8,128)(2,1)}, bf16[96,768]{1,0:T(8,128)(2,1)}, u32[]{:S(2)}, u32[]{:S(2)}) collective-permute-start(bf16[96,768]{1,0:T(8,128)(2,1)} %bitcast.167), channel_id=1, source_target_pairs={{0,2},{1,3},{2,0},{3,1},{4,6},{5,7},{6,4},{7,5},{8,10},{9,11},{10,... | collective-permute-start | bytes 442376 | tf_op jit(solution)/shard_map/ppermute | solution.py:31
  360.8 29.8 %collective-permute-start.43 = (bf16[96,768]{1,0:T(8,128)(2,1)}, bf16[96,768]{1,0:T(8,128)(2,1)}, u32[]{:S(2)}, u32[]{:S(2)}) collective-permute-start(bf16[96,768]{1,0:T(8,128)(2,1)} %bitcast.166), channel_id=1, source_target_pairs={{0,3},{1,0},{2,1},{3,2},{4,7},{5,4},{6,5},{7,6},{8,11},{9,8},{10,9... | collective-permute-start | bytes 442376 | tf_op jit(solution)/shard_map/ppermute | solution.py:31
  378.1 5.9 %collective-permute-start.28 = (bf16[4,96,2560]{2,1,0:T(8,128)(2,1)S(1)}, bf16[4,96,2560]{2,1,0:T(8,128)(2,1)S(1)}, u32[]{:S(2)}, u32[]{:S(2)}) collective-permute-start(bf16[4,96,2560]{2,1,0:T(8,128)(2,1)S(1)} %pad_maximum_fusion.1), channel_id=1, source_target_pairs={{0,4},{4,0},{8,12},{12,8},{16,20},{20,16},{24,28},{28,24},{1,5},{5... | collective-permute-start | bytes 5898248 | tf_op jit(solution)/shard_map/ppermute | solution.py:76
  383.9 12.1 %collective-permute-start.32 = (bf16[200,768]{1,0:T(8,128)(2,1)S(1)}, bf16[200,768]{1,0:T(8,128)(2,1)S(1)}, u32[]{:S(2)}, u32[]{:S(2)}) collective-permute-start(bf16[200,768]{1,0:T(8,128)(2,1)S(1)} %get-tuple-element.166), channel_id=1, source_target_pairs={{0,3},{1,0},{2,1},{3,2},{4,7},{5,4},{6,5},{7,6},{8,11},{9,8},{10,9... | collective-permute-start | bytes 921608 | tf_op jit(solution)/shard_map/ppermute | solution.py:70
  384.0 23.3 %collective-permute-start.33 = (bf16[200,768]{1,0:T(8,128)(2,1)}, bf16[200,768]{1,0:T(8,128)(2,1)}, u32[]{:S(2)}, u32[]{:S(2)}) collective-permute-start(bf16[200,768]{1,0:T(8,128)(2,1)} %get-tuple-element.165), channel_id=1, source_target_pairs={{0,2},{1,3},{2,0},{3,1},{4,6},{5,7},{6,4},{7,5},{8,10},{9,11},{10,... | collective-permute-start | bytes 921608 | tf_op jit(solution)/shard_map/ppermute | solution.py:70
  387.8 19.5 %collective-permute-start.34 = (bf16[200,768]{1,0:T(8,128)(2,1)}, bf16[200,768]{1,0:T(8,128)(2,1)}, u32[]{:S(2)}, u32[]{:S(2)}) collective-permute-start(bf16[200,768]{1,0:T(8,128)(2,1)} %get-tuple-element.164), channel_id=1, source_target_pairs={{0,1},{1,2},{2,3},{3,0},{4,5},{5,6},{6,7},{7,4},{8,9},{9,10},{10,1... | collective-permute-start | bytes 921608 | tf_op jit(solution)/shard_map/ppermute | solution.py:70
  389.6 20.5 %collective-permute-start.29 = (bf16[96,2560]{1,0:T(8,128)(2,1)}, bf16[96,2560]{1,0:T(8,128)(2,1)}, u32[]{:S(2)}, u32[]{:S(2)}) collective-permute-start(bf16[96,2560]{1,0:T(8,128)(2,1)} %get-tuple-element.160), channel_id=1, source_target_pairs={{0,8},{4,12},{8,0},{12,4},{16,24},{20,28},{24,16},{28,20},{1,9},{5... | collective-permute-start | bytes 1474568 | tf_op jit(solution)/shard_map/ppermute | solution.py:76
  390.6 19.5 %collective-permute-start.30 = (bf16[96,2560]{1,0:T(8,128)(2,1)}, bf16[96,2560]{1,0:T(8,128)(2,1)}, u32[]{:S(2)}, u32[]{:S(2)}) collective-permute-start(bf16[96,2560]{1,0:T(8,128)(2,1)} %get-tuple-element.162), channel_id=1, source_target_pairs={{0,16},{4,20},{8,24},{12,28},{16,0},{20,4},{24,8},{28,12},{1,17},{... | collective-permute-start | bytes 1474568 | tf_op jit(solution)/shard_map/ppermute | solution.py:76
  396.0 24.7 %collective-permute-start.31 = (bf16[96,2560]{1,0:T(8,128)(2,1)}, bf16[96,2560]{1,0:T(8,128)(2,1)}, u32[]{:S(2)}, u32[]{:S(2)}) collective-permute-start(bf16[96,2560]{1,0:T(8,128)(2,1)} %get-tuple-element.161), channel_id=1, source_target_pairs={{0,24},{4,28},{8,16},{12,20},{16,8},{20,12},{24,0},{28,4},{1,25},{... | collective-permute-start | bytes 1474568 | tf_op jit(solution)/shard_map/ppermute | solution.py:76
  425.7 8.0 %collective-permute-start.35 = (bf16[96,640]{0,1:T(8,128)(2,1)S(1)}, bf16[96,640]{0,1:T(8,128)(2,1)S(1)}, u32[]{:S(2)}, u32[]{:S(2)}) collective-permute-start(bf16[96,640]{0,1:T(8,128)(2,1)S(1)} %get-tuple-element.188), channel_id=1, source_target_pairs={{0,1},{1,2},{2,3},{3,0},{4,5},{5,6},{6,7},{7,4},{8,9},{9,10},{10,1... | collective-permute-start | bytes 368648 | tf_op jit(solution)/shard_map/ppermute | solution.py:31
  426.3 15.4 %collective-permute-start.36 = (bf16[96,640]{0,1:T(8,128)(2,1)S(1)}, bf16[96,640]{0,1:T(8,128)(2,1)S(1)}, u32[]{:S(2)}, u32[]{:S(2)}) collective-permute-start(bf16[96,640]{0,1:T(8,128)(2,1)S(1)} %get-tuple-element.189), channel_id=1, source_target_pairs={{0,2},{1,3},{2,0},{3,1},{4,6},{5,7},{6,4},{7,5},{8,10},{9,11},{10,... | collective-permute-start | bytes 368648 | tf_op jit(solution)/shard_map/ppermute | solution.py:31
  427.8 13.9 %collective-permute-start.37 = (bf16[96,640]{0,1:T(8,128)(2,1)S(1)}, bf16[96,640]{0,1:T(8,128)(2,1)S(1)}, u32[]{:S(2)}, u32[]{:S(2)}) collective-permute-start(bf16[96,640]{0,1:T(8,128)(2,1)S(1)} %get-tuple-element.190), channel_id=1, source_target_pairs={{0,3},{1,0},{2,1},{3,2},{4,7},{5,4},{6,5},{7,6},{8,11},{9,8},{10,9... | collective-permute-start | bytes 368648 | tf_op jit(solution)/shard_map/ppermute | solution.py:31
  446.0 27.9 %slice-start.2 = ((f32[96,640]{0,1:T(8,128)}), f32[96,576]{0,1:T(8,128)S(1)}, s32[]{:S(2)}) async-start(f32[96,640]{0,1:T(8,128)} %copy-done.34), calls=%async_computation.11 | async-start | bytes 589824 | tf_op jit(solution)/shard_map/slice | solution.py:543
  446.1 7.6 %collective-permute-start.38 = (bf16[96,1152]{0,1:T(8,128)(2,1)S(1)}, bf16[96,1152]{0,1:T(8,128)(2,1)S(1)}, u32[]{:S(2)}, u32[]{:S(2)}) collective-permute-start(bf16[96,1152]{0,1:T(8,128)(2,1)S(1)} %get-tuple-element.178), channel_id=1, source_target_pairs={{0,1},{1,2},{2,3},{3,0},{4,5},{5,6},{6,7},{7,4},{8,9},{9,10},{10,1... | collective-permute-start | bytes 663560 | tf_op jit(solution)/shard_map/ppermute | solution.py:31
  446.1 27.5 %collective-permute-start.39 = (bf16[96,1152]{0,1:T(8,128)(2,1)S(1)}, bf16[96,1152]{0,1:T(8,128)(2,1)S(1)}, u32[]{:S(2)}, u32[]{:S(2)}) collective-permute-start(bf16[96,1152]{0,1:T(8,128)(2,1)S(1)} %get-tuple-element.180), channel_id=1, source_target_pairs={{0,2},{1,3},{2,0},{3,1},{4,6},{5,7},{6,4},{7,5},{8,10},{9,11},{10,... | collective-permute-start | bytes 663560 | tf_op jit(solution)/shard_map/ppermute | solution.py:31
  447.6 26.1 %collective-permute-start.40 = (bf16[96,1152]{0,1:T(8,128)(2,1)S(1)}, bf16[96,1152]{0,1:T(8,128)(2,1)S(1)}, u32[]{:S(2)}, u32[]{:S(2)}) collective-permute-start(bf16[96,1152]{0,1:T(8,128)(2,1)S(1)} %get-tuple-element.179), channel_id=1, source_target_pairs={{0,3},{1,0},{2,1},{3,2},{4,7},{5,4},{6,5},{7,6},{8,11},{9,8},{10,9... | collective-permute-start | bytes 663560 | tf_op jit(solution)/shard_map/ppermute | solution.py:31
  (154 other events, 1157.7 us)
Sparse Core Ops, SparseCore 0:
  41.3 46.5 all-gather.3
  90.3 38.9 all-gather.5
  131.1 40.9 all-gather.7
  202.7 57.9 reduce-scatter.5
  266.1 57.6 reduce-scatter.3
  334.5 72.6 reduce-scatter.7

commit v4 on v3

--- a/solution.py
+++ b/solution.py
@@ -369,8 +369,9 @@
         [piece[:, 4 * part :].reshape(srow, shared_cols) for piece in line_order(time_back)]
     )
     time_all = spread(jnp.concatenate([branch_rows(time_back), shared_rows], axis=1))
-    fc1_own, came_x = together(fc1_weight, came_x)
+    fc1_own, held_x = together(fc1_weight, sent_x)
     fc1_back = line_gather(fc1_own)
+    *fc1_back, came_x = together(*fc1_back, came_x)
     fc2_own, time_all = together(fc2_own, time_all)
     fc2_back = line_gather(fc2_own)
     space_all = spread(branch_rows(space_back))

time: 493 us -> 496 us (level)
    ppermute x12, waiting for transfers between devices: 57.2 us -> 65.3 us  [swap_blocks(): moved.append(lax.ppermute(blocks[k], 'tensor', pairs))]
    ppermute x24, waiting for transfers between devices: 66.4 us -> 58.4 us  [line_shift(): lax.ppermute(block, 'tensor', [(i, (i + step) % count) for i in range(cou...]
    unnamed x337 -> x339, local copies, waits for them, and re-layouts: 21.6 us -> 21.7 us
where the time goes in v4:
time: 496 us; the launch traced here: 488 us
  waiting for transfers between devices  138 us (28%)
  matrix products  135 us (27%)
  local copies, waits for them, and re-layouts  63.9 us (13%)
  starting transfers between devices  56.7 us (11%)
  Pallas kernels  40.7 us (8%)
  other arithmetic  35.1 us (7%)
  between operations  17.9 us (4%)
    ppermute x12, waiting for transfers between devices, swap_blocks(): moved.append(lax.ppermute(blocks[k], 'tensor', pairs))  65.3 us
    ppermute x24, waiting for transfers between devices, line_shift(): lax.ppermute(block, 'tensor', [(i, (i + step) % count) for i in range(cou...  58.4 us
    dot_general x12, matrix products, dot_tn(): lax.dot_general(left, right, (((0,), (0,)), ((), ())), preferred_element_...  51.3 us
    dot_general x10, matrix products, dot_nn(): lax.dot_general(left, right, (((1,), (0,)), ((), ())), preferred_element_...  50.4 us
    dot_general x8, matrix products, dot_nt(): lax.dot_general(left, right, (((1,), (1,)), ((), ())), preferred_element_...  33.4 us
    ppermute x24, starting transfers between devices, line_shift(): lax.ppermute(block, 'tensor', [(i, (i + step) % count) for i in range(cou...  31.9 us
    pallas_call x2, Pallas kernels, attend_back(): pl.pallas_call(partial(attend_back_kernel, group, keys, width), grid=(blo...  27.9 us
    unnamed x339, local copies, waits for them, and re-layouts  21.7 us
  transfers between devices with their start and end apart: 53, of which 17 were waited for; matrix products, arithmetic and copies ran while one was open for 42% of the time, Pallas kernels for 8%

profile of v4, /device:TPU:24, one launch (start us, length us, event | category | flops | bytes accessed | tf_op | source)
XLA Modules:
  0.0 487.7 jit_solution(5499746077080897001)
XLA Ops:
  16.0 4.1 convolution_convert_fusion.8
  21.0 16.4 %collective-permute-done.1 = bf16[96,1024]{0,1:T(8,128)(2,1)S(1)} collective-permute-done((bf16[96,1024]{0,1:T(8,128)(2,1)S(1)}, bf16[96,1024]{0,1:T(8,128)(2,1)S(1)}, u32[]{:S(2)}, u32[]{:S(2)}) %collective-permute-start.1) | collective-permute-done | bytes 196640 | tf_op jit(solution)/shard_map/ppermute | solution.py:31
  45.1 2.2 collective-permute-done.15
  47.3 9.3 %collective-permute-done.16 = bf16[96,768]{1,0:T(8,128)(2,1)S(1)} collective-permute-done((bf16[96,768]{1,0:T(8,128)(2,1)S(1)}, bf16[96,768]{1,0:T(8,128)(2,1)S(1)}, u32[]{:S(2)}, u32[]{:S(2)}) %collective-permute-start.16) | collective-permute-done | bytes 147488 | tf_op jit(solution)/shard_map/ppermute | solution.py:31
  62.0 2.2 collective-permute-start.10
  64.9 2.0 fusion.142.clone.4
  67.1 25.6 %collective-permute-done.10 = bf16[200,768]{1,0:T(8,128)(2,1)S(1)} collective-permute-done((bf16[200,768]{1,0:T(8,128)(2,1)S(1)}, bf16[200,768]{1,0:T(8,128)(2,1)S(1)}, u32[]{:S(2)}, u32[]{:S(2)}) %collective-permute-start.10) | collective-permute-done | bytes 307232 | tf_op jit(solution)/shard_map/ppermute | solution.py:70
  96.1 5.7 %collective-permute-done.9 = bf16[200,768]{1,0:T(8,128)(2,1)} collective-permute-done((bf16[200,768]{1,0:T(8,128)(2,1)}, bf16[200,768]{1,0:T(8,128)(2,1)}, u32[]{:S(2)}, u32[]{:S(2)}) %collective-permute-start.9) | collective-permute-done | bytes 307232 | tf_op jit(solution)/shard_map/ppermute | solution.py:70
  110.3 2.1 collective-permute-start.3
  114.6 5.9 %add_convert_fusion.1 = bf16[784,2304]{1,0:T(8,128)(2,1)S(1)} fusion(f32[2304]{0:T(1024)S(1)} %get-tuple-element.269, bf16[768,4096]{1,0:T(8,128)(2,1)} %all-gather.4.cloned.1.call-done, f32[784,768]{1,0:T(8,128)} %copy-done.25, f32[768]{0:T(1024)S(1)} %get-tuple-element.158, f32[768]{0:T(1024)S(1)} %get-tuple-element.159, f32[784]{0:T(1024)S(1)} %add_rsqrt_fusion.2, ...), kind=kOutput, calls=%fused_computation.10 | convolution fusion | flops 2781155328 | bytes 9581696 | tf_op jit(solution)/shard_map/dot_general | solution.py:18
  120.5 4.6 attend.2
  125.9 2.2 add_convert_fusion.6
  128.2 4.7 convolution_convert_fusion.7
  133.8 2.9 collective-permute-start.12
  143.7 2.6 collective-permute-done.12
  146.3 10.6 %collective-permute-done.13 = bf16[200,768]{1,0:T(8,128)(2,1)} collective-permute-done((bf16[200,768]{1,0:T(8,128)(2,1)S(1)}, bf16[200,768]{1,0:T(8,128)(2,1)}, u32[]{:S(2)}, u32[]{:S(2)}) %collective-permute-start.13) | collective-permute-done | bytes 307232 | tf_op jit(solution)/shard_map/ppermute | solution.py:70
  156.9 4.4 fusion.164
  162.1 5.7 %add_convert_fusion = bf16[800,2304]{1,0:T(8,128)(2,1)S(1)} fusion(f32[2304]{0:T(1024)S(1)} %copy-done.98, bf16[768,3072]{1,0:T(8,128)(2,1)} %all-gather.6.cloned.1.call-done, f32[800,768]{1,0:T(8,128)S(1)} %get-tuple-element.273, f32[768]{0:T(1024)S(1)} %copy-done.136, f32[768]{0:T(1024)S(1)} %copy-done.91, f32[800]{0:T(1024)S(1)} %add_rsqrt_fusion.1, ...), kind=kOutput, calls=%fused_computation.9 | convolution fusion | flops 2837913600 | bytes 9704704 | tf_op jit(solution)/shard_map/dot_general | solution.py:18
  171.6 6.5 %attend.3 = bf16[4,200,768]{2,1,0:T(8,128)(2,1)S(1)} custom-call(bf16[4,200,2304]{2,1,0:T(8,128)(2,1)S(1)} %bitcast.176), custom_call_target="tpu_custom_call" | custom-call | flops 8000000000 | bytes 4915200 | tf_op jit(solution)/shard_map/attend/pallas_call | solution.py:201
  178.1 3.0 fusion.165
  183.1 10.4 %multiply_convert_fusion.1 = (bf16[800,3072]{1,0:T(8,128)(2,1)S(1)}, f32[800,3072]{1,0:T(8,128)}) fusion(f32[3072]{0:T(1024)S(1)} %copy-done.95, bf16[768,3072]{1,0:T(8,128)(2,1)} %all-gather.8.cloned.1.call-done, f32[800,768]{1,0:T(8,128)} %copy-done.16, f32[768]{0:T(1024)S(1)} %copy-done.138, f32[768]{0:T(1024)S(1)} %copy-done.93, ...), kind=kOutput, calls=%fused_computation.7 | convolution fusion | flops 3792691200 | bytes 21946624 | tf_op jit(solution)/shard_map/dot_general | solution.py:18
  193.5 3.7 collective-permute-done.19.refs_4_
  198.2 6.9 %convolution_convert_fusion.3 = bf16[768,3072]{1,0:T(8,128)(2,1)} fusion(bf16[800,768]{1,0:T(8,128)(2,1)S(1)} %copy-done.28, bf16[800,3072]{1,0:T(8,128)(2,1)S(1)} %get-tuple-element.96), kind=kOutput, calls=%fused_computation.19 | convolution fusion | flops 3777232896 | bytes 10862592 | tf_op jit(solution)/shard_map/dot_general | solution.py:26
  205.2 2.1 reduce.3
  210.4 10.5 %multiply_convert_fusion = bf16[800,3072]{1,0:T(8,128)(2,1)S(1)} fusion(bf16[800,768]{1,0:T(8,128)(2,1)S(1)} %copy-done.29, bf16[768,3072]{1,0:T(8,128)(2,1)S(1)} %bitcast.172, f32[800,3072]{1,0:T(8,128)} %get-tuple-element.277, f32[3072]{0:T(1024)S(1)} %copy-done.96), kind=kOutput, calls=%fused_computation.6 | convolution fusion | flops 3806822400 | bytes 20705280 | tf_op jit(solution)/shard_map/dot_general | solution.py:18
  220.9 2.2 copy-done.27
  223.1 7.7 %convolution_convert_fusion.2 = bf16[768,3072]{1,0:T(8,128)(2,1)} fusion(bf16[800,3072]{1,0:T(8,128)(2,1)S(1)} %multiply_convert_fusion, f32[800,768]{1,0:T(8,128)S(1)} %copy-done.17, f32[768]{0:T(1024)S(1)} %copy-done.139, f32[768]{0:T(1024)S(1)} %copy-done.94, f32[800]{0:T(1024)S(1)} %copy-done.88, f32[800]{0:T(1024)S(1)} %broadcast_multiply_fusion.4), kind=kOutput, calls=%fused_computation.18 | convolution fusion | flops 3780304896 | bytes 12103936 | tf_op jit(solution)/shard_map/dot_general | solution.py:26
  230.8 3.2 reduce.4
  234.0 8.5 %multiply_reduce_fusion = (bf16[768]{0:T(1024)(128)(2,1)S(1)}, f32[800]{0:T(1024)S(1)}, f32[800]{0:T(1024)S(1)}, bf16[768]{0:T(1024)(128)(2,1)S(1)}, f32[800,768]{1,0:T(8,128)S(1)}) fusion(f32[800,768]{1,0:T(8,128)S(1)} %copy-done.17, f32[800]{0:T(1024)S(1)} %copy-done.88, f32[800]{0:T(1024)S(1)} %broadcast_multiply_fusion.4, f32[768]{0:T(1024)S(1)} %copy-done.94, ...), kind=kOutput, calls=%fused_computation.66 | convolution fusion | flops 3780400128 | bytes 14567936 | tf_op jit(solution)/shard_map/dot_general | solution.py:22
  243.8 3.3 convolution_convert_fusion.6
  247.2 14.7 %attend_back.2 = (bf16[4,200,2304]{2,1,0:T(8,128)(2,1)S(1)}, f32[1,2304]{1,0:T(1,128)S(1)}) custom-call(bf16[4,200,2304]{2,1,0:T(8,128)(2,1)S(1)} %bitcast.177, bf16[4,200,768]{2,1,0:T(8,128)(2,1)S(1)} %bitcast.186), custom_call_target="tpu_custom_call" | custom-call | flops 17999998976 | bytes 8601600 | tf_op jit(solution)/shard_map/attend_back/pallas_call | solution.py:218
  263.8 4.3 convolution_convert_fusion.14
  271.9 5.5 %collective-permute-start.44 = (bf16[96,768]{1,0:T(8,128)(2,1)S(1)}, bf16[96,768]{1,0:T(8,128)(2,1)S(1)}, u32[]{:S(2)}, u32[]{:S(2)}) collective-permute-start(bf16[96,768]{1,0:T(8,128)(2,1)S(1)} %bitcast.215), channel_id=1, source_target_pairs={{0,1},{1,2},{2,3},{3,0},{4,5},{5,6},{6,7},{7,4},{8,9},{9,10},{10,1... | collective-permute-start | bytes 442376 | tf_op jit(solution)/shard_map/ppermute | solution.py:31
  277.5 3.2 collective-permute-start.45
  281.4 6.1 %multiply_reduce_fusion.1 = (bf16[768]{0:T(1024)(128)(2,1)S(1)}, f32[800]{0:T(1024)S(1)}, f32[800]{0:T(1024)S(1)}, bf16[768]{0:T(1024)(128)(2,1)S(1)}, f32[800,768]{1,0:T(8,128)S(1)}) fusion(f32[800,768]{1,0:T(8,128)S(1)} %copy-done.21, f32[800]{0:T(1024)S(1)} %copy-done.86, f32[800]{0:T(1024)S(1)} %broadcast_multiply_fusion.5, f32[768]{0:T(1024)S(1)} %copy-done.92, ...), kind=kOutput, calls=%fused_computation.67 | convolution fusion | flops 2836681728 | bytes 12159488 | tf_op jit(solution)/shard_map/dot_general | solution.py:22
  288.8 3.0 convolution_convert_fusion.5
  292.8 3.7 collective-permute-start.25
  297.0 5.8 %convolution_convert_fusion.1 = bf16[768,2304]{1,0:T(8,128)(2,1)} fusion(bf16[800,2304]{1,0:T(8,128)(2,1)S(1)} %bitcast.179, f32[800,768]{1,0:T(8,128)S(1)} %copy-done.21, f32[768]{0:T(1024)S(1)} %copy-done.137, f32[768]{0:T(1024)S(1)} %copy-done.92, f32[800]{0:T(1024)S(1)} %copy-done.86, f32[800]{0:T(1024)S(1)} %broadcast_multiply_fusion.5), kind=kOutput, calls=%fused_computation.17 | convolution fusion | flops 2835996672 | bytes 9695488 | tf_op jit(solution)/shard_map/dot_general | solution.py:26
  303.0 2.9 reshape_reshape.3
  307.7 13.8 %collective-permute-done.26 = bf16[200,768]{1,0:T(8,128)(2,1)} collective-permute-done((bf16[200,768]{1,0:T(8,128)(2,1)}, bf16[200,768]{1,0:T(8,128)(2,1)}, u32[]{:S(2)}, u32[]{:S(2)}) %collective-permute-start.26) | collective-permute-done | bytes 307232 | tf_op jit(solution)/shard_map/ppermute | solution.py:70
  321.6 3.5 fusion.166
  325.1 2.5 convolution_convert_fusion.10
  331.4 3.4 pad_maximum_fusion
  334.8 2.4 convolution_convert_fusion.9
  337.2 2.0 copy-done.6
  339.2 13.3 %attend_back.3 = (bf16[7,112,2304]{2,1,0:T(8,128)(2,1)S(1)}, f32[1,2304]{1,0:T(1,128)S(1)}) custom-call(bf16[7,112,2304]{2,1,0:T(8,128)(2,1)S(1)} %bitcast.181, bf16[7,112,768]{2,1,0:T(8,128)(2,1)S(1)} %bitcast.189), custom_call_target="tpu_custom_call" | custom-call | flops 17999998976 | bytes 8429568 | tf_op jit(solution)/shard_map/attend_back/pallas_call | solution.py:218
  355.4 2.0 reshape.403
  360.7 3.5 collective-permute-start.42
  364.9 2.1 collective-permute-start.43
  367.0 5.0 %fusion.8 = f32[784,768]{1,0:T(8,128)S(1)} fusion(bf16[784,2304]{1,0:T(8,128)(2,1)S(1)} %bitcast.182, bf16[768,4096]{1,0:T(8,128)(2,1)} %all-gather.4.cloned.1.call-done), kind=kOutput, calls=%fused_computation.33 | convolution fusion | flops 2774532096 | bytes 9560064 | tf_op jit(solution)/shard_map/dot_general | solution.py:22
  374.8 2.1 fusion.58
  377.3 4.4 convolution_convert_fusion
  383.8 3.2 convolution_convert_fusion.4
  388.1 2.1 collective-permute-start.33
  395.7 4.4 collective-permute-done.32
  401.6 4.0 multiply_convert_fusion.2
  406.8 2.0 fusion.96
  408.8 2.6 collective-permute-done.33
  411.4 2.3 pad_maximum_fusion.3
  414.0 10.6 %collective-permute-done.31 = bf16[96,2560]{1,0:T(8,128)(2,1)} collective-permute-done((bf16[96,2560]{1,0:T(8,128)(2,1)}, bf16[96,2560]{1,0:T(8,128)(2,1)}, u32[]{:S(2)}, u32[]{:S(2)}) %collective-permute-start.31) | collective-permute-done | bytes 491552 | tf_op jit(solution)/shard_map/ppermute | solution.py:76
  432.3 5.3 %convolution_add_fusion = f32[784,768]{1,0:T(8,128)} fusion(f32[784,768]{1,0:T(8,128)S(1)} %copy-done.31, bf16[800,768]{1,0:T(8,128)(2,1)} %pad_maximum_fusion.3, s32[784]{0:T(1024)S(1)} %copy-done.131, s32[800]{0:T(1024)S(1)} %copy-done.59, s32[800]{0:T(1024)S(1)} %copy-done.114, s32[800]{0:T(1024)S(1)} %copy-done.127, s32[800]{0:T(1024)S(1)} %copy-done.124, ...), kind=kOutput, calls=%fused_computation.100 | convolution fusion | flops 971507712 | bytes 6074368 | tf_op jit(solution)/shard_map/dot_general | solution.py:26
  437.6 7.9 %collective-permute-done.36 = bf16[96,640]{0,1:T(8,128)(2,1)S(1)} collective-permute-done((bf16[96,640]{0,1:T(8,128)(2,1)S(1)}, bf16[96,640]{0,1:T(8,128)(2,1)S(1)}, u32[]{:S(2)}, u32[]{:S(2)}) %collective-permute-start.36) | collective-permute-done | bytes 122912 | tf_op jit(solution)/shard_map/ppermute | solution.py:31
  455.6 2.0 collective-permute-done.38
  457.6 20.0 %collective-permute-done.39 = bf16[96,1152]{0,1:T(8,128)(2,1)S(1)} collective-permute-done((bf16[96,1152]{0,1:T(8,128)(2,1)S(1)}, bf16[96,1152]{0,1:T(8,128)(2,1)S(1)}, u32[]{:S(2)}, u32[]{:S(2)}) %collective-permute-start.39) | collective-permute-done | bytes 221216 | tf_op jit(solution)/shard_map/ppermute | solution.py:31
  (651 shorter events, 113.0 us)
Async XLA Ops:
  7.2 101.4 %all-gather.4.cloned.1.call-start = ((), (), s32[]{:S(2)}) async-start(), calls=%async_computation.3 | async-start | bytes 7077888 | tf_op jit(solution)/shard_map/all_gather | solution.py:334
  12.5 8.5 %collective-permute-start = (bf16[96,1024]{0,1:T(8,128)(2,1)S(1)}, bf16[96,1024]{0,1:T(8,128)(2,1)S(1)}, u32[]{:S(2)}, u32[]{:S(2)}) collective-permute-start(bf16[96,1024]{0,1:T(8,128)(2,1)S(1)} %pad_maximum_fusion.8), channel_id=1, source_target_pairs={{0,1},{1,2},{2,3},{3,0},{4,5},{5,6},{6,7},{7,4},{8,9},{9,10},{10,1... | collective-permute-start | bytes 589832 | tf_op jit(solution)/shard_map/ppermute | solution.py:31
  12.6 24.8 %collective-permute-start.1 = (bf16[96,1024]{0,1:T(8,128)(2,1)S(1)}, bf16[96,1024]{0,1:T(8,128)(2,1)S(1)}, u32[]{:S(2)}, u32[]{:S(2)}) collective-permute-start(bf16[96,1024]{0,1:T(8,128)(2,1)S(1)} %pad_maximum_fusion.8), channel_id=1, source_target_pairs={{0,2},{1,3},{2,0},{3,1},{4,6},{5,7},{6,4},{7,5},{8,10},{9,11},{10,... | collective-permute-start | bytes 589832 | tf_op jit(solution)/shard_map/ppermute | solution.py:31
  14.5 22.9 %collective-permute-start.2 = (bf16[96,1024]{0,1:T(8,128)(2,1)S(1)}, bf16[96,1024]{0,1:T(8,128)(2,1)S(1)}, u32[]{:S(2)}, u32[]{:S(2)}) collective-permute-start(bf16[96,1024]{0,1:T(8,128)(2,1)S(1)} %pad_maximum_fusion.8), channel_id=1, source_target_pairs={{0,3},{1,0},{2,1},{3,2},{4,7},{5,4},{6,5},{7,6},{8,11},{9,8},{10,9... | collective-permute-start | bytes 589832 | tf_op jit(solution)/shard_map/ppermute | solution.py:31
  15.1 141.8 %copy-start.58 = (s32[800]{0:T(1024)}, s32[800]{0:T(1024)S(1)}, u32[]{:S(2)}) copy-start(s32[800]{0:T(1024)S(1)} %iota.280) | copy-start | bytes 9604
  20.3 40.8 %copy-start.35 = (bf16[800,768]{1,0:T(8,128)(2,1)}, bf16[800,768]{1,0:T(8,128)(2,1)S(1)}, u32[]{:S(2)}) copy-start(bf16[800,768]{1,0:T(8,128)(2,1)S(1)} %convolution_convert_fusion.8) | copy-start | bytes 3686404
  41.2 120.7 %all-gather.6.cloned.1.call-start = ((), (), s32[]{:S(2)}) async-start(), calls=%async_computation.4 | async-start | bytes 5308416 | tf_op jit(solution)/shard_map/all_gather | solution.py:334
  41.7 5.6 %collective-permute-start.15 = (bf16[96,768]{1,0:T(8,128)(2,1)S(1)}, bf16[96,768]{1,0:T(8,128)(2,1)S(1)}, u32[]{:S(2)}, u32[]{:S(2)}) collective-permute-start(bf16[96,768]{1,0:T(8,128)(2,1)S(1)} %pad_maximum_fusion.11), channel_id=1, source_target_pairs={{0,1},{1,2},{2,3},{3,0},{4,5},{5,6},{6,7},{7,4},{8,9},{9,10},{10,1... | collective-permute-start | bytes 442376 | tf_op jit(solution)/shard_map/ppermute | solution.py:31
  41.8 14.8 %collective-permute-start.16 = (bf16[96,768]{1,0:T(8,128)(2,1)S(1)}, bf16[96,768]{1,0:T(8,128)(2,1)S(1)}, u32[]{:S(2)}, u32[]{:S(2)}) collective-permute-start(bf16[96,768]{1,0:T(8,128)(2,1)S(1)} %pad_maximum_fusion.11), channel_id=1, source_target_pairs={{0,2},{1,3},{2,0},{3,1},{4,6},{5,7},{6,4},{7,5},{8,10},{9,11},{10,... | collective-permute-start | bytes 442376 | tf_op jit(solution)/shard_map/ppermute | solution.py:31
  43.2 13.4 %collective-permute-start.17 = (bf16[96,768]{1,0:T(8,128)(2,1)S(1)}, bf16[96,768]{1,0:T(8,128)(2,1)S(1)}, u32[]{:S(2)}, u32[]{:S(2)}) collective-permute-start(bf16[96,768]{1,0:T(8,128)(2,1)S(1)} %pad_maximum_fusion.11), channel_id=1, source_target_pairs={{0,3},{1,0},{2,1},{3,2},{4,7},{5,4},{6,5},{7,6},{8,11},{9,8},{10,9... | collective-permute-start | bytes 442376 | tf_op jit(solution)/shard_map/ppermute | solution.py:31
  58.3 36.0 %copy-start.156 = (s32[2]{0:T(128)S(1)}, s32[2]{0:T(128)}, u32[]{:S(2)}) copy-start(s32[2]{0:T(128)} %param.13) | copy-start | bytes 28
  58.3 124.7 %all-gather.8.cloned.1.call-start = ((), (), s32[]{:S(2)}) async-start(), calls=%async_computation.5 | async-start | bytes 5308416 | tf_op jit(solution)/shard_map/all_gather | solution.py:334
  58.4 44.6 %collective-permute-start.6 = (bf16[96,768]{1,0:T(8,128)(2,1)}, bf16[96,768]{1,0:T(8,128)(2,1)}, u32[]{:S(2)}, u32[]{:S(2)}) collective-permute-start(bf16[96,768]{1,0:T(8,128)(2,1)} %param.16), channel_id=1, source_target_pairs={{0,1},{1,2},{2,3},{3,0},{4,5},{5,6},{6,7},{7,4},{8,9},{9,10},{10,1... | collective-permute-start | bytes 442376 | tf_op jit(solution)/shard_map/ppermute | solution.py:31
  58.4 44.5 %collective-permute-start.7 = (bf16[96,768]{1,0:T(8,128)(2,1)}, bf16[96,768]{1,0:T(8,128)(2,1)}, u32[]{:S(2)}, u32[]{:S(2)}) collective-permute-start(bf16[96,768]{1,0:T(8,128)(2,1)} %param.16), channel_id=1, source_target_pairs={{0,2},{1,3},{2,0},{3,1},{4,6},{5,7},{6,4},{7,5},{8,10},{9,11},{10,... | collective-permute-start | bytes 442376 | tf_op jit(solution)/shard_map/ppermute | solution.py:31
  59.2 43.8 %collective-permute-start.8 = (bf16[96,768]{1,0:T(8,128)(2,1)}, bf16[96,768]{1,0:T(8,128)(2,1)}, u32[]{:S(2)}, u32[]{:S(2)}) collective-permute-start(bf16[96,768]{1,0:T(8,128)(2,1)} %param.16), channel_id=1, source_target_pairs={{0,3},{1,0},{2,1},{3,2},{4,7},{5,4},{6,5},{7,6},{8,11},{9,8},{10,9... | collective-permute-start | bytes 442376 | tf_op jit(solution)/shard_map/ppermute | solution.py:31
  62.0 30.7 %collective-permute-start.10 = (bf16[200,768]{1,0:T(8,128)(2,1)S(1)}, bf16[200,768]{1,0:T(8,128)(2,1)S(1)}, u32[]{:S(2)}, u32[]{:S(2)}) collective-permute-start(bf16[200,768]{1,0:T(8,128)(2,1)S(1)} %get-tuple-element.185), channel_id=1, source_target_pairs={{0,2},{1,3},{2,0},{3,1},{4,6},{5,7},{6,4},{7,5},{8,10},{9,11},{10,... | collective-permute-start | bytes 921608 | tf_op jit(solution)/shard_map/ppermute | solution.py:70
  64.2 31.8 %collective-permute-start.11 = (bf16[200,768]{1,0:T(8,128)(2,1)}, bf16[200,768]{1,0:T(8,128)(2,1)}, u32[]{:S(2)}, u32[]{:S(2)}) collective-permute-start(bf16[200,768]{1,0:T(8,128)(2,1)} %get-tuple-element.184), channel_id=1, source_target_pairs={{0,3},{1,0},{2,1},{3,2},{4,7},{5,4},{6,5},{7,6},{8,11},{9,8},{10,9... | collective-permute-start | bytes 921608 | tf_op jit(solution)/shard_map/ppermute | solution.py:70
  64.6 63.5 %copy-start.60 = (s32[800]{0:T(1024)}, s32[800]{0:T(1024)S(1)}, u32[]{:S(2)}) copy-start(s32[800]{0:T(1024)S(1)} %rem.278) | copy-start | bytes 9604
  64.7 31.3 %copy-start.140 = (pred[784]{0:T(1024)(128)(4,1)}, pred[784]{0:T(1024)(128)(4,1)S(1)}, u32[]{:S(2)}) copy-start(pred[784]{0:T(1024)(128)(4,1)S(1)} %fusion.121) | copy-start | bytes 2356
  64.7 31.2 %copy-start.102 = (pred[784]{0:T(1024)(128)(4,1)}, pred[784]{0:T(1024)(128)(4,1)S(1)}, u32[]{:S(2)}) copy-start(pred[784]{0:T(1024)(128)(4,1)S(1)} %get-tuple-element.284) | copy-start | bytes 2356
  64.7 31.2 %copy-start.105 = (pred[784]{0:T(1024)(128)(4,1)}, pred[784]{0:T(1024)(128)(4,1)S(1)}, u32[]{:S(2)}) copy-start(pred[784]{0:T(1024)(128)(4,1)S(1)} %get-tuple-element.285) | copy-start | bytes 2356
  64.8 31.2 %copy-start.65 = (s32[784]{0:T(1024)}, s32[784]{0:T(1024)S(1)}, u32[]{:S(2)}) copy-start(s32[784]{0:T(1024)S(1)} %get-tuple-element.290) | copy-start | bytes 9412
  64.8 31.2 %copy-start.68 = (s32[784]{0:T(1024)}, s32[784]{0:T(1024)S(1)}, u32[]{:S(2)}) copy-start(s32[784]{0:T(1024)S(1)} %get-tuple-element.291) | copy-start | bytes 9412
  64.8 31.2 %copy-start.71 = (s32[784]{0:T(1024)}, s32[784]{0:T(1024)S(1)}, u32[]{:S(2)}) copy-start(s32[784]{0:T(1024)S(1)} %get-tuple-element.292) | copy-start | bytes 9412
  92.7 9.1 %collective-permute-start.9 = (bf16[200,768]{1,0:T(8,128)(2,1)}, bf16[200,768]{1,0:T(8,128)(2,1)}, u32[]{:S(2)}, u32[]{:S(2)}) collective-permute-start(bf16[200,768]{1,0:T(8,128)(2,1)} %get-tuple-element.183), channel_id=1, source_target_pairs={{0,1},{1,2},{2,3},{3,0},{4,5},{5,6},{6,7},{7,4},{8,9},{9,10},{10,1... | collective-permute-start | bytes 921608 | tf_op jit(solution)/shard_map/ppermute | solution.py:70
  96.1 43.4 %copy-start.14 = (bf16[4,200,768]{2,1,0:T(8,128)(2,1)}, bf16[4,200,768]{2,1,0:T(8,128)(2,1)S(1)}, u32[]{:S(2)}) copy-start(bf16[4,200,768]{2,1,0:T(8,128)(2,1)S(1)} %pad.33) | copy-start | bytes 3686404
  108.6 160.3 %reduce-scatter.6.cloned.1.call-start = ((), (), s32[]{:S(2)}) async-start(), calls=%async_computation.7 | async-start | bytes 5308416 | tf_op jit(solution)/shard_map/reduce_scatter | solution.py:465
  110.3 15.5 %collective-permute-start.3 = (bf16[96,768]{1,0:T(8,128)(2,1)S(1)}, bf16[96,768]{1,0:T(8,128)(2,1)S(1)}, u32[]{:S(2)}, u32[]{:S(2)}) collective-permute-start(bf16[96,768]{1,0:T(8,128)(2,1)S(1)} %bitcast.210), channel_id=1, source_target_pairs={{0,1},{1,2},{2,3},{3,0},{4,5},{5,6},{6,7},{7,4},{8,9},{9,10},{10,1... | collective-permute-start | bytes 442376 | tf_op jit(solution)/shard_map/ppermute | solution.py:31
  112.4 13.4 %collective-permute-start.4 = (bf16[96,768]{1,0:T(8,128)(2,1)S(1)}, bf16[96,768]{1,0:T(8,128)(2,1)S(1)}, u32[]{:S(2)}, u32[]{:S(2)}) collective-permute-start(bf16[96,768]{1,0:T(8,128)(2,1)S(1)} %bitcast.211), channel_id=1, source_target_pairs={{0,2},{1,3},{2,0},{3,1},{4,6},{5,7},{6,4},{7,5},{8,10},{9,11},{10,... | collective-permute-start | bytes 442376 | tf_op jit(solution)/shard_map/ppermute | solution.py:31
  112.4 13.4 %collective-permute-start.5 = (bf16[96,768]{1,0:T(8,128)(2,1)S(1)}, bf16[96,768]{1,0:T(8,128)(2,1)S(1)}, u32[]{:S(2)}, u32[]{:S(2)}) collective-permute-start(bf16[96,768]{1,0:T(8,128)(2,1)S(1)} %bitcast.212), channel_id=1, source_target_pairs={{0,3},{1,0},{2,1},{3,2},{4,7},{5,4},{6,5},{7,6},{8,11},{9,8},{10,9... | collective-permute-start | bytes 442376 | tf_op jit(solution)/shard_map/ppermute | solution.py:31
  133.8 12.5 %collective-permute-start.12 = (bf16[200,768]{1,0:T(8,128)(2,1)}, bf16[200,768]{1,0:T(8,128)(2,1)}, u32[]{:S(2)}, u32[]{:S(2)}) collective-permute-start(bf16[200,768]{1,0:T(8,128)(2,1)} %get-tuple-element.182), channel_id=1, source_target_pairs={{0,3},{1,0},{2,1},{3,2},{4,7},{5,4},{6,5},{7,6},{8,11},{9,8},{10,9... | collective-permute-start | bytes 921608 | tf_op jit(solution)/shard_map/ppermute | solution.py:70
  136.7 20.2 %collective-permute-start.13 = (bf16[200,768]{1,0:T(8,128)(2,1)S(1)}, bf16[200,768]{1,0:T(8,128)(2,1)}, u32[]{:S(2)}, u32[]{:S(2)}) collective-permute-start(bf16[200,768]{1,0:T(8,128)(2,1)S(1)} %get-tuple-element.181), channel_id=1, source_target_pairs={{0,2},{1,3},{2,0},{3,1},{4,6},{5,7},{6,4},{7,5},{8,10},{9,11},{10,... | collective-permute-start | bytes 921608 | tf_op jit(solution)/shard_map/ppermute | solution.py:70
  137.6 19.3 %collective-permute-start.14 = (bf16[200,768]{1,0:T(8,128)(2,1)S(1)}, bf16[200,768]{1,0:T(8,128)(2,1)}, u32[]{:S(2)}, u32[]{:S(2)}) collective-permute-start(bf16[200,768]{1,0:T(8,128)(2,1)S(1)} %get-tuple-element.180), channel_id=1, source_target_pairs={{0,1},{1,2},{2,3},{3,0},{4,5},{5,6},{6,7},{7,4},{8,9},{9,10},{10,1... | collective-permute-start | bytes 921608 | tf_op jit(solution)/shard_map/ppermute | solution.py:70
  168.0 25.4 %collective-permute-start.18 = (bf16[96,3072]{1,0:T(8,128)(2,1)S(1)}, bf16[96,3072]{1,0:T(8,128)(2,1)S(1)}, u32[]{:S(2)}, u32[]{:S(2)}) collective-permute-start(bf16[96,3072]{1,0:T(8,128)(2,1)S(1)} %pad_maximum_fusion.5.refs_0_), channel_id=1, source_target_pairs={{0,8},{4,12},{8,0},{12,4},{16,24},{20,28},{24,16},{28,20},{1,9},{5... | collective-permute-start | bytes 1769480 | tf_op jit(solution)/shard_map/ppermute | solution.py:76
  169.6 27.6 %collective-permute-start.19 = (bf16[96,3072]{1,0:T(8,128)(2,1)S(1)}, bf16[96,3072]{1,0:T(8,128)(2,1)S(1)}, u32[]{:S(2)}, u32[]{:S(2)}) collective-permute-start(bf16[96,3072]{1,0:T(8,128)(2,1)S(1)} %pad_maximum_fusion.5.refs_0_), channel_id=1, source_target_pairs={{0,16},{4,20},{8,24},{12,28},{16,0},{20,4},{24,8},{28,12},{1,17},{... | collective-permute-start | bytes 1769480 | tf_op jit(solution)/shard_map/ppermute | solution.py:76
  171.0 26.2 %collective-permute-start.20 = (bf16[96,3072]{1,0:T(8,128)(2,1)S(1)}, bf16[96,3072]{1,0:T(8,128)(2,1)S(1)}, u32[]{:S(2)}, u32[]{:S(2)}) collective-permute-start(bf16[96,3072]{1,0:T(8,128)(2,1)S(1)} %pad_maximum_fusion.5.refs_0_), channel_id=1, source_target_pairs={{0,24},{4,28},{8,16},{12,20},{16,8},{20,12},{24,0},{28,4},{1,25},{... | collective-permute-start | bytes 1769480 | tf_op jit(solution)/shard_map/ppermute | solution.py:76
  197.2 11.4 %collective-permute-start.21 = (bf16[96,3072]{1,0:T(8,128)(2,1)S(1)}, bf16[96,3072]{1,0:T(8,128)(2,1)S(1)}, u32[]{:S(2)}, u32[]{:S(2)}) collective-permute-start(bf16[96,3072]{1,0:T(8,128)(2,1)S(1)} %pad_maximum_fusion.5.refs_0_), channel_id=1, source_target_pairs={{0,4},{4,0},{8,12},{12,8},{16,20},{20,16},{24,28},{28,24},{1,5},{5... | collective-permute-start | bytes 1769480 | tf_op jit(solution)/shard_map/ppermute | solution.py:76
  197.2 11.4 %collective-permute-start.22 = (bf16[96,3072]{1,0:T(8,128)(2,1)S(1)}, bf16[96,3072]{1,0:T(8,128)(2,1)S(1)}, u32[]{:S(2)}, u32[]{:S(2)}) collective-permute-start(bf16[96,3072]{1,0:T(8,128)(2,1)S(1)} %collective-permute-done.18.refs_2_), channel_id=1, source_target_pairs={{0,4},{4,0},{8,12},{12,8},{16,20},{20,16},{24,28},{28,24},{1,5},{5... | collective-permute-start | bytes 1769480 | tf_op jit(solution)/shard_map/ppermute | solution.py:76
  197.7 10.9 %collective-permute-start.23 = (bf16[96,3072]{1,0:T(8,128)(2,1)S(1)}, bf16[96,3072]{1,0:T(8,128)(2,1)}, u32[]{:S(2)}, u32[]{:S(2)}) collective-permute-start(bf16[96,3072]{1,0:T(8,128)(2,1)S(1)} %collective-permute-done.19.refs_4_), channel_id=1, source_target_pairs={{0,4},{4,0},{8,12},{12,8},{16,20},{20,16},{24,28},{28,24},{1,5},{5... | collective-permute-start | bytes 1769480 | tf_op jit(solution)/shard_map/ppermute | solution.py:76
  197.7 10.9 %collective-permute-start.24 = (bf16[96,3072]{1,0:T(8,128)(2,1)S(1)}, bf16[96,3072]{1,0:T(8,128)(2,1)}, u32[]{:S(2)}, u32[]{:S(2)}) collective-permute-start(bf16[96,3072]{1,0:T(8,128)(2,1)S(1)} %collective-permute-done.20.refs_6_), channel_id=1, source_target_pairs={{0,4},{4,0},{8,12},{12,8},{16,20},{20,16},{24,28},{28,24},{1,5},{5... | collective-permute-start | bytes 1769480 | tf_op jit(solution)/shard_map/ppermute | solution.py:76
  205.2 150.2 %reduce-scatter.4.cloned.1.call-start = ((), (), s32[]{:S(2)}) async-start(), calls=%async_computation.6 | async-start | bytes 5308416 | tf_op jit(solution)/shard_map/reduce_scatter | solution.py:465
  268.1 178.2 %reduce-scatter.8.cloned.1.call-start = ((), (), s32[]{:S(2)}) async-start(), calls=%async_computation.8 | async-start | bytes 7962624 | tf_op jit(solution)/shard_map/reduce_scatter | solution.py:465
  271.9 24.6 %collective-permute-start.44 = (bf16[96,768]{1,0:T(8,128)(2,1)S(1)}, bf16[96,768]{1,0:T(8,128)(2,1)S(1)}, u32[]{:S(2)}, u32[]{:S(2)}) collective-permute-start(bf16[96,768]{1,0:T(8,128)(2,1)S(1)} %bitcast.215), channel_id=1, source_target_pairs={{0,1},{1,2},{2,3},{3,0},{4,5},{5,6},{6,7},{7,4},{8,9},{9,10},{10,1... | collective-permute-start | bytes 442376 | tf_op jit(solution)/shard_map/ppermute | solution.py:31
  277.5 28.4 %collective-permute-start.45 = (bf16[96,768]{1,0:T(8,128)(2,1)S(1)}, bf16[96,768]{1,0:T(8,128)(2,1)}, u32[]{:S(2)}, u32[]{:S(2)}) collective-permute-start(bf16[96,768]{1,0:T(8,128)(2,1)S(1)} %bitcast.214), channel_id=1, source_target_pairs={{0,2},{1,3},{2,0},{3,1},{4,6},{5,7},{6,4},{7,5},{8,10},{9,11},{10,... | collective-permute-start | bytes 442376 | tf_op jit(solution)/shard_map/ppermute | solution.py:31
  281.4 24.5 %collective-permute-start.46 = (bf16[96,768]{1,0:T(8,128)(2,1)}, bf16[96,768]{1,0:T(8,128)(2,1)}, u32[]{:S(2)}, u32[]{:S(2)}) collective-permute-start(bf16[96,768]{1,0:T(8,128)(2,1)} %bitcast.163), channel_id=1, source_target_pairs={{0,3},{1,0},{2,1},{3,2},{4,7},{5,4},{6,5},{7,6},{8,11},{9,8},{10,9... | collective-permute-start | bytes 442376 | tf_op jit(solution)/shard_map/ppermute | solution.py:31
  292.8 14.9 %collective-permute-start.25 = (bf16[200,768]{1,0:T(8,128)(2,1)}, bf16[200,768]{1,0:T(8,128)(2,1)}, u32[]{:S(2)}, u32[]{:S(2)}) collective-permute-start(bf16[200,768]{1,0:T(8,128)(2,1)} %get-tuple-element.178), channel_id=1, source_target_pairs={{0,1},{1,2},{2,3},{3,0},{4,5},{5,6},{6,7},{7,4},{8,9},{9,10},{10,1... | collective-permute-start | bytes 921608 | tf_op jit(solution)/shard_map/ppermute | solution.py:70
  296.5 25.0 %collective-permute-start.26 = (bf16[200,768]{1,0:T(8,128)(2,1)}, bf16[200,768]{1,0:T(8,128)(2,1)}, u32[]{:S(2)}, u32[]{:S(2)}) collective-permute-start(bf16[200,768]{1,0:T(8,128)(2,1)} %get-tuple-element.177), channel_id=1, source_target_pairs={{0,2},{1,3},{2,0},{3,1},{4,6},{5,7},{6,4},{7,5},{8,10},{9,11},{10,... | collective-permute-start | bytes 921608 | tf_op jit(solution)/shard_map/ppermute | solution.py:70
  296.5 25.0 %collective-permute-start.27 = (bf16[200,768]{1,0:T(8,128)(2,1)}, bf16[200,768]{1,0:T(8,128)(2,1)}, u32[]{:S(2)}, u32[]{:S(2)}) collective-permute-start(bf16[200,768]{1,0:T(8,128)(2,1)} %get-tuple-element.176), channel_id=1, source_target_pairs={{0,3},{1,0},{2,1},{3,2},{4,7},{5,4},{6,5},{7,6},{8,11},{9,8},{10,9... | collective-permute-start | bytes 921608 | tf_op jit(solution)/shard_map/ppermute | solution.py:70
  360.0 31.8 %collective-permute-start.41 = (bf16[96,768]{1,0:T(8,128)(2,1)}, bf16[96,768]{1,0:T(8,128)(2,1)}, u32[]{:S(2)}, u32[]{:S(2)}) collective-permute-start(bf16[96,768]{1,0:T(8,128)(2,1)} %bitcast.168), channel_id=1, source_target_pairs={{0,1},{1,2},{2,3},{3,0},{4,5},{5,6},{6,7},{7,4},{8,9},{9,10},{10,1... | collective-permute-start | bytes 442376 | tf_op jit(solution)/shard_map/ppermute | solution.py:31
  360.7 33.0 %collective-permute-start.42 = (bf16[96,768]{1,0:T(8,128)(2,1)}, bf16[96,768]{1,0:T(8,128)(2,1)}, u32[]{:S(2)}, u32[]{:S(2)}) collective-permute-start(bf16[96,768]{1,0:T(8,128)(2,1)} %bitcast.167), channel_id=1, source_target_pairs={{0,2},{1,3},{2,0},{3,1},{4,6},{5,7},{6,4},{7,5},{8,10},{9,11},{10,... | collective-permute-start | bytes 442376 | tf_op jit(solution)/shard_map/ppermute | solution.py:31
  364.9 29.9 %collective-permute-start.43 = (bf16[96,768]{1,0:T(8,128)(2,1)}, bf16[96,768]{1,0:T(8,128)(2,1)}, u32[]{:S(2)}, u32[]{:S(2)}) collective-permute-start(bf16[96,768]{1,0:T(8,128)(2,1)} %bitcast.166), channel_id=1, source_target_pairs={{0,3},{1,0},{2,1},{3,2},{4,7},{5,4},{6,5},{7,6},{8,11},{9,8},{10,9... | collective-permute-start | bytes 442376 | tf_op jit(solution)/shard_map/ppermute | solution.py:31
  382.2 6.0 %collective-permute-start.28 = (bf16[4,96,2560]{2,1,0:T(8,128)(2,1)S(1)}, bf16[4,96,2560]{2,1,0:T(8,128)(2,1)S(1)}, u32[]{:S(2)}, u32[]{:S(2)}) collective-permute-start(bf16[4,96,2560]{2,1,0:T(8,128)(2,1)S(1)} %pad_maximum_fusion.1), channel_id=1, source_target_pairs={{0,4},{4,0},{8,12},{12,8},{16,20},{20,16},{24,28},{28,24},{1,5},{5... | collective-permute-start | bytes 5898248 | tf_op jit(solution)/shard_map/ppermute | solution.py:76
  388.0 12.1 %collective-permute-start.32 = (bf16[200,768]{1,0:T(8,128)(2,1)S(1)}, bf16[200,768]{1,0:T(8,128)(2,1)S(1)}, u32[]{:S(2)}, u32[]{:S(2)}) collective-permute-start(bf16[200,768]{1,0:T(8,128)(2,1)S(1)} %get-tuple-element.174), channel_id=1, source_target_pairs={{0,3},{1,0},{2,1},{3,2},{4,7},{5,4},{6,5},{7,6},{8,11},{9,8},{10,9... | collective-permute-start | bytes 921608 | tf_op jit(solution)/shard_map/ppermute | solution.py:70
  388.1 23.3 %collective-permute-start.33 = (bf16[200,768]{1,0:T(8,128)(2,1)}, bf16[200,768]{1,0:T(8,128)(2,1)}, u32[]{:S(2)}, u32[]{:S(2)}) collective-permute-start(bf16[200,768]{1,0:T(8,128)(2,1)} %get-tuple-element.173), channel_id=1, source_target_pairs={{0,2},{1,3},{2,0},{3,1},{4,6},{5,7},{6,4},{7,5},{8,10},{9,11},{10,... | collective-permute-start | bytes 921608 | tf_op jit(solution)/shard_map/ppermute | solution.py:70
  391.9 19.6 %collective-permute-start.34 = (bf16[200,768]{1,0:T(8,128)(2,1)}, bf16[200,768]{1,0:T(8,128)(2,1)}, u32[]{:S(2)}, u32[]{:S(2)}) collective-permute-start(bf16[200,768]{1,0:T(8,128)(2,1)} %get-tuple-element.172), channel_id=1, source_target_pairs={{0,1},{1,2},{2,3},{3,0},{4,5},{5,6},{6,7},{7,4},{8,9},{9,10},{10,1... | collective-permute-start | bytes 921608 | tf_op jit(solution)/shard_map/ppermute | solution.py:70
  393.7 20.3 %collective-permute-start.29 = (bf16[96,2560]{1,0:T(8,128)(2,1)}, bf16[96,2560]{1,0:T(8,128)(2,1)}, u32[]{:S(2)}, u32[]{:S(2)}) collective-permute-start(bf16[96,2560]{1,0:T(8,128)(2,1)} %get-tuple-element.168), channel_id=1, source_target_pairs={{0,8},{4,12},{8,0},{12,4},{16,24},{20,28},{24,16},{28,20},{1,9},{5... | collective-permute-start | bytes 1474568 | tf_op jit(solution)/shard_map/ppermute | solution.py:76
  394.9 19.1 %collective-permute-start.30 = (bf16[96,2560]{1,0:T(8,128)(2,1)}, bf16[96,2560]{1,0:T(8,128)(2,1)}, u32[]{:S(2)}, u32[]{:S(2)}) collective-permute-start(bf16[96,2560]{1,0:T(8,128)(2,1)} %get-tuple-element.170), channel_id=1, source_target_pairs={{0,16},{4,20},{8,24},{12,28},{16,0},{20,4},{24,8},{28,12},{1,17},{... | collective-permute-start | bytes 1474568 | tf_op jit(solution)/shard_map/ppermute | solution.py:76
  400.1 24.5 %collective-permute-start.31 = (bf16[96,2560]{1,0:T(8,128)(2,1)}, bf16[96,2560]{1,0:T(8,128)(2,1)}, u32[]{:S(2)}, u32[]{:S(2)}) collective-permute-start(bf16[96,2560]{1,0:T(8,128)(2,1)} %get-tuple-element.169), channel_id=1, source_target_pairs={{0,24},{4,28},{8,16},{12,20},{16,8},{20,12},{24,0},{28,4},{1,25},{... | collective-permute-start | bytes 1474568 | tf_op jit(solution)/shard_map/ppermute | solution.py:76
  429.6 8.0 %collective-permute-start.35 = (bf16[96,640]{0,1:T(8,128)(2,1)S(1)}, bf16[96,640]{0,1:T(8,128)(2,1)S(1)}, u32[]{:S(2)}, u32[]{:S(2)}) collective-permute-start(bf16[96,640]{0,1:T(8,128)(2,1)S(1)} %get-tuple-element.196), channel_id=1, source_target_pairs={{0,1},{1,2},{2,3},{3,0},{4,5},{5,6},{6,7},{7,4},{8,9},{9,10},{10,1... | collective-permute-start | bytes 368648 | tf_op jit(solution)/shard_map/ppermute | solution.py:31
  430.2 15.4 %collective-permute-start.36 = (bf16[96,640]{0,1:T(8,128)(2,1)S(1)}, bf16[96,640]{0,1:T(8,128)(2,1)S(1)}, u32[]{:S(2)}, u32[]{:S(2)}) collective-permute-start(bf16[96,640]{0,1:T(8,128)(2,1)S(1)} %get-tuple-element.197), channel_id=1, source_target_pairs={{0,2},{1,3},{2,0},{3,1},{4,6},{5,7},{6,4},{7,5},{8,10},{9,11},{10,... | collective-permute-start | bytes 368648 | tf_op jit(solution)/shard_map/ppermute | solution.py:31
  431.7 13.9 %collective-permute-start.37 = (bf16[96,640]{0,1:T(8,128)(2,1)S(1)}, bf16[96,640]{0,1:T(8,128)(2,1)S(1)}, u32[]{:S(2)}, u32[]{:S(2)}) collective-permute-start(bf16[96,640]{0,1:T(8,128)(2,1)S(1)} %get-tuple-element.198), channel_id=1, source_target_pairs={{0,3},{1,0},{2,1},{3,2},{4,7},{5,4},{6,5},{7,6},{8,11},{9,8},{10,9... | collective-permute-start | bytes 368648 | tf_op jit(solution)/shard_map/ppermute | solution.py:31
  450.0 7.6 %collective-permute-start.38 = (bf16[96,1152]{0,1:T(8,128)(2,1)S(1)}, bf16[96,1152]{0,1:T(8,128)(2,1)S(1)}, u32[]{:S(2)}, u32[]{:S(2)}) collective-permute-start(bf16[96,1152]{0,1:T(8,128)(2,1)S(1)} %get-tuple-element.186), channel_id=1, source_target_pairs={{0,1},{1,2},{2,3},{3,0},{4,5},{5,6},{6,7},{7,4},{8,9},{9,10},{10,1... | collective-permute-start | bytes 663560 | tf_op jit(solution)/shard_map/ppermute | solution.py:31
  450.0 27.5 %collective-permute-start.39 = (bf16[96,1152]{0,1:T(8,128)(2,1)S(1)}, bf16[96,1152]{0,1:T(8,128)(2,1)S(1)}, u32[]{:S(2)}, u32[]{:S(2)}) collective-permute-start(bf16[96,1152]{0,1:T(8,128)(2,1)S(1)} %get-tuple-element.188), channel_id=1, source_target_pairs={{0,2},{1,3},{2,0},{3,1},{4,6},{5,7},{6,4},{7,5},{8,10},{9,11},{10,... | collective-permute-start | bytes 663560 | tf_op jit(solution)/shard_map/ppermute | solution.py:31
  451.5 26.1 %collective-permute-start.40 = (bf16[96,1152]{0,1:T(8,128)(2,1)S(1)}, bf16[96,1152]{0,1:T(8,128)(2,1)S(1)}, u32[]{:S(2)}, u32[]{:S(2)}) collective-permute-start(bf16[96,1152]{0,1:T(8,128)(2,1)S(1)} %get-tuple-element.187), channel_id=1, source_target_pairs={{0,3},{1,0},{2,1},{3,2},{4,7},{5,4},{6,5},{7,6},{8,11},{9,8},{10,9... | collective-permute-start | bytes 663560 | tf_op jit(solution)/shard_map/ppermute | solution.py:31
  (155 other events, 1100.6 us)
Sparse Core Ops, SparseCore 0:
  41.3 46.4 all-gather.3
  89.7 38.9 all-gather.5
  130.5 38.9 all-gather.7
  205.3 59.4 reduce-scatter.5
  268.5 59.3 reduce-scatter.3
  337.3 73.5 reduce-scatter.7
